TPU v7x, 512 devices: a whole 4x4x16 slice. The times are simulated.
512 devices in a mesh: batch: 64 (over z, y), proto: 8 (over x, core).
Axes of the slice: x: 4, y: 4, z: 16, core: 2. Of those that a mesh axis runs over, the one named last changes fastest.
Arguments:
- embeddings: bfloat16 [65536, 256], P('batch'), as said below
- prototypes: bfloat16 [16384, 256], P('proto'), as said below
- partner: int32 [65536], P('batch'), may hold values from 0 to 65535, as said below
Outputs:
- emb_grad: float32 [65536, 256], P('batch')
- proto_grad: float32 [16384, 256], P('proto')
Inputs may be any that keep to these rules, and one draw needn't show every extreme that they name: partner[partner[b]] == b for every view b, and partner[b] lies in the aligned block of 1024 views whose block index differs from that of b by 32. `embeddings`: no row is zero. `prototypes`: no row is zero.
All inputs are finite; a program needn't handle non-finite values.
Results may differ from a plain program's by a relative error of at most 0.0016.
Values may be sent and summed in bfloat16 or wider, within the bound.
No kernel may reach another device: no remote copies, remote signals or barrier semaphores. Data moves between devices by JAX's collectives and lax.ppermute only.
A program may use at most 64 MiB of HBM per device.

v0:
```python
import jax
import jax.numpy as jnp
from jax import lax
from jax.sharding import PartitionSpec as P

ITERS = 3


epsilon_code = 0.05
sharpness_divisor = 0.1
norm_floor = 1e-06


def shifted(value, axis, steps):
    count = lax.axis_size(axis)
    pairs = [(source, (source + steps) % count) for source in range(count)]
    return lax.ppermute(value, axis, pairs)


def unit_rows(values):
    wide = values.astype(jnp.float32)
    scale = lax.rsqrt(jnp.mean(wide * wide, axis=1, keepdims=True) + norm_floor) / jnp.sqrt(
        jnp.float32(wide.shape[1])
    )
    return (wide * scale, scale)


def norm_back(upstream, units, scale):
    return scale * (upstream - units * jnp.sum(units * upstream, axis=1, keepdims=True))


def contract_rows(left, right):
    return lax.dot_general(
        left, right, (((0,), (0,)), ((), ())), preferred_element_type=jnp.float32
    )


def body(embeddings, prototypes, partner):
    view_units, view_scale = unit_rows(embeddings)
    proto_units, proto_scale = unit_rows(prototypes)
    views = view_units.astype(jnp.bfloat16)
    protos = proto_units.astype(jnp.bfloat16)
    row_count = views.shape[0]
    links = jnp.remainder(partner, row_count)
    separation_measure = lax.axis_size("batch") // 2
    centroid_raw_affinities = jnp.dot(views, protos.T, preferred_element_type=jnp.float32)
    kernel = jnp.exp(centroid_raw_affinities / epsilon_code)

    def column_scale_of(weight):
        column_part = jnp.sum(weight[:, None] * kernel, axis=0)
        return 1.0 / lax.psum(column_part, "batch")

    weight = jnp.ones((row_count,), jnp.float32)
    for sweep in range(ITERS - 1):
        column_scale = column_scale_of(weight)
        row_part = jnp.sum(kernel * column_scale[None, :], axis=1)
        weight = 1.0 / lax.psum(row_part, "proto")
    column_scale = column_scale_of(weight)
    tempered_affinities = jnp.exp(centroid_raw_affinities / sharpness_divisor)
    soft_part = jnp.sum(tempered_affinities, axis=1)
    dispersion_width = kernel * column_scale[None, :]
    line_aggregate, soft_total = lax.psum((jnp.sum(dispersion_width, axis=1), soft_part), "proto")
    balanced_transport_labels = (dispersion_width * (1.0 / line_aggregate)[:, None]).astype(
        jnp.bfloat16
    )
    received_pieces = shifted(balanced_transport_labels, "batch", separation_measure)
    centroid_agreement = received_pieces[links]
    estimated_likelihood = tempered_affinities * (1.0 / soft_total)[:, None]
    logit_gradient = (
        (estimated_likelihood - centroid_agreement.astype(jnp.float32)) / sharpness_divisor
    ).astype(jnp.bfloat16)
    view_part = jnp.dot(logit_gradient, protos, preferred_element_type=jnp.float32)
    view_upstream = lax.psum(view_part, "proto")
    emb_grad = norm_back(view_upstream, view_units, view_scale)
    proto_upstream = lax.psum(contract_rows(logit_gradient, views), "batch")
    proto_grad = norm_back(proto_upstream, proto_units, proto_scale)
    return (emb_grad, proto_grad)


def solution(mesh):
    return jax.shard_map(
        body,
        mesh=mesh,
        in_specs=(P("batch", None), P("proto", None), P("batch")),
        out_specs=(P("batch", None), P("proto", None)),
        check_vma=False,
    )
```

profile of v0, /device:TPU:1, one launch (start us, length us, event | category | flops | bytes accessed | tf_op | source)
XLA Modules:
  0.0 1259.2 jit_solution(6247067676049251214)
XLA Ops:
  10.1 6.3 fusion.4
  16.3 124.7 %psum.64 = f32[2048]{0:T(1024)S(1)} all-reduce(f32[2048]{0:T(1024)S(1)} %get-tuple-element.6), channel_id=1, replica_groups=mesh['batch'=64,'proto'=8] {'batch'}, use_global_device_ids=true, to_apply=%region_5.6 | all-reduce | flops 2048 | bytes 16384 | tf_op jit(solution)/shard_map/psum | solution.py:51
  141.0 5.1 fusion
  146.1 40.6 %psum.65 = f32[1024]{0:T(1024)S(1)} all-reduce(f32[1024]{0:T(1024)S(1)} %get-tuple-element.3), channel_id=1, replica_groups=mesh['batch'=64,'proto'=8] {'proto'}, use_global_device_ids=true, to_apply=%region_7.8 | all-reduce | flops 1024 | bytes 8192 | tf_op jit(solution)/shard_map/psum | solution.py:57
  186.7 4.3 multiply_reduce_fusion.2
  191.0 112.9 %psum.66 = f32[2048]{0:T(1024)S(1)} all-reduce(f32[2048]{0:T(1024)S(1)} %multiply_reduce_fusion.2), channel_id=1, replica_groups=mesh['batch'=64,'proto'=8] {'batch'}, use_global_device_ids=true, to_apply=%region_9.10 | all-reduce | flops 2048 | bytes 16384 | tf_op jit(solution)/shard_map/psum | solution.py:51
  303.9 4.8 multiply_reduce_fusion.1
  308.7 39.6 %psum.67 = f32[1024]{0:T(1024)S(1)} all-reduce(f32[1024]{0:T(1024)S(1)} %multiply_reduce_fusion.1), channel_id=1, replica_groups=mesh['batch'=64,'proto'=8] {'proto'}, use_global_device_ids=true, to_apply=%region_11.12 | all-reduce | flops 1024 | bytes 8192 | tf_op jit(solution)/shard_map/psum | solution.py:57
  348.3 4.3 multiply_reduce_fusion
  352.6 114.8 %psum.68 = f32[2048]{0:T(1024)S(1)} all-reduce(f32[2048]{0:T(1024)S(1)} %multiply_reduce_fusion), channel_id=1, replica_groups=mesh['batch'=64,'proto'=8] {'batch'}, use_global_device_ids=true, to_apply=%region_13.14 | all-reduce | flops 2048 | bytes 16384 | tf_op jit(solution)/shard_map/psum | solution.py:51
  467.5 4.8 multiply_reduce_fusion.4
  472.3 39.9 %all-reduce = (f32[1024]{0:T(1024)S(1)}, f32[1024]{0:T(1024)S(1)}) all-reduce(f32[1024]{0:T(1024)S(1)} %multiply_reduce_fusion.4, f32[1024]{0:T(1024)S(1)} %get-tuple-element.2), channel_id=1, replica_groups=mesh['batch'=64,'proto'=8] {'proto'}, use_global_device_ids=true, to_apply=%region_15.16 | all-reduce | flops 2048 | bytes 16384 | tf_op jit(solution)/shard_map/psum | solution.py:62
  512.2 4.4 multiply_convert_fusion.1
  516.6 6.3 collective-permute-start
  522.9 293.5 %collective-permute-done = bf16[1024,2048]{1,0:T(8,128)(2,1)} collective-permute-done((bf16[1024,2048]{1,0:T(8,128)(2,1)S(1)}, bf16[1024,2048]{1,0:T(8,128)(2,1)}, u32[]{:S(2)}, u32[]{:S(2)}) %collective-permute-start) | collective-permute-done | bytes 4194336 | tf_op jit(solution)/shard_map/ppermute | solution.py:17
  816.4 11.6 gather_fusion
  828.0 6.1 multiply_convert_fusion
  836.0 2.3 fusion.16
  838.4 5.0 fusion.20
  843.5 129.7 %all-reduce.4.cloned.1.call-done = f32[1024,256]{1,0:T(8,128)} async-done(((f32[1024,256]{1,0:T(8,128)}), f32[1024,256]{1,0:T(8,128)}) %all-reduce.4.cloned.1.call-update) | async-done | bytes 1048592 | tf_op jit(solution)/shard_map/psum | solution.py:73
  974.7 2.5 fusion.14
  977.3 270.0 %all-reduce.6.cloned.1.call-done = f32[2048,256]{1,0:T(8,128)} async-done(((f32[2048,256]{1,0:T(8,128)}), f32[2048,256]{1,0:T(8,128)}) %all-reduce.6.cloned.1.call-update) | async-done | bytes 2097168 | tf_op jit(solution)/shard_map/psum | solution.py:75
  1247.2 2.2 fusion.5
  1249.5 2.9 fusion.7
  (25 shorter events, 6.5 us)
Async XLA Ops:
  7.2 966.0 %all-reduce.4.cloned.1.call-start = ((), (), s32[]{:S(2)}) async-start(), calls=%async_computation | async-start | bytes 2097152 | tf_op jit(solution)/shard_map/psum | solution.py:73
  472.3 50.6 %copy-start.3 = (s32[1024]{0:T(1024)S(1)}, s32[1024]{0:T(1024)}, u32[]{:S(2)}) copy-start(s32[1024]{0:T(1024)} %param.5) | copy-start | bytes 12292
  516.6 299.8 %collective-permute-start = (bf16[1024,2048]{1,0:T(8,128)(2,1)S(1)}, bf16[1024,2048]{1,0:T(8,128)(2,1)}, u32[]{:S(2)}, u32[]{:S(2)}) collective-permute-start(bf16[1024,2048]{1,0:T(8,128)(2,1)S(1)} %multiply_convert_fusion.1), channel_id=1, source_target_pairs={{0,256},{8,264},{16,272},{24,280},{32,288},{40,296},{48,304},{56,3... | collective-permute-start | bytes 12582920 | tf_op jit(solution)/shard_map/ppermute | solution.py:17
  828.0 8.0 copy-start
  834.0 1.9 copy-start.2
  836.0 2.4 copy-start.1
  838.3 408.9 %all-reduce.6.cloned.1.call-start = ((), (), s32[]{:S(2)}) async-start(), calls=%async_computation.1 | async-start | bytes 4194304 | tf_op jit(solution)/shard_map/psum | solution.py:75
Sparse Core Ops, SparseCore 0:
  838.5 134.6 all-reduce.3
  977.1 270.0 all-reduce.5
where the time goes:
time: 1270 us; the launch traced here: 1260 us
  waiting for transfers between devices  693 us (55%)
  blocking collectives  472 us (37%)
  other arithmetic  45.9 us (4%)
  between operations  14.2 us (1%)
  matrix products  13.6 us (1%)
  local copies, waits for them, and re-layouts  13.5 us (1%)
    psum x3, blocking collectives, column_scale_of(): return 1.0 / lax.psum(column_part, 'batch')  352 us
    ppermute x1, waiting for transfers between devices, shifted(): return lax.ppermute(value, axis, pairs)  294 us
    psum x1, waiting for transfers between devices, body(): proto_upstream = lax.psum(contract_rows(logit_gradient, views), 'batch')  270 us
    psum x1, waiting for transfers between devices, body(): view_upstream = lax.psum(view_part, 'proto')  130 us
    psum x2, blocking collectives, body(): weight = 1.0 / lax.psum(row_part, 'proto')  80.1 us
    psum x1, blocking collectives, body(): lax.psum((jnp.sum(dispersion_width, axis=1), soft_part), 'proto')  39.9 us
  transfers between devices with their start and end apart: 3, of which 3 were waited for; matrix products, arithmetic and copies ran while one was open for 1% of the time, Pallas kernels for 0%

commit v1 on v0

v1 whole, which is shorter than its diff:
```python
import jax
import jax.numpy as jnp
from jax import lax
from jax.sharding import Mesh, PartitionSpec as P

ITERS = 3


epsilon_code = 0.05
sharpness_divisor = 0.1
norm_floor = 1e-06
rows_axes = ("z", "y")
proto_axes = ("x", "core")


def shifted(value, axis, steps):
    count = lax.axis_size(axis)
    pairs = [(source, (source + steps) % count) for source in range(count)]
    return lax.ppermute(value, axis, pairs)


def gathered(value, axis):
    count = lax.axis_size(axis)
    copies = jnp.broadcast_to(value[None], (count,) + value.shape)
    return lax.all_to_all(copies, axis, 0, 0, tiled=True)


def unit_rows(values):
    wide = values.astype(jnp.float32)
    scale = lax.rsqrt(jnp.mean(wide * wide, axis=1, keepdims=True) + norm_floor) / jnp.sqrt(
        jnp.float32(wide.shape[1])
    )
    return (wide * scale, scale)


def norm_back(upstream, units, scale):
    return scale * (upstream - units * jnp.sum(units * upstream, axis=1, keepdims=True))


def block(value, index, count):
    size = value.shape[0] // count
    return lax.dynamic_slice_in_dim(value, index * size, size, 0)


def scatter_sum(value, axis):
    count = lax.axis_size(axis)
    me = lax.axis_index(axis)
    total = block(value, me, count)
    for step in range(1, count):
        total = total + shifted(block(value, (me + step) % count, count), axis, step)
    return total


def gather_blocks(value, axis):
    count = lax.axis_size(axis)
    me = lax.axis_index(axis)
    pieces = [value] + [shifted(value, axis, step) for step in range(1, count)]
    out = jnp.zeros((count,) + value.shape, value.dtype)
    for step, piece in enumerate(pieces):
        out = lax.dynamic_update_slice_in_dim(out, piece[None], (me + count - step) % count, 0)
    return out.reshape((-1,) + value.shape[1:])


def contract_rows(left, right):
    return lax.dot_general(
        left, right, (((0,), (0,)), ((), ())), preferred_element_type=jnp.float32
    )


def column_scale_of(part):
    part = lax.psum(part, "y")
    return 1.0 / jnp.sum(gathered(part, "z"), axis=0)


def row_totals(*parts):
    stacked = jnp.concatenate(parts)
    total = jnp.sum(gathered(stacked, proto_axes), axis=0)
    return jnp.split(total, len(parts))


def body(embeddings, prototypes, partner):
    view_units, view_scale = unit_rows(embeddings)
    proto_units, proto_scale = unit_rows(prototypes)
    views = view_units.astype(jnp.bfloat16)
    protos = proto_units.astype(jnp.bfloat16)
    row_count = views.shape[0]
    links = jnp.remainder(partner, row_count)
    other = shifted(embeddings, "z", lax.axis_size("z") // 2)[links]
    other_views = unit_rows(other)[0].astype(jnp.bfloat16)

    scores = jnp.dot(views, protos.T, preferred_element_type=jnp.float32)
    tempered = jnp.exp(scores / sharpness_divisor)
    kernel = tempered * tempered
    soft_part = jnp.sum(tempered, axis=1)
    column_scale = column_scale_of(jnp.sum(kernel, axis=0))
    other_scores = jnp.dot(other_views, protos.T, preferred_element_type=jnp.float32)
    other_kernel = jnp.exp(other_scores / epsilon_code)
    for sweep in range(ITERS - 1):
        row_part = jnp.sum(kernel * column_scale[None, :], axis=1)
        if sweep == 0:
            row_total, soft_total = row_totals(row_part, soft_part)
        else:
            (row_total,) = row_totals(row_part)
        weight = 1.0 / row_total
        column_scale = column_scale_of(jnp.sum(weight[:, None] * kernel, axis=0))
    dispersion = other_kernel * column_scale[None, :]
    (line_total,) = row_totals(jnp.sum(dispersion, axis=1))
    codes = (dispersion * (1.0 / line_total)[:, None]).astype(jnp.bfloat16)
    likelihood = tempered * (1.0 / soft_total)[:, None]
    logit_gradient = ((likelihood - codes.astype(jnp.float32)) / sharpness_divisor).astype(
        jnp.bfloat16
    )

    proto_part = contract_rows(logit_gradient, views)
    view_part = jnp.dot(logit_gradient, protos, preferred_element_type=jnp.float32)

    y, z, x, core = (lax.axis_index(name) for name in ("y", "z", "x", "core"))
    y_count, z_count, x_count = (lax.axis_size(name) for name in ("y", "z", "x"))

    def mine(value, outer, outer_count, inner, inner_count):
        return block(block(value, outer, outer_count), inner, inner_count)

    view_sum = scatter_sum(scatter_sum(view_part, "core"), "x")
    proto_sum = scatter_sum(proto_part, "y")
    proto_sum = lax.all_to_all(
        proto_sum.reshape(z_count, -1, proto_sum.shape[1]), "z", 0, 0, tiled=True
    ).sum(axis=0)
    emb_rows = unit_rows(mine(embeddings, core, 2, x, x_count))
    proto_rows = unit_rows(mine(prototypes, y, y_count, z, z_count))
    emb_piece = norm_back(view_sum, *emb_rows)
    proto_piece = norm_back(proto_sum, *proto_rows)
    emb_grad = gather_blocks(gather_blocks(emb_piece, "x"), "core")
    proto_grad = gathered(proto_piece, "z").reshape(-1, proto_piece.shape[1])
    proto_grad = gather_blocks(proto_grad, "y")
    return (emb_grad, proto_grad)


def solution(mesh):
    inner = Mesh(mesh.devices.reshape(16, 4, 4, 2), ("z", "y", "x", "core"))
    return jax.shard_map(
        body,
        mesh=inner,
        in_specs=(P(rows_axes, None), P(proto_axes, None), P(rows_axes)),
        out_specs=(P(rows_axes, None), P(proto_axes, None)),
        check_vma=False,
    )
```

time: 1270 us -> 336 us (0.26)
  waiting for transfers between devices: 693 us -> 96.4 us
  blocking collectives: 472 us -> 79.5 us
  starting transfers between devices: 6.34 us -> 92.4 us
  between operations: 14.2 us -> 1.42 us
    psum x6 -> x3, blocking collectives: 472 us -> 24.2 us  [column_scale_of(): part = lax.psum(part, 'y')]
    psum x2 -> x0, waiting for transfers between devices: 400 us -> none  [the longest x1 270 us: body(): proto_upstream = lax.psum(contract_rows(logit_gradient, views), 'batch')]
    ppermute x1 -> x15, waiting for transfers between devices: 294 us -> 58.6 us  [shifted(): return lax.ppermute(value, axis, pairs)]
    all_to_all x0 -> x3, blocking collectives: none -> 55.4 us  [gathered(): return lax.all_to_all(copies, axis, 0, 0, tiled=True)]
    all_to_all x0 -> x5, starting transfers between devices: none -> 43.2 us  [the longest x4 35.1 us: gathered(): return lax.all_to_all(copies, axis, 0, 0, tiled=True)]
    ppermute x1 -> x15, starting transfers between devices: 6.26 us -> 49.2 us  [shifted(): return lax.ppermute(value, axis, pairs)]
    all_to_all x0 -> x5, waiting for transfers between devices: none -> 37.8 us  [the longest x4 24 us: gathered(): return lax.all_to_all(copies, axis, 0, 0, tiled=True)]
  transfers between devices with their start and end apart: 3 -> 20, of which waited for: 3 -> 16; matrix products, arithmetic and copies ran while one was open for 1% -> 5% of each run, Pallas kernels for 0% -> 0%
where the time goes in v1:
time: 336 us; the launch traced here: 334 us
  waiting for transfers between devices  96.4 us (29%)
  starting transfers between devices  92.4 us (28%)
  blocking collectives  79.5 us (24%)
  other arithmetic  36.5 us (11%)
  matrix products  15.7 us (5%)
  local copies, waits for them, and re-layouts  12 us (4%)
    ppermute x15, waiting for transfers between devices, shifted(): return lax.ppermute(value, axis, pairs)  58.6 us
    all_to_all x3, blocking collectives, gathered(): return lax.all_to_all(copies, axis, 0, 0, tiled=True)  55.4 us
    ppermute x15, starting transfers between devices, shifted(): return lax.ppermute(value, axis, pairs)  49.2 us
    all_to_all x4, starting transfers between devices, gathered(): return lax.all_to_all(copies, axis, 0, 0, tiled=True)  35.1 us
    psum x3, blocking collectives, column_scale_of(): part = lax.psum(part, 'y')  24.2 us
    all_to_all x4, waiting for transfers between devices, gathered(): return lax.all_to_all(copies, axis, 0, 0, tiled=True)  24 us
    all_to_all x1, waiting for transfers between devices, body(): lax.all_to_all(proto_sum.reshape(z_count, -1, proto_sum.shape[1]), 'z', 0...  13.8 us
    reduce_sum x2, other arithmetic, body(): row_part = jnp.sum(kernel * column_scale[None, :], axis=1)  9.64 us
  transfers between devices with their start and end apart: 20, of which 16 were waited for; matrix products, arithmetic and copies ran while one was open for 5% of the time, Pallas kernels for 0%

profile of v1, /device:TPU:1, one launch (start us, length us, event | category | flops | bytes accessed | tf_op | source)
XLA Modules:
  0.0 334.0 jit_solution(3493263576027540021)
XLA Ops:
  3.5 6.4 %fusion.3 = (f32[2048]{0:T(1024)S(1)}, f32[1024,2048]{1,0:T(8,128)}) fusion(bf16[2048,256]{1,0:T(8,128)(2,1)} %param.4, f32[2048]{0:T(1024)S(1)} %rsqrt_multiply_fusion, bf16[1024,256]{1,0:T(8,128)(2,1)} %param.3, f32[1024]{0:T(1024)S(1)} %rsqrt_multiply_fusion.2), kind=kOutput, calls=%fused_computation.14 | convolution fusion | flops 1082390528 | bytes 9981952 | tf_op jit(solution)/shard_map/dot_general | solution.py:91
  9.9 9.6 %psum.21 = f32[2048]{0:T(1024)S(1)} all-reduce(f32[2048]{0:T(1024)S(1)} %get-tuple-element.16), channel_id=1, replica_groups=mesh['z'=16,'y'=4,'x'=4,'core'=2] {'y'}, use_global_device_ids=true, to_apply=%region_4.5 | all-reduce | flops 2048 | bytes 16384 | tf_op jit(solution)/shard_map/psum | solution.py:71
  19.6 26.7 %all_to_all.46 = f32[16,1,2048]{2,1,0:T(1,128)S(1)} all-to-all(f32[16,1,2048]{2,1,0:T(1,128)S(1)} %broadcast_in_dim.40), channel_id=1, replica_groups=mesh['z'=16,'y'=4,'x'=4,'core'=2] {'z'}, dimensions={0} | all-to-all | bytes 262144 | tf_op jit(solution)/shard_map/all_to_all | solution.py:25
  51.1 13.2 %all_to_all.47 = f32[8,1,2048]{2,1,0:T(1,128)S(1)} all-to-all(f32[8,1,2048]{2,1,0:T(1,128)S(1)} %broadcast_in_dim.41), channel_id=1, replica_groups=mesh['z'=16,'y'=4,'x'=4,'core'=2] {'x','core'}, dimensions={0} | all-to-all | bytes 131072 | tf_op jit(solution)/shard_map/all_to_all | solution.py:25
  68.8 6.1 %psum.22 = f32[2048]{0:T(1024)S(1)} all-reduce(f32[2048]{0:T(1024)S(1)} %multiply_reduce_fusion.2), channel_id=1, replica_groups=mesh['z'=16,'y'=4,'x'=4,'core'=2] {'y'}, use_global_device_ids=true, to_apply=%region_11.12 | all-reduce | flops 2048 | bytes 16384 | tf_op jit(solution)/shard_map/psum | solution.py:71
  75.0 15.5 %all_to_all.48 = f32[16,1,2048]{2,1,0:T(1,128)S(1)} all-to-all(f32[16,1,2048]{2,1,0:T(1,128)S(1)} %broadcast_in_dim.43), channel_id=1, replica_groups=mesh['z'=16,'y'=4,'x'=4,'core'=2] {'z'}, dimensions={0} | all-to-all | bytes 262144 | tf_op jit(solution)/shard_map/all_to_all | solution.py:25
  90.6 5.1 %multiply_reduce_fusion.1 = f32[1024]{0:T(1024)S(1)} fusion(f32[2048]{0:T(1024)S(1)} %broadcast_divide_fusion.1, f32[1024,2048]{1,0:T(8,128)} %get-tuple-element.17), kind=kLoop, calls=%fused_computation.4 | loop fusion | flops 8387584 | bytes 8400896 | tf_op jit(solution)/shard_map/reduce_sum | solution.py:99
  96.3 7.3 %all-to-all-start.3 = ((f32[8,1,1024]{2,1,0:T(1,128)}), f32[8,1,1024]{2,1,0:T(1,128)S(1)}, u32[]{:S(2)}, u32[]{:S(2)}) async-start(f32[8,1,1024]{2,1,0:T(1,128)} %broadcast_in_dim.44), calls=%async_computation.3 | async-start | bytes 65536 | tf_op jit(solution)/shard_map/all_to_all | solution.py:25
  112.8 8.4 %psum.23 = f32[2048]{0:T(1024)S(1)} all-reduce(f32[2048]{0:T(1024)S(1)} %multiply_reduce_fusion), channel_id=1, replica_groups=mesh['z'=16,'y'=4,'x'=4,'core'=2] {'y'}, use_global_device_ids=true, to_apply=%region_16.17 | all-reduce | flops 2048 | bytes 16384 | tf_op jit(solution)/shard_map/psum | solution.py:71
  122.0 8.7 %all-to-all-start.4 = ((f32[16,1,2048]{2,1,0:T(1,128)}), f32[16,1,2048]{2,1,0:T(1,128)S(1)}, u32[]{:S(2)}, u32[]{:S(2)}) async-start(f32[16,1,2048]{2,1,0:T(1,128)} %broadcast_in_dim.45), calls=%async_computation.4 | async-start | bytes 262144 | tf_op jit(solution)/shard_map/all_to_all | solution.py:25
  130.8 11.1 %collective-permute-done = bf16[1024,256]{1,0:T(8,128)(2,1)S(1)} collective-permute-done((bf16[1024,256]{1,0:T(8,128)(2,1)S(1)}, bf16[1024,256]{1,0:T(8,128)(2,1)S(1)}, u32[]{:S(2)}, u32[]{:S(2)}) %collective-permute-start) | collective-permute-done | bytes 524320 | tf_op jit(solution)/shard_map/ppermute | solution.py:19
  146.1 18.7 %all-to-all-done.4 = f32[16,1,2048]{2,1,0:T(1,128)S(1)} async-done(((f32[16,1,2048]{2,1,0:T(1,128)}), f32[16,1,2048]{2,1,0:T(1,128)S(1)}, u32[]{:S(2)}, u32[]{:S(2)}) %all-to-all-start.4) | async-done | bytes 131104 | tf_op jit(solution)/shard_map/all_to_all | solution.py:25
  169.7 6.4 %all-to-all-start.5 = ((f32[8,1,1024]{2,1,0:T(1,128)}), f32[8,1,1024]{2,1,0:T(1,128)S(1)}, u32[]{:S(2)}, u32[]{:S(2)}) async-start(f32[8,1,1024]{2,1,0:T(1,128)} %broadcast_in_dim.46), calls=%async_computation.5 | async-start | bytes 65536 | tf_op jit(solution)/shard_map/all_to_all | solution.py:25
  176.0 4.7 %all-to-all-done.5 = f32[8,1,1024]{2,1,0:T(1,128)S(1)} async-done(((f32[8,1,1024]{2,1,0:T(1,128)}), f32[8,1,1024]{2,1,0:T(1,128)S(1)}, u32[]{:S(2)}, u32[]{:S(2)}) %all-to-all-start.5) | async-done | bytes 32800 | tf_op jit(solution)/shard_map/all_to_all | solution.py:25
  180.8 7.5 %multiply_convert_fusion = bf16[1024,2048]{1,0:T(8,128)(2,1)S(1)} fusion(f32[1024,2048]{1,0:T(8,128)} %get-tuple-element.17, f32[1024,2048]{1,0:T(8,128)} %get-tuple-element.19, f32[1024]{0:T(1024)S(1)} %broadcast_divide_fusion.3, f32[2048]{0:T(1024)S(1)} %broadcast_divide_fusion, f32[1024]{0:T(1024)S(1)} %get-tuple-element.14), kind=kLoop, calls=%fused_computation.1 | loop fusion | flops 20971520 | bytes 20987904 | tf_op jit(solution)/shard_map/convert_element_type | solution.py:110
  195.9 4.9 %collective-permute-start.11 = (f32[512,256]{1,0:T(8,128)}, f32[512,256]{1,0:T(8,128)}, u32[]{:S(2)}, u32[]{:S(2)}) collective-permute-start(f32[512,256]{1,0:T(8,128)} %get-tuple-element.9), channel_id=1, source_target_pairs={{0,24},{8,0},{16,8},{24,16},{1,25},{9,1},{17,9},{25,17},{2,26},{10... | collective-permute-start | bytes 1572872 | tf_op jit(solution)/shard_map/ppermute | solution.py:19
  202.7 6.8 %collective-permute-done.10 = f32[512,256]{1,0:T(8,128)} collective-permute-done((f32[512,256]{1,0:T(8,128)}, f32[512,256]{1,0:T(8,128)}, u32[]{:S(2)}, u32[]{:S(2)}) %collective-permute-start.10) | collective-permute-done | bytes 524320 | tf_op jit(solution)/shard_map/ppermute | solution.py:19
  209.5 10.4 %collective-permute-done.11 = f32[512,256]{1,0:T(8,128)} collective-permute-done((f32[512,256]{1,0:T(8,128)}, f32[512,256]{1,0:T(8,128)}, u32[]{:S(2)}, u32[]{:S(2)}) %collective-permute-start.11) | collective-permute-done | bytes 524320 | tf_op jit(solution)/shard_map/ppermute | solution.py:19
  224.1 8.1 %all-to-all-start.6 = ((f32[16,32,256]{2,1,0:T(8,128)}), f32[16,32,256]{2,1,0:T(8,128)S(1)}, u32[]{:S(2)}, u32[]{:S(2)}) async-start(f32[16,32,256]{2,1,0:T(8,128)} %bitcast.8), calls=%async_computation.6 | async-start | bytes 1048576 | tf_op jit(solution)/shard_map/all_to_all | solution.py:125
  241.3 13.8 %all-to-all-done.6 = f32[16,32,256]{2,1,0:T(8,128)S(1)} async-done(((f32[16,32,256]{2,1,0:T(8,128)}), f32[16,32,256]{2,1,0:T(8,128)S(1)}, u32[]{:S(2)}, u32[]{:S(2)}) %all-to-all-start.6) | async-done | bytes 524320 | tf_op jit(solution)/shard_map/all_to_all | solution.py:125
  256.2 12.7 %all-to-all-start.7 = ((f32[16,32,256]{2,1,0:T(8,128)}), f32[16,32,256]{2,1,0:T(8,128)S(1)}, u32[]{:S(2)}, u32[]{:S(2)}) async-start(f32[16,32,256]{2,1,0:T(8,128)} %broadcast_in_dim.53), calls=%async_computation.7 | async-start | bytes 1048576 | tf_op jit(solution)/shard_map/all_to_all | solution.py:25
  286.2 5.5 %collective-permute-start.6 = (f32[128,256]{1,0:T(8,128)S(1)}, f32[128,256]{1,0:T(8,128)S(1)}, u32[]{:S(2)}, u32[]{:S(2)}) collective-permute-start(f32[128,256]{1,0:T(8,128)S(1)} %get-tuple-element.5), channel_id=1, source_target_pairs={{0,4},{2,6},{4,0},{6,2},{1,5},{3,7},{5,1},{7,3},{8,12},{10,14},{12... | collective-permute-start | bytes 393224 | tf_op jit(solution)/shard_map/ppermute | solution.py:19
  312.9 6.1 %collective-permute-done.12 = f32[512,256]{1,0:T(8,128)S(1)} collective-permute-done((f32[512,256]{1,0:T(8,128)S(1)}, f32[512,256]{1,0:T(8,128)S(1)}, u32[]{:S(2)}, u32[]{:S(2)}) %collective-permute-start.12) | collective-permute-done | bytes 524320 | tf_op jit(solution)/shard_map/ppermute | solution.py:19
  319.1 11.6 %collective-permute-done.13 = f32[512,256]{1,0:T(8,128)S(1)} collective-permute-done((f32[512,256]{1,0:T(8,128)S(1)}, f32[512,256]{1,0:T(8,128)S(1)}, u32[]{:S(2)}, u32[]{:S(2)}) %collective-permute-start.13) | collective-permute-done | bytes 524320 | tf_op jit(solution)/shard_map/ppermute | solution.py:19
  (99 shorter events, 97.2 us)
Async XLA Ops:
  64.3 39.3 %copy-start.4 = (bf16[1024,256]{1,0:T(8,128)(2,1)S(1)}, bf16[1024,256]{1,0:T(8,128)(2,1)}, u32[]{:S(2)}) copy-start(bf16[1024,256]{1,0:T(8,128)(2,1)} %param.3) | copy-start | bytes 1572868
  90.6 40.1 %copy-start.6 = (s32[1024]{0:T(1024)S(1)}, s32[1024]{0:T(1024)}, u32[]{:S(2)}) copy-start(s32[1024]{0:T(1024)} %param.5) | copy-start | bytes 12292
  95.7 69.1 %copy-start.2 = (bf16[2048,256]{1,0:T(8,128)(2,1)S(1)}, bf16[2048,256]{1,0:T(8,128)(2,1)}, u32[]{:S(2)}) copy-start(bf16[2048,256]{1,0:T(8,128)(2,1)} %param.4) | copy-start | bytes 3145732
  96.3 12.0 %all-to-all-start.3 = ((f32[8,1,1024]{2,1,0:T(1,128)}), f32[8,1,1024]{2,1,0:T(1,128)S(1)}, u32[]{:S(2)}, u32[]{:S(2)}) async-start(f32[8,1,1024]{2,1,0:T(1,128)} %broadcast_in_dim.44), calls=%async_computation.3 | async-start | bytes 65536 | tf_op jit(solution)/shard_map/all_to_all | solution.py:25
  103.6 38.3 %collective-permute-start = (bf16[1024,256]{1,0:T(8,128)(2,1)S(1)}, bf16[1024,256]{1,0:T(8,128)(2,1)S(1)}, u32[]{:S(2)}, u32[]{:S(2)}) collective-permute-start(bf16[1024,256]{1,0:T(8,128)(2,1)S(1)} %copy-done.4), channel_id=1, source_target_pairs={{0,256},{32,288},{64,320},{96,352},{128,384},{160,416},{192,448},{... | collective-permute-start | bytes 1572872 | tf_op jit(solution)/shard_map/ppermute | solution.py:19
  122.0 42.7 %all-to-all-start.4 = ((f32[16,1,2048]{2,1,0:T(1,128)}), f32[16,1,2048]{2,1,0:T(1,128)S(1)}, u32[]{:S(2)}, u32[]{:S(2)}) async-start(f32[16,1,2048]{2,1,0:T(1,128)} %broadcast_in_dim.45), calls=%async_computation.4 | async-start | bytes 262144 | tf_op jit(solution)/shard_map/all_to_all | solution.py:25
  169.7 11.1 %all-to-all-start.5 = ((f32[8,1,1024]{2,1,0:T(1,128)}), f32[8,1,1024]{2,1,0:T(1,128)S(1)}, u32[]{:S(2)}, u32[]{:S(2)}) async-start(f32[8,1,1024]{2,1,0:T(1,128)} %broadcast_in_dim.46), calls=%async_computation.5 | async-start | bytes 65536 | tf_op jit(solution)/shard_map/all_to_all | solution.py:25
  193.0 16.5 %collective-permute-start.10 = (f32[512,256]{1,0:T(8,128)}, f32[512,256]{1,0:T(8,128)}, u32[]{:S(2)}, u32[]{:S(2)}) collective-permute-start(f32[512,256]{1,0:T(8,128)} %get-tuple-element.10), channel_id=1, source_target_pairs={{0,16},{8,24},{16,0},{24,8},{1,17},{9,25},{17,1},{25,9},{2,18},{10... | collective-permute-start | bytes 1572872 | tf_op jit(solution)/shard_map/ppermute | solution.py:19
  195.9 24.0 %collective-permute-start.11 = (f32[512,256]{1,0:T(8,128)}, f32[512,256]{1,0:T(8,128)}, u32[]{:S(2)}, u32[]{:S(2)}) collective-permute-start(f32[512,256]{1,0:T(8,128)} %get-tuple-element.9), channel_id=1, source_target_pairs={{0,24},{8,0},{16,8},{24,16},{1,25},{9,1},{17,9},{25,17},{2,26},{10... | collective-permute-start | bytes 1572872 | tf_op jit(solution)/shard_map/ppermute | solution.py:19
  200.8 21.1 %collective-permute-start.9 = (f32[512,256]{1,0:T(8,128)}, f32[512,256]{1,0:T(8,128)}, u32[]{:S(2)}, u32[]{:S(2)}) collective-permute-start(f32[512,256]{1,0:T(8,128)} %get-tuple-element.8), channel_id=1, source_target_pairs={{0,8},{8,16},{16,24},{24,0},{1,9},{9,17},{17,25},{25,1},{2,10},{10... | collective-permute-start | bytes 1572872 | tf_op jit(solution)/shard_map/ppermute | solution.py:19
  224.1 31.0 %all-to-all-start.6 = ((f32[16,32,256]{2,1,0:T(8,128)}), f32[16,32,256]{2,1,0:T(8,128)S(1)}, u32[]{:S(2)}, u32[]{:S(2)}) async-start(f32[16,32,256]{2,1,0:T(8,128)} %bitcast.8), calls=%async_computation.6 | async-start | bytes 1048576 | tf_op jit(solution)/shard_map/all_to_all | solution.py:125
  235.9 4.3 %collective-permute-start.1 = (f32[512,256]{1,0:T(8,128)S(1)}, f32[512,256]{1,0:T(8,128)}, u32[]{:S(2)}, u32[]{:S(2)}) collective-permute-start(f32[512,256]{1,0:T(8,128)S(1)} %constant_dynamic-slice_fusion.6), channel_id=1, source_target_pairs={{0,1},{1,0},{2,3},{3,2},{4,5},{5,4},{6,7},{7,6},{8,9},{9,8},{10,11... | collective-permute-start | bytes 1572872 | tf_op jit(solution)/shard_map/ppermute | solution.py:19
  256.2 46.1 %all-to-all-start.7 = ((f32[16,32,256]{2,1,0:T(8,128)}), f32[16,32,256]{2,1,0:T(8,128)S(1)}, u32[]{:S(2)}, u32[]{:S(2)}) async-start(f32[16,32,256]{2,1,0:T(8,128)} %broadcast_in_dim.53), calls=%async_computation.7 | async-start | bytes 1048576 | tf_op jit(solution)/shard_map/all_to_all | solution.py:25
  269.0 8.6 %collective-permute-start.2 = (f32[128,256]{1,0:T(8,128)S(1)}, f32[128,256]{1,0:T(8,128)S(1)}, u32[]{:S(2)}, u32[]{:S(2)}) collective-permute-start(f32[128,256]{1,0:T(8,128)S(1)} %get-tuple-element.11), channel_id=1, source_target_pairs={{0,2},{2,4},{4,6},{6,0},{1,3},{3,5},{5,7},{7,1},{8,10},{10,12},{12... | collective-permute-start | bytes 393224 | tf_op jit(solution)/shard_map/ppermute | solution.py:19
  271.2 7.3 %collective-permute-start.3 = (f32[128,256]{1,0:T(8,128)S(1)}, f32[128,256]{1,0:T(8,128)S(1)}, u32[]{:S(2)}, u32[]{:S(2)}) collective-permute-start(f32[128,256]{1,0:T(8,128)S(1)} %get-tuple-element.13), channel_id=1, source_target_pairs={{0,4},{2,6},{4,0},{6,2},{1,5},{3,7},{5,1},{7,3},{8,12},{10,14},{12... | collective-permute-start | bytes 393224 | tf_op jit(solution)/shard_map/ppermute | solution.py:19
  274.9 7.0 %collective-permute-start.4 = (f32[128,256]{1,0:T(8,128)S(1)}, f32[128,256]{1,0:T(8,128)S(1)}, u32[]{:S(2)}, u32[]{:S(2)}) collective-permute-start(f32[128,256]{1,0:T(8,128)S(1)} %get-tuple-element.12), channel_id=1, source_target_pairs={{0,6},{2,0},{4,2},{6,4},{1,7},{3,1},{5,3},{7,5},{8,14},{10,8},{12,... | collective-permute-start | bytes 393224 | tf_op jit(solution)/shard_map/ppermute | solution.py:19
  284.0 9.6 %collective-permute-start.5 = (f32[128,256]{1,0:T(8,128)S(1)}, f32[128,256]{1,0:T(8,128)S(1)}, u32[]{:S(2)}, u32[]{:S(2)}) collective-permute-start(f32[128,256]{1,0:T(8,128)S(1)} %get-tuple-element.5), channel_id=1, source_target_pairs={{0,2},{2,4},{4,6},{6,0},{1,3},{3,5},{5,7},{7,1},{8,10},{10,12},{12... | collective-permute-start | bytes 393224 | tf_op jit(solution)/shard_map/ppermute | solution.py:19
  286.2 9.6 %collective-permute-start.6 = (f32[128,256]{1,0:T(8,128)S(1)}, f32[128,256]{1,0:T(8,128)S(1)}, u32[]{:S(2)}, u32[]{:S(2)}) collective-permute-start(f32[128,256]{1,0:T(8,128)S(1)} %get-tuple-element.5), channel_id=1, source_target_pairs={{0,4},{2,6},{4,0},{6,2},{1,5},{3,7},{5,1},{7,3},{8,12},{10,14},{12... | collective-permute-start | bytes 393224 | tf_op jit(solution)/shard_map/ppermute | solution.py:19
  291.7 6.0 %collective-permute-start.7 = (f32[128,256]{1,0:T(8,128)S(1)}, f32[128,256]{1,0:T(8,128)S(1)}, u32[]{:S(2)}, u32[]{:S(2)}) collective-permute-start(f32[128,256]{1,0:T(8,128)S(1)} %get-tuple-element.5), channel_id=1, source_target_pairs={{0,6},{2,0},{4,2},{6,4},{1,7},{3,1},{5,3},{7,5},{8,14},{10,8},{12,... | collective-permute-start | bytes 393224 | tf_op jit(solution)/shard_map/ppermute | solution.py:19
  297.7 11.7 %collective-permute-start.8 = (f32[512,256]{1,0:T(8,128)S(1)}, f32[512,256]{1,0:T(8,128)S(1)}, u32[]{:S(2)}, u32[]{:S(2)}) collective-permute-start(f32[512,256]{1,0:T(8,128)S(1)} %bitcast.34), channel_id=1, source_target_pairs={{0,1},{1,0},{2,3},{3,2},{4,5},{5,4},{6,7},{7,6},{8,9},{9,8},{10,11... | collective-permute-start | bytes 1572872 | tf_op jit(solution)/shard_map/ppermute | solution.py:19
  302.4 16.6 %collective-permute-start.12 = (f32[512,256]{1,0:T(8,128)S(1)}, f32[512,256]{1,0:T(8,128)S(1)}, u32[]{:S(2)}, u32[]{:S(2)}) collective-permute-start(f32[512,256]{1,0:T(8,128)S(1)} %bitcast.30), channel_id=1, source_target_pairs={{0,8},{8,16},{16,24},{24,0},{1,9},{9,17},{17,25},{25,1},{2,10},{10... | collective-permute-start | bytes 1572872 | tf_op jit(solution)/shard_map/ppermute | solution.py:19
  306.4 24.3 %collective-permute-start.13 = (f32[512,256]{1,0:T(8,128)S(1)}, f32[512,256]{1,0:T(8,128)S(1)}, u32[]{:S(2)}, u32[]{:S(2)}) collective-permute-start(f32[512,256]{1,0:T(8,128)S(1)} %bitcast.31), channel_id=1, source_target_pairs={{0,16},{8,24},{16,0},{24,8},{1,17},{9,25},{17,1},{25,9},{2,18},{10... | collective-permute-start | bytes 1572872 | tf_op jit(solution)/shard_map/ppermute | solution.py:19
  309.5 23.2 %copy-start.3 = (f32[2,512,256]{2,1,0:T(8,128)}, f32[2,512,256]{2,1,0:T(8,128)S(1)}, u32[]{:S(2)}) copy-start(f32[2,512,256]{2,1,0:T(8,128)S(1)} %bitcast_dynamic-update-slice_fusion.4) | copy-start | bytes 3145732
  309.5 23.1 %collective-permute-start.14 = (f32[512,256]{1,0:T(8,128)S(1)}, f32[512,256]{1,0:T(8,128)S(1)}, u32[]{:S(2)}, u32[]{:S(2)}) collective-permute-start(f32[512,256]{1,0:T(8,128)S(1)} %bitcast.32), channel_id=1, source_target_pairs={{0,24},{8,0},{16,8},{24,16},{1,25},{9,1},{17,9},{25,17},{2,26},{10... | collective-permute-start | bytes 1572872 | tf_op jit(solution)/shard_map/ppermute | solution.py:19
  (3 other events, 12.7 us)

commit v2 on v0

v2 whole, which is shorter than its diff:
```python
import functools

import jax
import jax.numpy as jnp
from jax import lax
from jax.experimental import pallas as pl
from jax.experimental.pallas import tpu as pltpu
from jax.sharding import Mesh, PartitionSpec as P

ITERS = 3


epsilon_code = 0.05
sharpness_divisor = 0.1
norm_floor = 1e-06
rows_axes = ("z", "y")
proto_axes = ("x", "core")
LANES = 128
ROWS = 256
f32 = jnp.float32
bf16 = jnp.bfloat16


def shifted(value, axis, steps):
    count = lax.axis_size(axis)
    pairs = [(source, (source + steps) % count) for source in range(count)]
    return lax.ppermute(value, axis, pairs)


def exchanged(value, axis):
    return lax.all_to_all(value, axis, 0, 0, tiled=True)


def gathered(value, axis):
    return exchanged(jnp.broadcast_to(value[None], (lax.axis_size(axis),) + value.shape), axis)


def unit_rows(values):
    wide = values.astype(f32)
    scale = lax.rsqrt(jnp.mean(wide * wide, axis=1, keepdims=True) + norm_floor) / jnp.sqrt(
        f32(wide.shape[1])
    )
    return (wide * scale, scale)


def norm_back(upstream, units, scale):
    return scale * (upstream - units * jnp.sum(units * upstream, axis=1, keepdims=True))


def block(value, index, count):
    size = value.shape[0] // count
    return lax.dynamic_slice_in_dim(value, index * size, size, 0)


def kernel_units(values):
    wide = values.astype(f32)
    mean = jnp.sum(wide * wide, axis=1, keepdims=True) * (1.0 / wide.shape[1])
    scale = lax.rsqrt(mean + norm_floor) * (1.0 / wide.shape[1] ** 0.5)
    return (wide * scale).astype(bf16)


def lane_sums(values):
    total = values[:, :LANES]
    for start in range(LANES, values.shape[1], LANES):
        total = total + values[:, start : start + LANES]
    return total


def as_row(partials):
    return jnp.sum(partials.T, axis=0, keepdims=True)


def as_column(row):
    return jnp.broadcast_to(row, (LANES, row.shape[1])).T


def tempered_kernel(emb_ref, proto_ref, temp_ref, views_ref, protos_ref, col_ref, soft_ref):
    protos_ref[...] = kernel_units(proto_ref[...])
    views_ref[...] = kernel_units(emb_ref[...])
    col_ref[...] = jnp.zeros_like(col_ref)

    @pl.loop(0, emb_ref.shape[0] // ROWS)
    def _(step):
        rows = pl.ds(pl.multiple_of(step * ROWS, ROWS), ROWS)
        scores = lax.dot_general(
            views_ref[rows, :],
            protos_ref[...],
            (((1,), (1,)), ((), ())),
            preferred_element_type=f32,
        )
        tempered = jnp.exp(scores * (1.0 / sharpness_divisor))
        temp_ref[rows, :] = tempered
        col_ref[...] += jnp.sum(tempered * tempered, axis=0, keepdims=True)
        soft_ref[:, rows] = as_row(lane_sums(tempered))


def codes_kernel(emb_ref, protos_ref, kernel_ref):
    @pl.loop(0, emb_ref.shape[0] // ROWS)
    def _(step):
        rows = pl.ds(pl.multiple_of(step * ROWS, ROWS), ROWS)
        scores = lax.dot_general(
            kernel_units(emb_ref[rows, :]),
            protos_ref[...],
            (((1,), (1,)), ((), ())),
            preferred_element_type=f32,
        )
        kernel_ref[rows, :] = jnp.exp(scores * (1.0 / epsilon_code))


def row_kernel(squared, temp_ref, totals_ref, row_ref):
    column_scale = 1.0 / jnp.sum(totals_ref[:, 0, :], axis=0, keepdims=True)

    @pl.loop(0, temp_ref.shape[0] // ROWS)
    def _(step):
        rows = pl.ds(pl.multiple_of(step * ROWS, ROWS), ROWS)
        value = temp_ref[rows, :]
        value = value * value if squared else value
        row_ref[:, rows] = as_row(lane_sums(value * column_scale))


def col_kernel(temp_ref, totals_ref, col_ref):
    count = temp_ref.shape[0]
    weight = 1.0 / jnp.sum(totals_ref[:, 0, :count], axis=0, keepdims=True)
    col_ref[...] = jnp.zeros_like(col_ref)
    for step in range(count // ROWS):
        wide = as_column(weight[:, step * ROWS : (step + 1) * ROWS])
        for start in range(0, temp_ref.shape[1], LANES):
            value = temp_ref[step * ROWS : (step + 1) * ROWS, start : start + LANES]
            col_ref[:, start : start + LANES] += jnp.sum(value * value * wide, axis=0, keepdims=True)


def gradient_kernel(
    temp_ref, other_ref, totals_ref, line_ref, soft_ref, views_ref, protos_ref, view_ref, proto_ref
):
    count = temp_ref.shape[0]
    column_scale = 1.0 / jnp.sum(totals_ref[:, 0, :], axis=0, keepdims=True)
    line = 1.0 / jnp.sum(line_ref[:, 0, :], axis=0, keepdims=True)
    soft = 1.0 / jnp.sum(soft_ref[:, 0, count:], axis=0, keepdims=True)
    proto_ref[...] = jnp.zeros_like(proto_ref)
    for step in range(count // ROWS):
        rows = slice(step * ROWS, (step + 1) * ROWS)
        line_wide = as_column(line[:, rows])[:, :1]
        soft_wide = as_column(soft[:, rows])[:, :1]
        codes = (other_ref[rows, :] * column_scale * line_wide).astype(bf16)
        likelihood = temp_ref[rows, :] * soft_wide
        grad = ((likelihood - codes.astype(f32)) * (1.0 / sharpness_divisor)).astype(bf16)
        view_ref[rows, :] = jnp.dot(grad, protos_ref[...], preferred_element_type=f32)
        proto_ref[...] += lax.dot_general(
            grad, views_ref[rows, :], (((0,), (0,)), ((), ())), preferred_element_type=f32
        )


def call(kernel, name, out_shape, *args, flops, size, exps=0, limit=16):
    return pl.pallas_call(
        kernel,
        name=name,
        out_shape=out_shape,
        in_specs=[pl.BlockSpec(memory_space=pltpu.VMEM)] * len(args),
        out_specs=jax.tree.map(lambda _: pl.BlockSpec(memory_space=pltpu.VMEM), out_shape),
        compiler_params=pltpu.CompilerParams(vmem_limit_bytes=limit * 2**20),
        cost_estimate=pl.CostEstimate(flops=flops, bytes_accessed=size, transcendentals=exps),
    )(*args)


def body(embeddings, prototypes, partner):
    count, width = embeddings.shape
    slots = prototypes.shape[0]
    shape = jax.ShapeDtypeStruct
    entries = count * slots
    links = jnp.remainder(partner, count)
    sent = shifted(embeddings, "z", lax.axis_size("z") // 2)

    tempered, views, protos, column_part, soft_part = call(
        tempered_kernel,
        "tempered",
        (
            pltpu.VMEM((count, slots), f32),
            shape((count, width), bf16),
            shape((slots, width), bf16),
            shape((1, slots), f32),
            shape((1, count), f32),
        ),
        embeddings,
        prototypes,
        flops=2 * entries * width,
        size=4 * entries,
        exps=entries,
    )

    def column_totals(part):
        return gathered(lax.psum(part, "y"), "z")

    def row_pass(squared, values, totals):
        return call(
            functools.partial(row_kernel, squared),
            "row_pass",
            shape((1, count), f32),
            values,
            totals,
            flops=3 * entries,
            size=4 * entries,
        )

    def column_pass(values, totals):
        return call(
            col_kernel,
            "column_pass",
            shape((1, slots), f32),
            values,
            totals,
            flops=3 * entries,
            size=4 * entries,
        )

    column_total = column_totals(column_part)
    row_part = row_pass(True, tempered, column_total)
    first = gathered(jnp.concatenate([row_part, soft_part], axis=1), proto_axes)
    first, sent = lax.optimization_barrier((first, sent))
    other = sent[links]
    column_total = column_totals(column_pass(tempered, first))
    for sweep in range(ITERS - 2):
        row_total = gathered(row_pass(True, tempered, column_total), proto_axes)
        column_total = column_totals(column_pass(tempered, row_total))
    other_kernel = call(
        codes_kernel,
        "partner_codes",
        pltpu.VMEM((count, slots), f32),
        other,
        protos,
        flops=2 * entries * width,
        size=4 * entries,
        exps=entries,
    )
    line_total = gathered(row_pass(False, other_kernel, column_total), proto_axes)
    view_part, proto_part = call(
        gradient_kernel,
        "gradient",
        (shape((count, width), f32), shape((slots, width), f32)),
        tempered,
        other_kernel,
        column_total,
        line_total,
        first,
        views,
        protos,
        flops=4 * entries * width,
        size=8 * entries,
    )

    y, z, x, core = (lax.axis_index(name) for name in ("y", "z", "x", "core"))
    y_count, z_count, x_count = (lax.axis_size(name) for name in ("y", "z", "x"))

    view_sum = exchanged(view_part.reshape(2 * x_count, -1, width), proto_axes).sum(axis=0)
    proto_sum = exchanged(proto_part.reshape(y_count, -1, width), "y").sum(axis=0)
    proto_sum = exchanged(proto_sum.reshape(z_count, -1, width), "z").sum(axis=0)
    emb_rows = unit_rows(block(embeddings, x * 2 + core, 2 * x_count))
    proto_rows = unit_rows(block(prototypes, y * z_count + z, y_count * z_count))
    emb_grad = gathered(norm_back(view_sum, *emb_rows), proto_axes).reshape(count, width)
    proto_grad = gathered(norm_back(proto_sum, *proto_rows), "z").reshape(-1, width)
    proto_grad = gathered(proto_grad, "y").reshape(slots, width)
    return (emb_grad, proto_grad)


def solution(mesh):
    inner = Mesh(mesh.devices.reshape(16, 4, 4, 2), ("z", "y", "x", "core"))
    return jax.shard_map(
        body,
        mesh=inner,
        in_specs=(P(rows_axes, None), P(proto_axes, None), P(rows_axes)),
        out_specs=(P(rows_axes, None), P(proto_axes, None)),
        check_vma=False,
    )
```

time: 1270 us -> 364 us (0.29)
  the two profiles are of different devices: /device:TPU:1 before, /device:TPU:32 now
where the time goes in v2:
time: 364 us; the launch traced here: 362 us
  blocking collectives  131 us (36%)
  waiting for transfers between devices  118 us (32%)
  starting transfers between devices  55.5 us (15%)
  local copies, waits for them, and re-layouts  36.6 us (10%)
  Pallas kernels  15.4 us (4%)
  other arithmetic  5.27 us (1%)
    all_to_all x5, blocking collectives, exchanged(): return lax.all_to_all(value, axis, 0, 0, tiled=True)  103 us
    all_to_all x7, waiting for transfers between devices, exchanged(): return lax.all_to_all(value, axis, 0, 0, tiled=True)  82.6 us
    all_to_all x7, starting transfers between devices, exchanged(): return lax.all_to_all(value, axis, 0, 0, tiled=True)  44.4 us
    ppermute x1, waiting for transfers between devices, shifted(): return lax.ppermute(value, axis, pairs)  34.9 us
    psum x3, blocking collectives, column_totals(): return gathered(lax.psum(part, 'y'), 'z')  28.6 us
    unnamed x26, local copies, waits for them, and re-layouts  27.9 us
    pallas_call x8, Pallas kernels, call(): pl.pallas_call(kernel, name=name, out_shape=out_shape, in_specs=[pl.Block...  15.4 us
    ppermute x1, starting transfers between devices, shifted(): return lax.ppermute(value, axis, pairs)  11.2 us
  transfers between devices with their start and end apart: 8, of which 7 were waited for; matrix products, arithmetic and copies ran while one was open for 3% of the time, Pallas kernels for 1%

profile of v2, /device:TPU:32, one launch (start us, length us, event | category | flops | bytes accessed | tf_op | source)
XLA Modules:
  0.0 362.4 jit_solution(11934949622226985829)
XLA Ops:
  2.9 3.4 tempered.1
  9.6 10.8 %psum.21 = f32[2048]{0:T(1024)S(1)} all-reduce(f32[2048]{0:T(1024)S(1)} %bitcast.17), channel_id=1, replica_groups=mesh['z'=16,'y'=4,'x'=4,'core'=2] {'y'}, use_global_device_ids=true, to_apply=%region_1.2 | all-reduce | flops 2048 | bytes 16384 | tf_op jit(solution)/shard_map/psum | solution.py:191
  21.1 15.2 %all-to-all-start = ((f32[16,1,2048]{2,1,0:T(1,128)}), f32[16,1,2048]{2,1,0:T(1,128)S(1)}, u32[]{:S(2)}, u32[]{:S(2)}) async-start(f32[16,1,2048]{2,1,0:T(1,128)} %broadcast_in_dim.35), calls=%async_computation | async-start | bytes 262144 | tf_op jit(solution)/shard_map/all_to_all | solution.py:31
  36.4 11.2 %collective-permute-start = (bf16[1024,256]{1,0:T(8,128)(2,1)S(1)}, bf16[1024,256]{1,0:T(8,128)(2,1)S(1)}, u32[]{:S(2)}, u32[]{:S(2)}) collective-permute-start(bf16[1024,256]{1,0:T(8,128)(2,1)S(1)} %copy-done.9), channel_id=1, source_target_pairs={{0,256},{32,288},{64,320},{96,352},{128,384},{160,416},{192,448},{... | collective-permute-start | bytes 1572872 | tf_op jit(solution)/shard_map/ppermute | solution.py:27
  55.4 4.3 %all-to-all-start.1 = ((f32[8,1,2048]{2,1,0:T(1,128)}), f32[8,1,2048]{2,1,0:T(1,128)S(1)}, u32[]{:S(2)}, u32[]{:S(2)}) async-start(f32[8,1,2048]{2,1,0:T(1,128)} %broadcast_in_dim.37), calls=%async_computation.1 | async-start | bytes 131072 | tf_op jit(solution)/shard_map/all_to_all | solution.py:31
  59.7 34.9 %collective-permute-done = bf16[1024,256]{1,0:T(8,128)(2,1)S(1)} collective-permute-done((bf16[1024,256]{1,0:T(8,128)(2,1)S(1)}, bf16[1024,256]{1,0:T(8,128)(2,1)S(1)}, u32[]{:S(2)}, u32[]{:S(2)}) %collective-permute-start) | collective-permute-done | bytes 524320 | tf_op jit(solution)/shard_map/ppermute | solution.py:27
  98.9 7.9 %psum.22 = f32[2048]{0:T(1024)S(1)} all-reduce(f32[2048]{0:T(1024)S(1)} %bitcast.14), channel_id=1, replica_groups=mesh['z'=16,'y'=4,'x'=4,'core'=2] {'y'}, use_global_device_ids=true, to_apply=%region_2.3 | all-reduce | flops 2048 | bytes 16384 | tf_op jit(solution)/shard_map/psum | solution.py:191
  106.9 21.3 %all_to_all.60.totals_ref = f32[16,1,2048]{2,1,0:T(1,128)S(1)} all-to-all(f32[16,1,2048]{2,1,0:T(1,128)S(1)} %broadcast_in_dim.80), channel_id=1, replica_groups=mesh['z'=16,'y'=4,'x'=4,'core'=2] {'z'}, dimensions={0} | all-to-all | bytes 262144 | tf_op jit(solution)/shard_map/all_to_all | solution.py:31
  132.8 9.2 %all_to_all.61.totals_ref = f32[8,1,1024]{2,1,0:T(1,128)S(1)} all-to-all(f32[8,1,1024]{2,1,0:T(1,128)S(1)} %broadcast_in_dim.82), channel_id=1, replica_groups=mesh['z'=16,'y'=4,'x'=4,'core'=2] {'x','core'}, dimensions={0} | all-to-all | bytes 65536 | tf_op jit(solution)/shard_map/all_to_all | solution.py:31
  143.0 9.9 %psum.23 = f32[2048]{0:T(1024)S(1)} all-reduce(f32[2048]{0:T(1024)S(1)} %bitcast.13), channel_id=1, replica_groups=mesh['z'=16,'y'=4,'x'=4,'core'=2] {'y'}, use_global_device_ids=true, to_apply=%region_3.4 | all-reduce | flops 2048 | bytes 16384 | tf_op jit(solution)/shard_map/psum | solution.py:191
  153.6 4.6 %all-to-all-start.4 = ((f32[16,1,2048]{2,1,0:T(1,128)}), f32[16,1,2048]{2,1,0:T(1,128)S(1)}, u32[]{:S(2)}, u32[]{:S(2)}) async-start(f32[16,1,2048]{2,1,0:T(1,128)} %broadcast_in_dim.84), calls=%async_computation.4 | async-start | bytes 262144 | tf_op jit(solution)/shard_map/all_to_all | solution.py:31
  158.2 3.9 %gather_fusion = bf16[1024,256]{1,0:T(8,128)(2,1)S(1)} fusion(bf16[1024,256]{1,0:T(8,128)(2,1)S(1)} %collective-permute-done, s32[1024]{0:T(1024)S(1)} %fusion.13), kind=kCustom, calls=%fused_computation | custom fusion | bytes 1052672 | tf_op jit(solution)/shard_map/gather | solution.py:219
  174.9 8.1 %all_to_all.62.line_ref = f32[8,1,1024]{2,1,0:T(1,128)S(1)} all-to-all(f32[8,1,1024]{2,1,0:T(1,128)S(1)} %broadcast_in_dim.86), channel_id=1, replica_groups=mesh['z'=16,'y'=4,'x'=4,'core'=2] {'x','core'}, dimensions={0} | all-to-all | bytes 65536 | tf_op jit(solution)/shard_map/all_to_all | solution.py:31
  186.4 4.7 %gradient.1 = (f32[1024,256]{1,0:T(8,128)}, f32[2048,256]{1,0:T(8,128)S(1)}) custom-call(f32[1024,2048]{1,0:T(8,128)S(1)} %copy-done.4, f32[1024,2048]{1,0:T(8,128)S(1)} %copy-done.7, f32[16,1,2048]{2,1,0:T(1,128)S(1)} %all-to-all-done.4.totals_ref, f32[8,1,1024]{2,1,0:T(1,128)S(1)} %all_to_all.62.line_ref, ...), custom_call_target="tpu_custom_call" | custom-call | flops 2147483648 | bytes 16777216 | tf_op jit(solution)/shard_map/gradient/pallas_call | solution.py:154
  191.1 29.0 %all_to_all.63 = f32[4,512,256]{2,1,0:T(8,128)S(1)} all-to-all(f32[4,512,256]{2,1,0:T(8,128)S(1)} %bitcast.12), channel_id=1, replica_groups=mesh['z'=16,'y'=4,'x'=4,'core'=2] {'y'}, dimensions={0} | all-to-all | bytes 4194304 | tf_op jit(solution)/shard_map/all_to_all | solution.py:31
  220.1 4.2 %all-to-all-start.6 = ((f32[8,128,256]{2,1,0:T(8,128)}), f32[8,128,256]{2,1,0:T(8,128)}, u32[]{:S(2)}, u32[]{:S(2)}) async-start(f32[8,128,256]{2,1,0:T(8,128)} %bitcast.6), calls=%async_computation.6 | async-start | bytes 2097152 | tf_op jit(solution)/shard_map/all_to_all | solution.py:31
  225.3 15.0 %all-to-all-done.6 = f32[8,128,256]{2,1,0:T(8,128)} async-done(((f32[8,128,256]{2,1,0:T(8,128)}), f32[8,128,256]{2,1,0:T(8,128)}, u32[]{:S(2)}, u32[]{:S(2)}) %all-to-all-start.6) | async-done | bytes 1048608 | tf_op jit(solution)/shard_map/all_to_all | solution.py:31
  240.3 8.9 %all-to-all-start.9 = ((f32[16,32,256]{2,1,0:T(8,128)}), f32[16,32,256]{2,1,0:T(8,128)S(1)}, u32[]{:S(2)}, u32[]{:S(2)}) async-start(f32[16,32,256]{2,1,0:T(8,128)} %bitcast.9), calls=%async_computation.9 | async-start | bytes 1048576 | tf_op jit(solution)/shard_map/all_to_all | solution.py:31
  250.9 26.1 %all-to-all-done.9 = f32[16,32,256]{2,1,0:T(8,128)S(1)} async-done(((f32[16,32,256]{2,1,0:T(8,128)}), f32[16,32,256]{2,1,0:T(8,128)S(1)}, u32[]{:S(2)}, u32[]{:S(2)}) %all-to-all-start.9) | async-done | bytes 524320 | tf_op jit(solution)/shard_map/all_to_all | solution.py:31
  278.1 3.6 all-to-all-start.7
  284.2 13.3 %all-to-all-done.7 = f32[8,128,256]{2,1,0:T(8,128)S(1)} async-done(((f32[8,128,256]{2,1,0:T(8,128)}), f32[8,128,256]{2,1,0:T(8,128)S(1)}, u32[]{:S(2)}, u32[]{:S(2)}) %all-to-all-start.7) | async-done | bytes 1048608 | tf_op jit(solution)/shard_map/all_to_all | solution.py:31
  297.6 35.0 %all_to_all.64 = f32[16,32,256]{2,1,0:T(8,128)S(1)} all-to-all(f32[16,32,256]{2,1,0:T(8,128)S(1)} %broadcast_in_dim.88), channel_id=1, replica_groups=mesh['z'=16,'y'=4,'x'=4,'core'=2] {'z'}, dimensions={0} | all-to-all | bytes 1048576 | tf_op jit(solution)/shard_map/all_to_all | solution.py:31
  334.0 3.6 all-to-all-start.11
  337.7 22.5 %all-to-all-done.11 = f32[4,512,256]{2,1,0:T(8,128)S(1)} async-done(((f32[4,512,256]{2,1,0:T(8,128)}), f32[4,512,256]{2,1,0:T(8,128)S(1)}, u32[]{:S(2)}, u32[]{:S(2)}) %all-to-all-start.11) | async-done | bytes 2097184 | tf_op jit(solution)/shard_map/all_to_all | solution.py:31
  (57 shorter events, 51.0 us)
Async XLA Ops:
  0.6 1.0 copy-start.8
  1.7 1.2 copy-start.10
  2.9 33.5 %copy-start.9 = (bf16[1024,256]{1,0:T(8,128)(2,1)S(1)}, bf16[1024,256]{1,0:T(8,128)(2,1)}, u32[]{:S(2)}) copy-start(bf16[1024,256]{1,0:T(8,128)(2,1)} %emb_ref.1) | copy-start | bytes 1572868
  6.4 3.2 copy-start
  21.1 29.0 %all-to-all-start = ((f32[16,1,2048]{2,1,0:T(1,128)}), f32[16,1,2048]{2,1,0:T(1,128)S(1)}, u32[]{:S(2)}, u32[]{:S(2)}) async-start(f32[16,1,2048]{2,1,0:T(1,128)} %broadcast_in_dim.35), calls=%async_computation | async-start | bytes 262144 | tf_op jit(solution)/shard_map/all_to_all | solution.py:31
  36.4 58.2 %collective-permute-start = (bf16[1024,256]{1,0:T(8,128)(2,1)S(1)}, bf16[1024,256]{1,0:T(8,128)(2,1)S(1)}, u32[]{:S(2)}, u32[]{:S(2)}) collective-permute-start(bf16[1024,256]{1,0:T(8,128)(2,1)S(1)} %copy-done.9), channel_id=1, source_target_pairs={{0,256},{32,288},{64,320},{96,352},{128,384},{160,416},{192,448},{... | collective-permute-start | bytes 1572872 | tf_op jit(solution)/shard_map/ppermute | solution.py:27
  50.2 3.4 copy-start.1
  55.4 39.2 %all-to-all-start.1 = ((f32[8,1,2048]{2,1,0:T(1,128)}), f32[8,1,2048]{2,1,0:T(1,128)S(1)}, u32[]{:S(2)}, u32[]{:S(2)}) async-start(f32[8,1,2048]{2,1,0:T(1,128)} %broadcast_in_dim.37), calls=%async_computation.1 | async-start | bytes 131072 | tf_op jit(solution)/shard_map/all_to_all | solution.py:31
  94.6 3.4 copy-start.2
  128.2 3.4 copy-start.3
  142.0 16.2 %copy-start.11 = (s32[1024]{0:T(1024)S(1)}, s32[1024]{0:T(1024)}, u32[]{:S(2)}) copy-start(s32[1024]{0:T(1024)} %param.5) | copy-start | bytes 12292
  153.6 17.0 %all-to-all-start.4 = ((f32[16,1,2048]{2,1,0:T(1,128)}), f32[16,1,2048]{2,1,0:T(1,128)S(1)}, u32[]{:S(2)}, u32[]{:S(2)}) async-start(f32[16,1,2048]{2,1,0:T(1,128)} %broadcast_in_dim.84), calls=%async_computation.4 | async-start | bytes 262144 | tf_op jit(solution)/shard_map/all_to_all | solution.py:31
  164.2 3.2 copy-start.5
  170.6 3.4 copy-start.6
  174.0 9.0 %copy-start.7 = (f32[1024,2048]{1,0:T(8,128)S(1)}, f32[1024,2048]{1,0:T(8,128)}, u32[]{:S(2)}) copy-start(f32[1024,2048]{1,0:T(8,128)} %copy-done.5) | copy-start | bytes 25165828
  183.0 3.4 copy-start.4
  220.1 20.2 %all-to-all-start.6 = ((f32[8,128,256]{2,1,0:T(8,128)}), f32[8,128,256]{2,1,0:T(8,128)}, u32[]{:S(2)}, u32[]{:S(2)}) async-start(f32[8,128,256]{2,1,0:T(8,128)} %bitcast.6), calls=%async_computation.6 | async-start | bytes 2097152 | tf_op jit(solution)/shard_map/all_to_all | solution.py:31
  240.3 36.7 %all-to-all-start.9 = ((f32[16,32,256]{2,1,0:T(8,128)}), f32[16,32,256]{2,1,0:T(8,128)S(1)}, u32[]{:S(2)}, u32[]{:S(2)}) async-start(f32[16,32,256]{2,1,0:T(8,128)} %bitcast.9), calls=%async_computation.9 | async-start | bytes 1048576 | tf_op jit(solution)/shard_map/all_to_all | solution.py:31
  278.1 19.5 %all-to-all-start.7 = ((f32[8,128,256]{2,1,0:T(8,128)}), f32[8,128,256]{2,1,0:T(8,128)S(1)}, u32[]{:S(2)}, u32[]{:S(2)}) async-start(f32[8,128,256]{2,1,0:T(8,128)} %broadcast_in_dim.87), calls=%async_computation.7 | async-start | bytes 2097152 | tf_op jit(solution)/shard_map/all_to_all | solution.py:31
  334.0 26.1 %all-to-all-start.11 = ((f32[4,512,256]{2,1,0:T(8,128)}), f32[4,512,256]{2,1,0:T(8,128)S(1)}, u32[]{:S(2)}, u32[]{:S(2)}) async-start(f32[4,512,256]{2,1,0:T(8,128)} %broadcast_in_dim.90), calls=%async_computation.11 | async-start | bytes 4194304 | tf_op jit(solution)/shard_map/all_to_all | solution.py:31

commit v3 on v2

v3 whole, which is shorter than its diff:
```python
import functools

import jax
import jax.numpy as jnp
from jax import lax
from jax.experimental import pallas as pl
from jax.experimental.pallas import tpu as pltpu
from jax.sharding import Mesh, PartitionSpec as P

ITERS = 3


epsilon_code = 0.05
sharpness_divisor = 0.1
norm_floor = 1e-06
rows_axes = ("z", "y")
proto_axes = ("x", "core")
LANES = 128
ROWS = 128
f32 = jnp.float32
bf16 = jnp.bfloat16
SENT = jnp.float16
FOLD = 8


def shifted(value, axis, steps):
    count = lax.axis_size(axis)
    pairs = [(source, (source + steps) % count) for source in range(count)]
    return lax.ppermute(value, axis, pairs)


def exchanged(value, axis):
    return lax.all_to_all(value, axis, 0, 0, tiled=True)


def gathered(value, axis):
    return exchanged(jnp.broadcast_to(value[None], (lax.axis_size(axis),) + value.shape), axis)


def unit_rows(values):
    wide = values.astype(f32)
    scale = lax.rsqrt(jnp.mean(wide * wide, axis=1, keepdims=True) + norm_floor) / jnp.sqrt(
        f32(wide.shape[1])
    )
    return (wide * scale, scale)


def row_scale(values):
    return unit_rows(values)[1]


def tangent(upstream, units):
    return upstream - units * jnp.sum(units * upstream, axis=1, keepdims=True)


def total(pieces):
    return jnp.sum(pieces.astype(f32), axis=0)


def block(value, index, count):
    size = value.shape[0] // count
    return lax.dynamic_slice_in_dim(value, index * size, size, 0)


def scatter_sum(value, axis):
    count = lax.axis_size(axis)
    me = lax.axis_index(axis)
    total = block(value, me, count).astype(f32)
    for step in range(1, count):
        piece = shifted(block(value, (me + step) % count, count), axis, step)
        total = total + piece.astype(f32)
    return total.astype(value.dtype)


def gather_blocks(value, axis):
    count = lax.axis_size(axis)
    me = lax.axis_index(axis)
    pieces = [value] + [shifted(value, axis, step) for step in range(1, count)]
    out = jnp.zeros((count,) + value.shape, value.dtype)
    for step, piece in enumerate(pieces):
        out = lax.dynamic_update_slice_in_dim(out, piece[None], (me + count - step) % count, 0)
    return out.reshape((-1,) + value.shape[1:])


def kernel_units(values):
    wide = values.astype(f32)
    mean = jnp.sum(wide * wide, axis=1, keepdims=True) * (1.0 / wide.shape[1])
    scale = lax.rsqrt(mean + norm_floor) * (1.0 / wide.shape[1] ** 0.5)
    return (wide * scale).astype(bf16)


def lane_sums(values):
    total = values[:, :LANES]
    for start in range(LANES, values.shape[1], LANES):
        total = total + values[:, start : start + LANES]
    return total


def as_row(partials):
    return jnp.sum(partials.T, axis=0, keepdims=True)


def as_column(row):
    return jnp.broadcast_to(row, (LANES, row.shape[1])).T


def column_tile(values, start):
    width = values.shape[1]
    return values[start // width : start // width + 1, start % width : start % width + LANES]


def add_column(ref, start, values):
    width = ref.shape[1]
    at = (slice(start // width, start // width + 1), slice(start % width, start % width + LANES))
    ref[at] += jnp.sum(values, axis=0, keepdims=True)


def tempered_kernel(emb_ref, proto_ref, temp_ref, views_ref, protos_ref, col_ref, soft_ref):
    @pl.when(pl.program_id(0) == 0)
    def _():
        protos_ref[...] = kernel_units(proto_ref[...])
        col_ref[...] = jnp.zeros_like(col_ref)

    views = kernel_units(emb_ref[...])
    views_ref[...] = views
    scores = lax.dot_general(
        views, protos_ref[...], (((1,), (1,)), ((), ())), preferred_element_type=f32
    )
    tempered = jnp.exp(scores * (1.0 / sharpness_divisor))
    temp_ref[...] = tempered
    for start in range(0, tempered.shape[1], LANES):
        value = tempered[:, start : start + LANES]
        add_column(col_ref, start, value * value)
    soft_ref[...] = as_row(lane_sums(tempered))


def codes_kernel(emb_ref, protos_ref, kernel_ref):
    scores = lax.dot_general(
        kernel_units(emb_ref[...]),
        protos_ref[...],
        (((1,), (1,)), ((), ())),
        preferred_element_type=f32,
    )
    kernel_ref[...] = jnp.exp(scores * (1.0 / epsilon_code))


def row_kernel(squared, temp_ref, totals_ref, *refs):
    row_ref = refs[-1]
    column_scale = 1.0 / jnp.sum(totals_ref[...], axis=0)
    total = jnp.zeros((temp_ref.shape[0], LANES), f32)
    for start in range(0, temp_ref.shape[1], LANES):
        value = temp_ref[:, start : start + LANES]
        value = value * value if squared else value
        total = total + value * column_tile(column_scale, start)
    rows = as_row(total)
    for to in range(row_ref.shape[0]):
        row_ref[to, :1, :] = rows
        if len(refs) > 1:
            row_ref[to, 1:, :] = refs[0][...]


def col_kernel(temp_ref, totals_ref, col_ref):
    @pl.when(pl.program_id(0) == 0)
    def _():
        col_ref[...] = jnp.zeros_like(col_ref)

    wide = as_column(1.0 / jnp.sum(totals_ref[:, 0, :], axis=0, keepdims=True))
    for start in range(0, temp_ref.shape[1], LANES):
        value = temp_ref[:, start : start + LANES]
        add_column(col_ref, start, value * value * wide)


def gradient_kernel(
    temp_ref, other_ref, totals_ref, line_ref, soft_ref, views_ref, protos_ref, view_ref, proto_ref, sum_ref
):
    step = pl.program_id(0)

    @pl.when(step == 0)
    def _():
        sum_ref[...] = jnp.zeros_like(sum_ref)

    column_scale = 1.0 / jnp.sum(totals_ref[...], axis=0)
    line = as_column(1.0 / jnp.sum(line_ref[:, 0, :], axis=0, keepdims=True))
    soft = as_column(1.0 / jnp.sum(soft_ref[:, 1, :], axis=0, keepdims=True))
    grads = []
    for start in range(0, temp_ref.shape[1], LANES):
        tile = slice(start, start + LANES)
        codes = (other_ref[:, tile] * column_tile(column_scale, start) * line).astype(bf16)
        likelihood = temp_ref[:, tile] * soft
        grads.append(
            ((likelihood - codes.astype(f32)) * (1.0 / sharpness_divisor)).astype(bf16)
        )
    grad = jnp.concatenate(grads, axis=1)
    view = jnp.dot(grad, protos_ref[...], preferred_element_type=f32)
    view_ref[...] = view.astype(view_ref.dtype)
    sum_ref[...] += lax.dot_general(
        grad, views_ref[...], (((0,), (0,)), ((), ())), preferred_element_type=f32
    )

    @pl.when(step == pl.num_programs(0) - 1)
    def _():
        proto_ref[...] = sum_ref[...].astype(proto_ref.dtype)


def whole(shape):
    return pl.BlockSpec(shape, lambda i: (0,) * len(shape))


def strip(shape, rows):
    return pl.BlockSpec((rows, shape[1]), lambda i: (i, 0))


def span(shape, rows):
    last = len(shape) - 1
    return pl.BlockSpec(shape[:-1] + (rows,), lambda i: (0,) * last + (i,))


def in_hbm(value):
    return pltpu.with_memory_space_constraint(value, pltpu.HBM)


def call(kernel, name, ins, outs, flops, size, exps=0, rows=ROWS, scratch=()):
    return pl.pallas_call(
        kernel,
        name=name,
        grid=(ins[0][0].shape[0] // rows,),
        out_shape=[jax.ShapeDtypeStruct(shape, kind) for shape, kind, _ in outs],
        in_specs=[spec for _, spec in ins],
        out_specs=[spec for _, _, spec in outs],
        scratch_shapes=scratch,
        compiler_params=pltpu.CompilerParams(vmem_limit_bytes=16 * 2**20),
        cost_estimate=pl.CostEstimate(flops=flops, bytes_accessed=size, transcendentals=exps),
    )(*[value for value, _ in ins])


def body(embeddings, prototypes, partner):
    count, width = embeddings.shape
    slots = prototypes.shape[0]
    entries = count * slots
    links = jnp.remainder(partner, count)
    y, z, x, core = (lax.axis_index(name) for name in ("y", "z", "x", "core"))
    y_count, z_count, x_count = (lax.axis_size(name) for name in ("y", "z", "x"))
    own = block(embeddings, x * 2 + core, 2 * x_count)
    sent = gathered(shifted(own, "z", z_count // 2), proto_axes).reshape(count, width)

    matrix, row, column = (count, slots), (1, count), (FOLD, slots // FOLD)
    members = 2 * x_count
    tempered, views, protos, column_part, soft_part = call(
        tempered_kernel,
        "tempered",
        [(embeddings, strip(embeddings.shape, ROWS)), (prototypes, whole(prototypes.shape))],
        [
            (matrix, f32, strip(matrix, ROWS)),
            ((count, width), bf16, strip((count, width), ROWS)),
            ((slots, width), bf16, whole((slots, width))),
            (column, f32, whole(column)),
            (row, f32, span(row, ROWS)),
        ],
        flops=2 * entries * width,
        size=4 * entries,
        exps=entries,
    )
    tempered = in_hbm(tempered)

    def column_totals(part):
        return gathered(lax.psum(part, "y"), "z")

    def row_totals(squared, values, totals, *soft):
        sums = (members, 1 + len(soft), count)
        (part,) = call(
            functools.partial(row_kernel, squared),
            "row_pass",
            [(values, strip(matrix, ROWS)), (totals, whole(totals.shape))]
            + [(value, span(row, ROWS)) for value in soft],
            [(sums, f32, span(sums, ROWS))],
            flops=3 * entries,
            size=4 * entries,
        )
        return exchanged(part, proto_axes)

    def column_pass(values, totals):
        return call(
            col_kernel,
            "column_pass",
            [(values, strip(matrix, ROWS)), (totals, span(totals.shape, ROWS))],
            [(column, f32, whole(column))],
            flops=3 * entries,
            size=4 * entries,
        )[0]

    column_total = column_totals(column_part)
    first = row_totals(True, tempered, column_total, soft_part)
    first, sent = lax.optimization_barrier((first, sent))
    other = sent[links]
    column_total = column_totals(column_pass(tempered, first))
    for sweep in range(ITERS - 2):
        row_total = row_totals(True, tempered, column_total)
        column_total = column_totals(column_pass(tempered, row_total))
    (other_kernel,) = call(
        codes_kernel,
        "partner_codes",
        [(other, strip(other.shape, ROWS)), (protos, whole(protos.shape))],
        [(matrix, f32, strip(matrix, ROWS))],
        flops=2 * entries * width,
        size=4 * entries,
        exps=entries,
    )
    other_kernel = in_hbm(other_kernel)
    line_total = row_totals(False, other_kernel, column_total)
    view_part, proto_part = call(
        gradient_kernel,
        "gradient",
        [
            (tempered, strip(matrix, ROWS)),
            (other_kernel, strip(matrix, ROWS)),
            (column_total, whole(column_total.shape)),
            (line_total, span(line_total.shape, ROWS)),
            (first, span(first.shape, ROWS)),
            (views, strip(views.shape, ROWS)),
            (protos, whole(protos.shape)),
        ],
        [
            ((count, width), f32, strip((count, width), ROWS)),
            ((slots, width), f32, whole((slots, width))),
        ],
        flops=4 * entries * width,
        size=8 * entries,
        scratch=[pltpu.VMEM((slots, width), f32)],
    )

    proto_rows = unit_rows(block(prototypes, y * z_count + z, y_count * z_count))[0]
    view_rows = unit_rows(block(embeddings, core * x_count + x, members))[0]
    proto_pieces = exchanged(proto_part.astype(SENT).reshape(y_count, -1, width), "y")
    proto_sum = total(proto_pieces).astype(SENT)
    proto_pieces = exchanged(proto_sum.reshape(z_count, -1, width), "z")
    proto_sum = (tangent(total(proto_pieces), proto_rows) * (1.0 / z_count)).astype(SENT)
    proto_sum = gathered(proto_sum, "z").reshape(-1, width)

    view_sum = scatter_sum(scatter_sum(view_part.astype(SENT), "core"), "x")
    view_sum = tangent(view_sum.astype(f32), view_rows).astype(SENT)
    view_sum = gather_blocks(gather_blocks(view_sum, "x"), "core")

    proto_sum = gathered(proto_sum, "y").reshape(slots, width)
    emb_grad = row_scale(embeddings) * view_sum.astype(f32)
    proto_grad = row_scale(prototypes) * float(z_count) * proto_sum.astype(f32)
    return (emb_grad, proto_grad)


def solution(mesh):
    inner = Mesh(mesh.devices.reshape(16, 4, 4, 2), ("z", "y", "x", "core"))
    return jax.shard_map(
        body,
        mesh=inner,
        in_specs=(P(rows_axes, None), P(proto_axes, None), P(rows_axes)),
        out_specs=(P(rows_axes, None), P(proto_axes, None)),
        check_vma=False,
    )
```

time: 364 us -> 291 us (0.80)
  the two profiles are of different devices: /device:TPU:32 before, /device:TPU:1 now
where the time goes in v3:
time: 291 us; the launch traced here: 289 us
  starting transfers between devices  96.5 us (33%)
  blocking collectives  76.8 us (26%)
  Pallas kernels  51.5 us (18%)
  waiting for transfers between devices  37.5 us (13%)
  local copies, waits for them, and re-layouts  17.7 us (6%)
  other arithmetic  7.76 us (3%)
    all_to_all x7, starting transfers between devices, exchanged(): return lax.all_to_all(value, axis, 0, 0, tiled=True)  56.2 us
    all_to_all x4, blocking collectives, exchanged(): return lax.all_to_all(value, axis, 0, 0, tiled=True)  53.2 us
    pallas_call x8, Pallas kernels, call(): pl.pallas_call(kernel, name=name, grid=(ins[0][0].shape[0] // rows,), out...  51.5 us
    ppermute x9, starting transfers between devices, shifted(): return lax.ppermute(value, axis, pairs)  40.3 us
    all_to_all x7, waiting for transfers between devices, exchanged(): return lax.all_to_all(value, axis, 0, 0, tiled=True)  29.4 us
    psum x3, blocking collectives, column_totals(): return gathered(lax.psum(part, 'y'), 'z')  23.6 us
    unnamed x18, local copies, waits for them, and re-layouts  9.49 us
    ppermute x9, waiting for transfers between devices, shifted(): return lax.ppermute(value, axis, pairs)  8.1 us
  transfers between devices with their start and end apart: 16, of which 10 were waited for; matrix products, arithmetic and copies ran while one was open for 3% of the time, Pallas kernels for 4%

profile of v3, /device:TPU:1, one launch (start us, length us, event | category | flops | bytes accessed | tf_op | source)
XLA Modules:
  0.0 288.9 jit_solution(15990853198921982514)
XLA Ops:
  2.9 5.3 %tempered.1 = (f32[1024,2048]{1,0:T(8,128)S(1)}, bf16[1024,256]{1,0:T(8,128)(2,1)S(1)}, bf16[2048,256]{1,0:T(8,128)(2,1)S(1)}, f32[8,256]{1,0:T(8,128)S(1)}, f32[1,1024]{1,0:T(1,128)S(1)}) custom-call(bf16[1024,256]{1,0:T(8,128)(2,1)S(1)} %copy-done.2, bf16[2048,256]{1,0:T(8,128)(2,1)S(1)} %copy-done.4), custom_call_target="tpu_custom_call" | custom-call | flops 1073741824 | bytes 8388608 | tf_op jit(solution)/shard_map/tempered/pallas_call | solution.py:223
  12.2 9.6 %psum.21 = f32[8,256]{1,0:T(8,128)S(1)} all-reduce(f32[8,256]{1,0:T(8,128)S(1)} %get-tuple-element.12), channel_id=1, replica_groups=mesh['z'=16,'y'=4,'x'=4,'core'=2] {'y'}, use_global_device_ids=true, to_apply=%region_1.2 | all-reduce | flops 2048 | bytes 16384 | tf_op jit(solution)/shard_map/psum | solution.py:266
  22.5 14.9 %all-to-all-start = ((f32[16,8,256]{2,1,0:T(8,128)}), f32[16,8,256]{2,1,0:T(8,128)S(1)}, u32[]{:S(2)}, u32[]{:S(2)}) async-start(f32[16,8,256]{2,1,0:T(8,128)} %broadcast_in_dim.32), calls=%async_computation | async-start | bytes 262144 | tf_op jit(solution)/shard_map/all_to_all | solution.py:33
  37.5 12.0 %collective-permute-start = (bf16[128,256]{1,0:T(8,128)(2,1)S(1)}, bf16[128,256]{1,0:T(8,128)(2,1)S(1)}, u32[]{:S(2)}, u32[]{:S(2)}) collective-permute-start(bf16[128,256]{1,0:T(8,128)(2,1)S(1)} %constant_dynamic-slice_fusion.4), channel_id=1, source_target_pairs={{0,256},{32,288},{64,320},{96,352},{128,384},{160,416},{192,448},{... | collective-permute-start | bytes 196616 | tf_op jit(solution)/shard_map/ppermute | solution.py:29
  53.1 9.8 %all-to-all-start.2 = ((bf16[8,128,256]{2,1,0:T(8,128)(2,1)}), bf16[8,128,256]{2,1,0:T(8,128)(2,1)S(1)}, u32[]{:S(2)}, u32[]{:S(2)}) async-start(bf16[8,128,256]{2,1,0:T(8,128)(2,1)} %broadcast_in_dim.33), calls=%async_computation.2 | async-start | bytes 1048576 | tf_op jit(solution)/shard_map/all_to_all | solution.py:33
  62.9 6.3 %row_pass.3 = f32[8,2,1024]{2,1,0:T(2,128)S(1)} custom-call(f32[1024,2048]{1,0:T(8,128)} %copy-done, f32[16,8,256]{2,1,0:T(8,128)S(1)} %all-to-all-done.totals_ref, f32[1,1024]{1,0:T(1,128)S(1)} %get-tuple-element.13.refs_0_), custom_call_target="tpu_custom_call" | custom-call | flops 6291456 | bytes 8388608 | tf_op jit(solution)/shard_map/row_pass/pallas_call | solution.py:223
  72.4 8.1 %all_to_all.55.totals_ref.soft_ref = f32[8,2,1024]{2,1,0:T(2,128)S(1)} all-to-all(f32[8,2,1024]{2,1,0:T(2,128)S(1)} %row_pass.3), channel_id=1, replica_groups=mesh['z'=16,'y'=4,'x'=4,'core'=2] {'x','core'}, dimensions={0} | all-to-all | bytes 131072 | tf_op jit(solution)/shard_map/all_to_all | solution.py:33
  80.5 6.2 %column_pass.2 = f32[8,256]{1,0:T(8,128)S(1)} custom-call(f32[1024,2048]{1,0:T(8,128)} %copy-done, f32[8,2,1024]{2,1,0:T(2,128)S(1)} %all_to_all.55.totals_ref.soft_ref), custom_call_target="tpu_custom_call" | custom-call | flops 6291456 | bytes 8388608 | tf_op jit(solution)/shard_map/column_pass/pallas_call | solution.py:223
  86.7 6.1 %psum.22 = f32[8,256]{1,0:T(8,128)S(1)} all-reduce(f32[8,256]{1,0:T(8,128)S(1)} %column_pass.2), channel_id=1, replica_groups=mesh['z'=16,'y'=4,'x'=4,'core'=2] {'y'}, use_global_device_ids=true, to_apply=%region_2.3 | all-reduce | flops 2048 | bytes 16384 | tf_op jit(solution)/shard_map/psum | solution.py:266
  92.8 22.6 %all_to_all.56.totals_ref = f32[16,8,256]{2,1,0:T(8,128)S(1)} all-to-all(f32[16,8,256]{2,1,0:T(8,128)S(1)} %broadcast_in_dim.35), channel_id=1, replica_groups=mesh['z'=16,'y'=4,'x'=4,'core'=2] {'z'}, dimensions={0} | all-to-all | bytes 262144 | tf_op jit(solution)/shard_map/all_to_all | solution.py:33
  115.4 6.3 %row_pass.4 = f32[8,1,1024]{2,1,0:T(1,128)S(1)} custom-call(f32[1024,2048]{1,0:T(8,128)} %copy-done, f32[16,8,256]{2,1,0:T(8,128)S(1)} %all_to_all.56.totals_ref), custom_call_target="tpu_custom_call" | custom-call | flops 6291456 | bytes 8388608 | tf_op jit(solution)/shard_map/row_pass/pallas_call | solution.py:223
  121.7 11.1 %all_to_all.57.totals_ref = f32[8,1,1024]{2,1,0:T(1,128)S(1)} all-to-all(f32[8,1,1024]{2,1,0:T(1,128)S(1)} %row_pass.4), channel_id=1, replica_groups=mesh['z'=16,'y'=4,'x'=4,'core'=2] {'x','core'}, dimensions={0} | all-to-all | bytes 65536 | tf_op jit(solution)/shard_map/all_to_all | solution.py:33
  132.8 6.2 %column_pass.3 = f32[8,256]{1,0:T(8,128)S(1)} custom-call(f32[1024,2048]{1,0:T(8,128)} %copy-done, f32[8,1,1024]{2,1,0:T(1,128)S(1)} %all_to_all.57.totals_ref), custom_call_target="tpu_custom_call" | custom-call | flops 6291456 | bytes 8388608 | tf_op jit(solution)/shard_map/column_pass/pallas_call | solution.py:223
  139.0 7.8 %psum.23 = f32[8,256]{1,0:T(8,128)S(1)} all-reduce(f32[8,256]{1,0:T(8,128)S(1)} %column_pass.3), channel_id=1, replica_groups=mesh['z'=16,'y'=4,'x'=4,'core'=2] {'y'}, use_global_device_ids=true, to_apply=%region_3.4 | all-reduce | flops 2048 | bytes 16384 | tf_op jit(solution)/shard_map/psum | solution.py:266
  155.1 4.2 %partner_codes.1.temp_ref.other_ref = f32[1024,2048]{1,0:T(8,128)S(1)} custom-call(bf16[1024,256]{1,0:T(8,128)(2,1)S(1)} %gather_fusion, bf16[2048,256]{1,0:T(8,128)(2,1)S(1)} %get-tuple-element.15.protos_ref), custom_call_target="tpu_custom_call" | custom-call | flops 1073741824 | bytes 8388608 | tf_op jit(solution)/shard_map/partner_codes/pallas_call | solution.py:223
  163.1 6.2 %row_pass.5 = f32[8,1,1024]{2,1,0:T(1,128)S(1)} custom-call(f32[1024,2048]{1,0:T(8,128)} %copy-done.1, f32[16,8,256]{2,1,0:T(8,128)S(1)} %all-to-all-done.5.totals_ref), custom_call_target="tpu_custom_call" | custom-call | flops 6291456 | bytes 8388608 | tf_op jit(solution)/shard_map/row_pass/pallas_call | solution.py:223
  169.3 11.4 %all_to_all.58.line_ref = f32[8,1,1024]{2,1,0:T(1,128)S(1)} all-to-all(f32[8,1,1024]{2,1,0:T(1,128)S(1)} %row_pass.5), channel_id=1, replica_groups=mesh['z'=16,'y'=4,'x'=4,'core'=2] {'x','core'}, dimensions={0} | all-to-all | bytes 65536 | tf_op jit(solution)/shard_map/all_to_all | solution.py:33
  180.7 10.9 %gradient.1 = (f32[1024,256]{1,0:T(8,128)S(1)}, f32[2048,256]{1,0:T(8,128)S(1)}) custom-call(f32[1024,2048]{1,0:T(8,128)} %copy-done, f32[1024,2048]{1,0:T(8,128)} %copy-done.1, f32[16,8,256]{2,1,0:T(8,128)S(1)} %all-to-all-done.5.totals_ref, f32[8,1,1024]{2,1,0:T(1,128)S(1)} %all_to_all.58.line_ref, f32[8,2,1024]{2,1,0:T(2,128)S(1)} %all_to_all.55.totals_ref.soft_ref, ...), custom_call_target="tpu_custom_call" | custom-call | flops 2147483648 | bytes 16777216 | tf_op jit(solution)/shard_map/gradient/pallas_call | solution.py:223
  192.7 4.2 %all-to-all-start.7 = ((f16[4,512,256]{2,1,0:T(8,128)(2,1)}), f16[4,512,256]{2,1,0:T(8,128)(2,1)}, u32[]{:S(2)}, u32[]{:S(2)}) async-start(f16[4,512,256]{2,1,0:T(8,128)(2,1)} %bitcast.25), calls=%async_computation.7 | async-start | bytes 2097152 | tf_op jit(solution)/shard_map/all_to_all | solution.py:33
  200.5 11.0 %all-to-all-done.7 = f16[4,512,256]{2,1,0:T(8,128)(2,1)} async-done(((f16[4,512,256]{2,1,0:T(8,128)(2,1)}), f16[4,512,256]{2,1,0:T(8,128)(2,1)}, u32[]{:S(2)}, u32[]{:S(2)}) %all-to-all-start.7) | async-done | bytes 1048608 | tf_op jit(solution)/shard_map/all_to_all | solution.py:33
  213.6 9.9 %all-to-all-start.8 = ((f16[16,32,256]{2,1,0:T(8,128)(2,1)}), f16[16,32,256]{2,1,0:T(8,128)(2,1)S(1)}, u32[]{:S(2)}, u32[]{:S(2)}) async-start(f16[16,32,256]{2,1,0:T(8,128)(2,1)} %bitcast.10), calls=%async_computation.8 | async-start | bytes 524288 | tf_op jit(solution)/shard_map/all_to_all | solution.py:33
  237.4 10.2 %all-to-all-start.9 = ((f16[16,32,256]{2,1,0:T(8,128)(2,1)}), f16[16,32,256]{2,1,0:T(8,128)(2,1)S(1)}, u32[]{:S(2)}, u32[]{:S(2)}) async-start(f16[16,32,256]{2,1,0:T(8,128)(2,1)} %broadcast_in_dim.79), calls=%async_computation.9 | async-start | bytes 524288 | tf_op jit(solution)/shard_map/all_to_all | solution.py:33
  260.4 7.2 %collective-permute-start.8 = (f16[512,256]{1,0:T(8,128)(2,1)S(1)}, f16[512,256]{1,0:T(8,128)(2,1)S(1)}, u32[]{:S(2)}, u32[]{:S(2)}) collective-permute-start(f16[512,256]{1,0:T(8,128)(2,1)S(1)} %bitcast.27), channel_id=1, source_target_pairs={{0,1},{1,0},{2,3},{3,2},{4,5},{5,4},{6,7},{7,6},{8,9},{9,8},{10,11... | collective-permute-start | bytes 786440 | tf_op jit(solution)/shard_map/ppermute | solution.py:29
  273.6 13.7 %all-to-all-done.10 = f16[4,512,256]{2,1,0:T(8,128)(2,1)S(1)} async-done(((f16[4,512,256]{2,1,0:T(8,128)(2,1)}), f16[4,512,256]{2,1,0:T(8,128)(2,1)S(1)}, u32[]{:S(2)}, u32[]{:S(2)}) %all-to-all-start.10) | async-done | bytes 1048608 | tf_op jit(solution)/shard_map/all_to_all | solution.py:33
  (79 shorter events, 66.5 us)
Async XLA Ops:
  0.6 1.0 copy-start.2
  1.7 1.2 copy-start.4
  2.9 34.5 %copy-start.3 = (bf16[1024,256]{1,0:T(8,128)(2,1)S(1)}, bf16[1024,256]{1,0:T(8,128)(2,1)}, u32[]{:S(2)}) copy-start(bf16[1024,256]{1,0:T(8,128)(2,1)} %emb_ref.1) | copy-start | bytes 1572868
  8.2 3.2 %copy-start = (f32[1024,2048]{1,0:T(8,128)}, f32[1024,2048]{1,0:T(8,128)S(1)}, u32[]{:S(2)}) copy-start(f32[1024,2048]{1,0:T(8,128)S(1)} %get-tuple-element.11.temp_ref) | copy-start | bytes 25165828
  22.5 29.8 %all-to-all-start = ((f32[16,8,256]{2,1,0:T(8,128)}), f32[16,8,256]{2,1,0:T(8,128)S(1)}, u32[]{:S(2)}, u32[]{:S(2)}) async-start(f32[16,8,256]{2,1,0:T(8,128)} %broadcast_in_dim.32), calls=%async_computation | async-start | bytes 262144 | tf_op jit(solution)/shard_map/all_to_all | solution.py:33
  37.5 14.8 %collective-permute-start = (bf16[128,256]{1,0:T(8,128)(2,1)S(1)}, bf16[128,256]{1,0:T(8,128)(2,1)S(1)}, u32[]{:S(2)}, u32[]{:S(2)}) collective-permute-start(bf16[128,256]{1,0:T(8,128)(2,1)S(1)} %constant_dynamic-slice_fusion.4), channel_id=1, source_target_pairs={{0,256},{32,288},{64,320},{96,352},{128,384},{160,416},{192,448},{... | collective-permute-start | bytes 196616 | tf_op jit(solution)/shard_map/ppermute | solution.py:29
  53.1 19.3 %all-to-all-start.2 = ((bf16[8,128,256]{2,1,0:T(8,128)(2,1)}), bf16[8,128,256]{2,1,0:T(8,128)(2,1)S(1)}, u32[]{:S(2)}, u32[]{:S(2)}) async-start(bf16[8,128,256]{2,1,0:T(8,128)(2,1)} %broadcast_in_dim.33), calls=%async_computation.2 | async-start | bytes 1048576 | tf_op jit(solution)/shard_map/all_to_all | solution.py:33
  132.8 18.3 %copy-start.8 = (s32[1024]{0:T(1024)S(1)}, s32[1024]{0:T(1024)}, u32[]{:S(2)}) copy-start(s32[1024]{0:T(1024)} %param.5) | copy-start | bytes 12292
  147.5 15.5 %all-to-all-start.5 = ((f32[16,8,256]{2,1,0:T(8,128)}), f32[16,8,256]{2,1,0:T(8,128)S(1)}, u32[]{:S(2)}, u32[]{:S(2)}) async-start(f32[16,8,256]{2,1,0:T(8,128)} %broadcast_in_dim.36), calls=%async_computation.5 | async-start | bytes 262144 | tf_op jit(solution)/shard_map/all_to_all | solution.py:33
  159.3 3.2 %copy-start.1 = (f32[1024,2048]{1,0:T(8,128)}, f32[1024,2048]{1,0:T(8,128)S(1)}, u32[]{:S(2)}) copy-start(f32[1024,2048]{1,0:T(8,128)S(1)} %partner_codes.1.temp_ref.other_ref) | copy-start | bytes 25165828
  162.5 18.2 %copy-start.7 = (bf16[1024,256]{1,0:T(8,128)(2,1)S(1)}, bf16[1024,256]{1,0:T(8,128)(2,1)}, u32[]{:S(2)}) copy-start(bf16[1024,256]{1,0:T(8,128)(2,1)} %copy-done.6) | copy-start | bytes 1572868
  191.5 5.5 %copy-start.5 = (bf16[2048,256]{1,0:T(8,128)(2,1)S(1)}, bf16[2048,256]{1,0:T(8,128)(2,1)}, u32[]{:S(2)}) copy-start(bf16[2048,256]{1,0:T(8,128)(2,1)} %proto_ref.1) | copy-start | bytes 3145732
  192.7 18.7 %all-to-all-start.7 = ((f16[4,512,256]{2,1,0:T(8,128)(2,1)}), f16[4,512,256]{2,1,0:T(8,128)(2,1)}, u32[]{:S(2)}, u32[]{:S(2)}) async-start(f16[4,512,256]{2,1,0:T(8,128)(2,1)} %bitcast.25), calls=%async_computation.7 | async-start | bytes 2097152 | tf_op jit(solution)/shard_map/all_to_all | solution.py:33
  197.8 25.8 %collective-permute-start.1 = (f16[512,256]{1,0:T(8,128)(2,1)S(1)}, f16[512,256]{1,0:T(8,128)(2,1)S(1)}, u32[]{:S(2)}, u32[]{:S(2)}) collective-permute-start(f16[512,256]{1,0:T(8,128)(2,1)S(1)} %constant_dynamic-slice_fusion.3), channel_id=1, source_target_pairs={{0,1},{1,0},{2,3},{3,2},{4,5},{5,4},{6,7},{7,6},{8,9},{9,8},{10,11... | collective-permute-start | bytes 786440 | tf_op jit(solution)/shard_map/ppermute | solution.py:29
  213.6 22.7 %all-to-all-start.8 = ((f16[16,32,256]{2,1,0:T(8,128)(2,1)}), f16[16,32,256]{2,1,0:T(8,128)(2,1)S(1)}, u32[]{:S(2)}, u32[]{:S(2)}) async-start(f16[16,32,256]{2,1,0:T(8,128)(2,1)} %bitcast.10), calls=%async_computation.8 | async-start | bytes 524288 | tf_op jit(solution)/shard_map/all_to_all | solution.py:33
  223.7 8.7 %collective-permute-start.2 = (f16[128,256]{1,0:T(8,128)(2,1)S(1)}, f16[128,256]{1,0:T(8,128)(2,1)S(1)}, u32[]{:S(2)}, u32[]{:S(2)}) collective-permute-start(f16[128,256]{1,0:T(8,128)(2,1)S(1)} %get-tuple-element.24), channel_id=1, source_target_pairs={{0,2},{2,4},{4,6},{6,0},{1,3},{3,5},{5,7},{7,1},{8,10},{10,12},{12... | collective-permute-start | bytes 196616 | tf_op jit(solution)/shard_map/ppermute | solution.py:29
  225.9 6.8 %collective-permute-start.3 = (f16[128,256]{1,0:T(8,128)(2,1)S(1)}, f16[128,256]{1,0:T(8,128)(2,1)S(1)}, u32[]{:S(2)}, u32[]{:S(2)}) collective-permute-start(f16[128,256]{1,0:T(8,128)(2,1)S(1)} %get-tuple-element.26), channel_id=1, source_target_pairs={{0,4},{2,6},{4,0},{6,2},{1,5},{3,7},{5,1},{7,3},{8,12},{10,14},{12... | collective-permute-start | bytes 196616 | tf_op jit(solution)/shard_map/ppermute | solution.py:29
  229.6 5.6 %collective-permute-start.4 = (f16[128,256]{1,0:T(8,128)(2,1)S(1)}, f16[128,256]{1,0:T(8,128)(2,1)S(1)}, u32[]{:S(2)}, u32[]{:S(2)}) collective-permute-start(f16[128,256]{1,0:T(8,128)(2,1)S(1)} %get-tuple-element.25), channel_id=1, source_target_pairs={{0,6},{2,0},{4,2},{6,4},{1,7},{3,1},{5,3},{7,5},{8,14},{10,8},{12,... | collective-permute-start | bytes 196616 | tf_op jit(solution)/shard_map/ppermute | solution.py:29
  237.4 30.2 %all-to-all-start.9 = ((f16[16,32,256]{2,1,0:T(8,128)(2,1)}), f16[16,32,256]{2,1,0:T(8,128)(2,1)S(1)}, u32[]{:S(2)}, u32[]{:S(2)}) async-start(f16[16,32,256]{2,1,0:T(8,128)(2,1)} %broadcast_in_dim.79), calls=%async_computation.9 | async-start | bytes 524288 | tf_op jit(solution)/shard_map/all_to_all | solution.py:33
  247.8 10.2 %collective-permute-start.5 = (f16[128,256]{1,0:T(8,128)(2,1)S(1)}, f16[128,256]{1,0:T(8,128)(2,1)S(1)}, u32[]{:S(2)}, u32[]{:S(2)}) collective-permute-start(f16[128,256]{1,0:T(8,128)(2,1)S(1)} %get-tuple-element.21), channel_id=1, source_target_pairs={{0,2},{2,4},{4,6},{6,0},{1,3},{3,5},{5,7},{7,1},{8,10},{10,12},{12... | collective-permute-start | bytes 196616 | tf_op jit(solution)/shard_map/ppermute | solution.py:29
  251.7 6.9 %collective-permute-start.6 = (f16[128,256]{1,0:T(8,128)(2,1)S(1)}, f16[128,256]{1,0:T(8,128)(2,1)S(1)}, u32[]{:S(2)}, u32[]{:S(2)}) collective-permute-start(f16[128,256]{1,0:T(8,128)(2,1)S(1)} %get-tuple-element.21), channel_id=1, source_target_pairs={{0,4},{2,6},{4,0},{6,2},{1,5},{3,7},{5,1},{7,3},{8,12},{10,14},{12... | collective-permute-start | bytes 196616 | tf_op jit(solution)/shard_map/ppermute | solution.py:29
  255.1 5.3 %collective-permute-start.7 = (f16[128,256]{1,0:T(8,128)(2,1)S(1)}, f16[128,256]{1,0:T(8,128)(2,1)S(1)}, u32[]{:S(2)}, u32[]{:S(2)}) collective-permute-start(f16[128,256]{1,0:T(8,128)(2,1)S(1)} %get-tuple-element.21), channel_id=1, source_target_pairs={{0,6},{2,0},{4,2},{6,4},{1,7},{3,1},{5,3},{7,5},{8,14},{10,8},{12,... | collective-permute-start | bytes 196616 | tf_op jit(solution)/shard_map/ppermute | solution.py:29
  260.4 11.9 %collective-permute-start.8 = (f16[512,256]{1,0:T(8,128)(2,1)S(1)}, f16[512,256]{1,0:T(8,128)(2,1)S(1)}, u32[]{:S(2)}, u32[]{:S(2)}) collective-permute-start(f16[512,256]{1,0:T(8,128)(2,1)S(1)} %bitcast.27), channel_id=1, source_target_pairs={{0,1},{1,0},{2,3},{3,2},{4,5},{5,4},{6,7},{7,6},{8,9},{9,8},{10,11... | collective-permute-start | bytes 786440 | tf_op jit(solution)/shard_map/ppermute | solution.py:29
  268.7 18.6 %all-to-all-start.10 = ((f16[4,512,256]{2,1,0:T(8,128)(2,1)}), f16[4,512,256]{2,1,0:T(8,128)(2,1)S(1)}, u32[]{:S(2)}, u32[]{:S(2)}) async-start(f16[4,512,256]{2,1,0:T(8,128)(2,1)} %broadcast_in_dim.81), calls=%async_computation.10 | async-start | bytes 2097152 | tf_op jit(solution)/shard_map/all_to_all | solution.py:33
  (1 other events, 0.8 us)

commit v4 on v1

v4 whole, which is shorter than its diff:
```python
import functools

import jax
import jax.numpy as jnp
from jax import lax
from jax.experimental import pallas as pl
from jax.experimental.pallas import tpu as pltpu
from jax.sharding import Mesh, PartitionSpec as P

ITERS = 3


epsilon_code = 0.05
sharpness_divisor = 0.1
norm_floor = 1e-06
rows_axes = ("z", "y")
proto_axes = ("x", "core")
LANES = 128
ROWS = 256
f32 = jnp.float32
bf16 = jnp.bfloat16
SENT = jnp.float16
FOLD = 8


def shifted(value, axis, steps):
    count = lax.axis_size(axis)
    pairs = [(source, (source + steps) % count) for source in range(count)]
    return lax.ppermute(value, axis, pairs)


def exchanged(value, axis):
    return lax.all_to_all(value, axis, 0, 0, tiled=True)


def gathered(value, axis):
    return exchanged(jnp.broadcast_to(value[None], (lax.axis_size(axis),) + value.shape), axis)


def unit_rows(values):
    wide = values.astype(f32)
    scale = lax.rsqrt(jnp.mean(wide * wide, axis=1, keepdims=True) + norm_floor) / jnp.sqrt(
        f32(wide.shape[1])
    )
    return (wide * scale, scale)


def row_scale(values):
    return unit_rows(values)[1]


def tangent(upstream, units):
    return upstream - units * jnp.sum(units * upstream, axis=1, keepdims=True)


def total(pieces):
    return jnp.sum(pieces.astype(f32), axis=0)


def block(value, index, count):
    size = value.shape[0] // count
    return lax.dynamic_slice_in_dim(value, index * size, size, 0)


def scatter_sum(value, axis):
    count = lax.axis_size(axis)
    me = lax.axis_index(axis)
    total = block(value, me, count).astype(f32)
    for step in range(1, count):
        piece = shifted(block(value, (me + step) % count, count), axis, step)
        total = total + piece.astype(f32)
    return total.astype(value.dtype)


def gather_blocks(value, axis):
    count = lax.axis_size(axis)
    me = lax.axis_index(axis)
    pieces = [value] + [shifted(value, axis, step) for step in range(1, count)]
    out = jnp.zeros((count,) + value.shape, value.dtype)
    for step, piece in enumerate(pieces):
        out = lax.dynamic_update_slice_in_dim(out, piece[None], (me + count - step) % count, 0)
    return out.reshape((-1,) + value.shape[1:])


def kernel_units(values):
    wide = values.astype(f32)
    mean = jnp.sum(wide * wide, axis=1, keepdims=True) * (1.0 / wide.shape[1])
    scale = lax.rsqrt(mean + norm_floor) * (1.0 / wide.shape[1] ** 0.5)
    return (wide * scale).astype(bf16)


def as_row(partials):
    return jnp.sum(partials.T, axis=0, keepdims=True)


def as_column(row):
    return jnp.broadcast_to(row, (LANES, row.shape[1])).T


def column_tile(values, start):
    width = values.shape[1]
    return values[start // width : start // width + 1, start % width : start % width + LANES]


def add_column(ref, start, values):
    width = ref.shape[2]
    tile = (0, slice(start // width, start // width + 1), slice(start % width, start % width + LANES))
    ref[tile] += jnp.sum(values, axis=0, keepdims=True)


def tiles(matrix):
    return range(0, matrix.shape[1], LANES)


def tempered_rows(units, protos_ref, divisor):
    scores = lax.dot_general(
        units, protos_ref[...], (((1,), (1,)), ((), ())), preferred_element_type=f32
    )
    return jnp.exp(scores * (1.0 / divisor))


def steps(count):
    return [slice(start, start + ROWS) for start in range(0, count, ROWS)]


def for_each_receiver(ref):
    for to in range(1, ref.shape[0]):
        ref[to] = ref[0]


def first_kernel(emb_ref, proto_ref, views_ref, protos_ref, col_ref):
    protos_ref[...] = kernel_units(proto_ref[...])
    views_ref[...] = kernel_units(emb_ref[...])
    col_ref[0] = jnp.zeros_like(col_ref[0])

    @pl.loop(0, emb_ref.shape[0] // ROWS)
    def _(step):
        rows = pl.ds(pl.multiple_of(step * ROWS, ROWS), ROWS)
        tempered = tempered_rows(views_ref[rows, :], protos_ref, sharpness_divisor)
        for start in tiles(tempered):
            value = tempered[:, start : start + LANES]
            add_column(col_ref, start, value * value)

    for_each_receiver(col_ref)


def rows_kernel(own, emb_ref, protos_ref, totals_ref, temp_ref, row_ref):
    column_scale = 1.0 / jnp.sum(totals_ref[...], axis=0)

    @pl.loop(0, emb_ref.shape[0] // ROWS)
    def _(step):
        rows = pl.ds(pl.multiple_of(step * ROWS, ROWS), ROWS)
        units = emb_ref[rows, :]
        if own:
            tempered = tempered_rows(units, protos_ref, sharpness_divisor)
        else:
            tempered = tempered_rows(kernel_units(units), protos_ref, epsilon_code)
        temp_ref[rows, :] = tempered
        total = soft = jnp.zeros((ROWS, LANES), f32)
        for start in tiles(tempered):
            value = tempered[:, start : start + LANES]
            if own:
                soft = soft + value
                value = value * value
            total = total + value * column_tile(column_scale, start)
        row_ref[0, :1, rows] = as_row(total)
        if own:
            row_ref[0, 1:, rows] = as_row(soft)

    for_each_receiver(row_ref)


def row_kernel(temp_ref, totals_ref, row_ref):
    column_scale = 1.0 / jnp.sum(totals_ref[...], axis=0)
    for rows in steps(temp_ref.shape[0]):
        total = jnp.zeros((ROWS, LANES), f32)
        for start in tiles(temp_ref):
            value = temp_ref[rows, start : start + LANES]
            total = total + value * value * column_tile(column_scale, start)
        row_ref[0, :, rows] = as_row(total)
    for_each_receiver(row_ref)


def col_kernel(temp_ref, totals_ref, col_ref):
    weight = 1.0 / jnp.sum(totals_ref[:, 0, :], axis=0, keepdims=True)
    col_ref[0] = jnp.zeros_like(col_ref[0])
    for rows in steps(temp_ref.shape[0]):
        wide = as_column(weight[:, rows])
        for start in tiles(temp_ref):
            value = temp_ref[rows, start : start + LANES]
            add_column(col_ref, start, value * value * wide)
    for_each_receiver(col_ref)


def gradient_kernel(
    other_ref, totals_ref, line_ref, soft_ref, views_ref, protos_ref, view_ref, proto_ref
):
    proto_ref[...] = jnp.zeros_like(proto_ref)
    column_scale = 1.0 / jnp.sum(totals_ref[...], axis=0)
    line_row = 1.0 / jnp.sum(line_ref[:, 0, :], axis=0, keepdims=True)
    soft_row = 1.0 / jnp.sum(soft_ref[:, 1, :], axis=0, keepdims=True)
    for rows in steps(other_ref.shape[0]):
        line = as_column(line_row[:, rows])
        soft = as_column(soft_row[:, rows])
        views = views_ref[rows, :]
        tempered = tempered_rows(views, protos_ref, sharpness_divisor)
        grads = []
        for start in tiles(tempered):
            codes = other_ref[rows, start : start + LANES]
            codes = (codes * column_tile(column_scale, start) * line).astype(bf16)
            likelihood = tempered[:, start : start + LANES] * soft
            grads.append(
                ((likelihood - codes.astype(f32)) * (1.0 / sharpness_divisor)).astype(bf16)
            )
        grad = jnp.concatenate(grads, axis=1)
        view_ref[rows, :] = jnp.dot(grad, protos_ref[...], preferred_element_type=f32)
        proto_ref[...] += lax.dot_general(
            grad, views, (((0,), (0,)), ((), ())), preferred_element_type=f32
        )


def call(kernel, name, ins, outs, flops, size, exps=0):
    in_vmem = pl.BlockSpec(memory_space=pltpu.VMEM)
    return pl.pallas_call(
        kernel,
        name=name,
        out_shape=[jax.ShapeDtypeStruct(shape, kind) for shape, kind in outs],
        in_specs=[in_vmem] * len(ins),
        out_specs=[in_vmem] * len(outs),
        compiler_params=pltpu.CompilerParams(vmem_limit_bytes=16 * 2**20),
        cost_estimate=pl.CostEstimate(flops=flops, bytes_accessed=size, transcendentals=exps),
    )(*ins)


def body(embeddings, prototypes, partner):
    count, width = embeddings.shape
    slots = prototypes.shape[0]
    entries = count * slots
    links = jnp.remainder(partner, count)
    y, z, x, core = (lax.axis_index(name) for name in ("y", "z", "x", "core"))
    y_count, z_count, x_count = (lax.axis_size(name) for name in ("y", "z", "x"))
    matrix, column = (count, slots), (FOLD, slots // FOLD)
    members = 2 * x_count
    own = block(embeddings, x * 2 + core, members)
    sent = shifted(own, "z", z_count // 2)
    views, protos, column_part = call(
        first_kernel,
        "first",
        [embeddings, prototypes],
        [((count, width), bf16), ((slots, width), bf16), ((y_count,) + column, f32)],
        flops=2 * entries * width,
        size=4 * slots * width,
        exps=entries,
    )

    def tempered_pass(mine, rows, totals):
        tempered, part = call(
            functools.partial(rows_kernel, mine),
            "tempered_pass",
            [rows, protos, totals],
            [(matrix, f32), ((members, 2 if mine else 1, count), f32)],
            flops=2 * entries * width,
            size=4 * slots * width,
            exps=entries,
        )
        return tempered, exchanged(part, proto_axes)

    def row_pass(tempered, totals):
        sums = ((members, 1, count), f32)
        (part,) = call(row_kernel, "row_pass", [tempered, totals], [sums], 3 * entries, 4 * count)
        return exchanged(part, proto_axes)

    def column_pass(tempered, totals):
        sums = ((y_count,) + column, f32)
        (part,) = call(col_kernel, "column_pass", [tempered, totals], [sums], 3 * entries, 4 * count)
        return total(exchanged(part, "y"))

    column_part, sent = lax.optimization_barrier((total(exchanged(column_part, "y")), sent))
    sent = gather_blocks(gather_blocks(sent, "core"), "x")
    column_total, sent = lax.optimization_barrier((gathered(column_part, "z"), sent))
    tempered, first = tempered_pass(True, views, column_total)
    for sweep in range(1, ITERS):
        row_total = row_pass(tempered, column_total) if sweep > 1 else first
        column_part = column_pass(tempered, row_total)
        if sweep == ITERS - 1:
            column_part, sent = lax.optimization_barrier((column_part, sent))
        column_total = gathered(column_part, "z")
    other_kernel, line_total = tempered_pass(False, sent[links], column_total)
    view_part, proto_part = call(
        gradient_kernel,
        "gradient",
        [other_kernel, column_total, line_total, first, views, protos],
        [((count, width), f32), ((slots, width), f32)],
        flops=6 * entries * width,
        size=8 * slots * width,
        exps=entries,
    )

    proto_rows = unit_rows(block(prototypes, y * z_count + z, y_count * z_count))[0]
    view_rows = unit_rows(block(embeddings, core * x_count + x, members))[0]
    proto_pieces = exchanged(proto_part.astype(SENT).reshape(y_count, -1, width), "y")
    proto_sum = total(proto_pieces).astype(SENT)
    proto_pieces = exchanged(proto_sum.reshape(z_count, -1, width), "z")
    proto_sum = (tangent(total(proto_pieces), proto_rows) * (1.0 / z_count)).astype(SENT)
    proto_sum = gathered(proto_sum, "z").reshape(-1, width)

    view_sum = scatter_sum(scatter_sum(view_part.astype(SENT), "core"), "x")
    view_sum = tangent(view_sum.astype(f32), view_rows).astype(SENT)
    view_sum = gather_blocks(gather_blocks(view_sum, "x"), "core")

    proto_sum = gathered(proto_sum, "y").reshape(slots, width)
    emb_grad = row_scale(embeddings) * view_sum.astype(f32)
    proto_grad = row_scale(prototypes) * float(z_count) * proto_sum.astype(f32)
    return (emb_grad, proto_grad)


def solution(mesh):
    inner = Mesh(mesh.devices.reshape(16, 4, 4, 2), ("z", "y", "x", "core"))
    return jax.shard_map(
        body,
        mesh=inner,
        in_specs=(P(rows_axes, None), P(proto_axes, None), P(rows_axes)),
        out_specs=(P(rows_axes, None), P(proto_axes, None)),
        check_vma=False,
    )
```

time: 336 us -> 252 us (0.75)
  waiting for transfers between devices: 96.4 us -> 48.1 us
  other arithmetic: 36.5 us -> 7.75 us
  Pallas kernels: 0 us -> 16.7 us
  matrix products: 15.7 us -> 0 us
  blocking collectives: 79.5 us -> 67.9 us
    ppermute x15 -> x13, waiting for transfers between devices: 58.6 us -> 9.09 us  [shifted(): return lax.ppermute(value, axis, pairs)]
    psum x3 -> x0, blocking collectives: 24.2 us -> none  [column_scale_of(): part = lax.psum(part, 'y')]
    reduce_sum x13 -> x7, other arithmetic: 20.2 us -> 1.84 us  [the longest x5 1.48 us: total(): return jnp.sum(pieces.astype(f32), axis=0)]
    pallas_call x0 -> x7, Pallas kernels: none -> 16.7 us  [call(): pl.pallas_call(kernel, name=name, out_shape=[jax.ShapeDtypeStruct(shape,...]
    dot_general x4 -> x0, matrix products: 15.7 us -> none  [the longest x1 6.43 us: body(): scores = jnp.dot(views, protos.T, preferred_element_type=jnp.float32)]
    all_to_all x3 -> x6, blocking collectives: 55.4 us -> 67.9 us  [exchanged(): return lax.all_to_all(value, axis, 0, 0, tiled=True)]
    ppermute x15 -> x13, starting transfers between devices: 49.2 us -> 59.1 us  [shifted(): return lax.ppermute(value, axis, pairs)]
    all_to_all x5 -> x7, starting transfers between devices: 43.2 us -> 34.2 us  [exchanged(): return lax.all_to_all(value, axis, 0, 0, tiled=True)]
  transfers between devices with their start and end apart: 20 -> 20, of which waited for: 16 -> 12; matrix products, arithmetic and copies ran while one was open for 5% -> 4% of each run, Pallas kernels for 0% -> 1%
where the time goes in v4:
time: 252 us; the launch traced here: 250 us
  starting transfers between devices  93.3 us (37%)
  blocking collectives  67.9 us (27%)
  waiting for transfers between devices  48.1 us (19%)
  Pallas kernels  16.7 us (7%)
  local copies, waits for them, and re-layouts  15.3 us (6%)
  other arithmetic  7.75 us (3%)
    all_to_all x6, blocking collectives, exchanged(): return lax.all_to_all(value, axis, 0, 0, tiled=True)  67.9 us
    ppermute x13, starting transfers between devices, shifted(): return lax.ppermute(value, axis, pairs)  59.1 us
    all_to_all x7, waiting for transfers between devices, exchanged(): return lax.all_to_all(value, axis, 0, 0, tiled=True)  39 us
    all_to_all x7, starting transfers between devices, exchanged(): return lax.all_to_all(value, axis, 0, 0, tiled=True)  34.2 us
    pallas_call x7, Pallas kernels, call(): pl.pallas_call(kernel, name=name, out_shape=[jax.ShapeDtypeStruct(shape,...  16.7 us
    ppermute x13, waiting for transfers between devices, shifted(): return lax.ppermute(value, axis, pairs)  9.09 us
    unnamed x18, local copies, waits for them, and re-layouts  6.89 us
  transfers between devices with their start and end apart: 20, of which 12 were waited for; matrix products, arithmetic and copies ran while one was open for 4% of the time, Pallas kernels for 1%

profile of v4, /device:TPU:1, one launch (start us, length us, event | category | flops | bytes accessed | tf_op | source)
XLA Modules:
  0.0 250.3 jit_solution(5168367860307108679)
XLA Ops:
  1.5 16.3 %collective-permute-start = (bf16[128,256]{1,0:T(8,128)(2,1)S(1)}, bf16[128,256]{1,0:T(8,128)(2,1)S(1)}, u32[]{:S(2)}, u32[]{:S(2)}) collective-permute-start(bf16[128,256]{1,0:T(8,128)(2,1)S(1)} %constant_dynamic-slice_fusion.4), channel_id=1, source_target_pairs={{0,256},{32,288},{64,320},{96,352},{128,384},{160,416},{192,448},{... | collective-permute-start | bytes 196616 | tf_op jit(solution)/shard_map/ppermute | solution.py:29
  23.5 4.2 %all-to-all-start = ((f32[4,8,256]{2,1,0:T(8,128)}), f32[4,8,256]{2,1,0:T(8,128)S(1)}, u32[]{:S(2)}, u32[]{:S(2)}) async-start(f32[4,8,256]{2,1,0:T(8,128)} %get-tuple-element.19), calls=%async_computation | async-start | bytes 65536 | tf_op jit(solution)/shard_map/all_to_all | solution.py:33
  27.7 4.3 %all-to-all-done = f32[4,8,256]{2,1,0:T(8,128)S(1)} async-done(((f32[4,8,256]{2,1,0:T(8,128)}), f32[4,8,256]{2,1,0:T(8,128)S(1)}, u32[]{:S(2)}, u32[]{:S(2)}) %all-to-all-start) | async-done | bytes 32800 | tf_op jit(solution)/shard_map/all_to_all | solution.py:33
  32.0 4.3 %collective-permute-start.1 = (bf16[128,256]{1,0:T(8,128)(2,1)S(1)}, bf16[128,256]{1,0:T(8,128)(2,1)S(1)}, u32[]{:S(2)}, u32[]{:S(2)}) collective-permute-start(bf16[128,256]{1,0:T(8,128)(2,1)S(1)} %collective-permute-done), channel_id=1, source_target_pairs={{0,1},{1,0},{2,3},{3,2},{4,5},{5,4},{6,7},{7,6},{8,9},{9,8},{10,11... | collective-permute-start | bytes 196616 | tf_op jit(solution)/shard_map/ppermute | solution.py:29
  41.1 4.9 %all-to-all-start.1 = ((f32[16,8,256]{2,1,0:T(8,128)}), f32[16,8,256]{2,1,0:T(8,128)S(1)}, u32[]{:S(2)}, u32[]{:S(2)}) async-start(f32[16,8,256]{2,1,0:T(8,128)} %broadcast_in_dim.84), calls=%async_computation.1 | async-start | bytes 262144 | tf_op jit(solution)/shard_map/all_to_all | solution.py:33
  45.9 4.4 %collective-permute-start.3 = (bf16[256,256]{1,0:T(8,128)(2,1)S(1)}, bf16[256,256]{1,0:T(8,128)(2,1)S(1)}, u32[]{:S(2)}, u32[]{:S(2)}) collective-permute-start(bf16[256,256]{1,0:T(8,128)(2,1)S(1)} %bitcast.44), channel_id=1, source_target_pairs={{0,4},{2,6},{4,0},{6,2},{1,5},{3,7},{5,1},{7,3},{8,12},{10,14},{12... | collective-permute-start | bytes 393224 | tf_op jit(solution)/shard_map/ppermute | solution.py:29
  61.1 12.3 %all_to_all.65.totals_ref.soft_ref = f32[8,2,1024]{2,1,0:T(2,128)S(1)} all-to-all(f32[8,2,1024]{2,1,0:T(2,128)S(1)} %get-tuple-element.24), channel_id=1, replica_groups=mesh['z'=16,'y'=4,'x'=4,'core'=2] {'x','core'}, dimensions={0} | all-to-all | bytes 131072 | tf_op jit(solution)/shard_map/all_to_all | solution.py:33
  74.5 6.7 %all_to_all.66 = f32[4,8,256]{2,1,0:T(8,128)S(1)} all-to-all(f32[4,8,256]{2,1,0:T(8,128)S(1)} %column_pass.2), channel_id=1, replica_groups=mesh['z'=16,'y'=4,'x'=4,'core'=2] {'y'}, dimensions={0} | all-to-all | bytes 65536 | tf_op jit(solution)/shard_map/all_to_all | solution.py:33
  81.1 20.2 %all_to_all.67.totals_ref = f32[16,8,256]{2,1,0:T(8,128)S(1)} all-to-all(f32[16,8,256]{2,1,0:T(8,128)S(1)} %broadcast_in_dim.92), channel_id=1, replica_groups=mesh['z'=16,'y'=4,'x'=4,'core'=2] {'z'}, dimensions={0} | all-to-all | bytes 262144 | tf_op jit(solution)/shard_map/all_to_all | solution.py:33
  105.6 11.2 %all_to_all.68.totals_ref = f32[8,1,1024]{2,1,0:T(1,128)S(1)} all-to-all(f32[8,1,1024]{2,1,0:T(1,128)S(1)} %row_pass.1), channel_id=1, replica_groups=mesh['z'=16,'y'=4,'x'=4,'core'=2] {'x','core'}, dimensions={0} | all-to-all | bytes 65536 | tf_op jit(solution)/shard_map/all_to_all | solution.py:33
  117.9 6.7 %all_to_all.69 = f32[4,8,256]{2,1,0:T(8,128)S(1)} all-to-all(f32[4,8,256]{2,1,0:T(8,128)S(1)} %column_pass.3), channel_id=1, replica_groups=mesh['z'=16,'y'=4,'x'=4,'core'=2] {'y'}, dimensions={0} | all-to-all | bytes 65536 | tf_op jit(solution)/shard_map/all_to_all | solution.py:33
  125.2 3.5 %all-to-all-start.7 = ((f32[16,8,256]{2,1,0:T(8,128)}), f32[16,8,256]{2,1,0:T(8,128)S(1)}, u32[]{:S(2)}, u32[]{:S(2)}) async-start(f32[16,8,256]{2,1,0:T(8,128)} %broadcast_in_dim.94), calls=%async_computation.7 | async-start | bytes 262144 | tf_op jit(solution)/shard_map/all_to_all | solution.py:33
  128.7 3.9 %gather_fusion = bf16[1024,256]{1,0:T(8,128)(2,1)S(1)} fusion(bf16[1024,256]{1,0:T(8,128)(2,1)S(1)} %bitcast.38, s32[1024]{0:T(1024)S(1)} %fusion.12), kind=kCustom, calls=%fused_computation | custom fusion | bytes 1052672 | tf_op jit(solution)/shard_map/gather | solution.py:288
  132.7 8.0 %all-to-all-done.7.totals_ref = f32[16,8,256]{2,1,0:T(8,128)S(1)} async-done(((f32[16,8,256]{2,1,0:T(8,128)}), f32[16,8,256]{2,1,0:T(8,128)S(1)}, u32[]{:S(2)}, u32[]{:S(2)}) %all-to-all-start.7) | async-done | bytes 131104 | tf_op jit(solution)/shard_map/all_to_all | solution.py:33
  143.4 10.9 %all_to_all.70.line_ref = f32[8,1,1024]{2,1,0:T(1,128)S(1)} all-to-all(f32[8,1,1024]{2,1,0:T(1,128)S(1)} %get-tuple-element.29), channel_id=1, replica_groups=mesh['z'=16,'y'=4,'x'=4,'core'=2] {'x','core'}, dimensions={0} | all-to-all | bytes 65536 | tf_op jit(solution)/shard_map/all_to_all | solution.py:33
  155.5 4.4 %gradient.1 = (f32[1024,256]{1,0:T(8,128)S(1)}, f32[2048,256]{1,0:T(8,128)S(1)}) custom-call(f32[1024,2048]{1,0:T(8,128)S(1)} %get-tuple-element.28.other_ref, f32[16,8,256]{2,1,0:T(8,128)S(1)} %all-to-all-done.7.totals_ref, f32[8,1,1024]{2,1,0:T(1,128)S(1)} %all_to_all.70.line_ref, f32[8,2,1024]{2,1,0:T(2,128)S(1)} %all_to_all.65.totals_ref.soft_ref, ...), custom_call_target="tpu_custom_call" | custom-call | flops 3221225472 | bytes 4194304 | tf_op jit(solution)/shard_map/gradient/pallas_call | solution.py:224
  161.0 4.3 %all-to-all-start.9 = ((f16[4,512,256]{2,1,0:T(8,128)(2,1)}), f16[4,512,256]{2,1,0:T(8,128)(2,1)}, u32[]{:S(2)}, u32[]{:S(2)}) async-start(f16[4,512,256]{2,1,0:T(8,128)(2,1)} %bitcast.39), calls=%async_computation.9 | async-start | bytes 2097152 | tf_op jit(solution)/shard_map/all_to_all | solution.py:33
  168.8 11.0 %all-to-all-done.9 = f16[4,512,256]{2,1,0:T(8,128)(2,1)} async-done(((f16[4,512,256]{2,1,0:T(8,128)(2,1)}), f16[4,512,256]{2,1,0:T(8,128)(2,1)}, u32[]{:S(2)}, u32[]{:S(2)}) %all-to-all-start.9) | async-done | bytes 1048608 | tf_op jit(solution)/shard_map/all_to_all | solution.py:33
  182.0 3.5 %all-to-all-start.10 = ((f16[16,32,256]{2,1,0:T(8,128)(2,1)}), f16[16,32,256]{2,1,0:T(8,128)(2,1)S(1)}, u32[]{:S(2)}, u32[]{:S(2)}) async-start(f16[16,32,256]{2,1,0:T(8,128)(2,1)} %bitcast.17), calls=%async_computation.10 | async-start | bytes 524288 | tf_op jit(solution)/shard_map/all_to_all | solution.py:33
  187.9 3.7 %collective-permute-start.7 = (f16[128,256]{1,0:T(8,128)(2,1)S(1)}, f16[128,256]{1,0:T(8,128)(2,1)S(1)}, u32[]{:S(2)}, u32[]{:S(2)}) collective-permute-start(f16[128,256]{1,0:T(8,128)(2,1)S(1)} %get-tuple-element.38), channel_id=1, source_target_pairs={{0,4},{2,6},{4,0},{6,2},{1,5},{3,7},{5,1},{7,3},{8,12},{10,14},{12... | collective-permute-start | bytes 196616 | tf_op jit(solution)/shard_map/ppermute | solution.py:29
  199.4 10.3 %all-to-all-start.11 = ((f16[16,32,256]{2,1,0:T(8,128)(2,1)}), f16[16,32,256]{2,1,0:T(8,128)(2,1)S(1)}, u32[]{:S(2)}, u32[]{:S(2)}) async-start(f16[16,32,256]{2,1,0:T(8,128)(2,1)} %broadcast_in_dim.100), calls=%async_computation.11 | async-start | bytes 524288 | tf_op jit(solution)/shard_map/all_to_all | solution.py:33
  222.2 7.1 %collective-permute-start.12 = (f16[512,256]{1,0:T(8,128)(2,1)S(1)}, f16[512,256]{1,0:T(8,128)(2,1)S(1)}, u32[]{:S(2)}, u32[]{:S(2)}) collective-permute-start(f16[512,256]{1,0:T(8,128)(2,1)S(1)} %bitcast.41), channel_id=1, source_target_pairs={{0,1},{1,0},{2,3},{3,2},{4,5},{5,4},{6,7},{7,6},{8,9},{9,8},{10,11... | collective-permute-start | bytes 786440 | tf_op jit(solution)/shard_map/ppermute | solution.py:29
  230.4 3.5 %all-to-all-start.12 = ((f16[4,512,256]{2,1,0:T(8,128)(2,1)}), f16[4,512,256]{2,1,0:T(8,128)(2,1)S(1)}, u32[]{:S(2)}, u32[]{:S(2)}) async-start(f16[4,512,256]{2,1,0:T(8,128)(2,1)} %broadcast_in_dim.102), calls=%async_computation.12 | async-start | bytes 2097152 | tf_op jit(solution)/shard_map/all_to_all | solution.py:33
  235.3 13.3 %all-to-all-done.12 = f16[4,512,256]{2,1,0:T(8,128)(2,1)S(1)} async-done(((f16[4,512,256]{2,1,0:T(8,128)(2,1)}), f16[4,512,256]{2,1,0:T(8,128)(2,1)S(1)}, u32[]{:S(2)}, u32[]{:S(2)}) %all-to-all-start.12) | async-done | bytes 1048608 | tf_op jit(solution)/shard_map/all_to_all | solution.py:33
  (95 shorter events, 66.3 us)
Async XLA Ops:
  1.5 30.5 %collective-permute-start = (bf16[128,256]{1,0:T(8,128)(2,1)S(1)}, bf16[128,256]{1,0:T(8,128)(2,1)S(1)}, u32[]{:S(2)}, u32[]{:S(2)}) collective-permute-start(bf16[128,256]{1,0:T(8,128)(2,1)S(1)} %constant_dynamic-slice_fusion.4), channel_id=1, source_target_pairs={{0,256},{32,288},{64,320},{96,352},{128,384},{160,416},{192,448},{... | collective-permute-start | bytes 196616 | tf_op jit(solution)/shard_map/ppermute | solution.py:29
  23.5 117.2 %copy-start.6 = (bf16[2048,256]{1,0:T(8,128)(2,1)}, bf16[2048,256]{1,0:T(8,128)(2,1)S(1)}, u32[]{:S(2)}) copy-start(bf16[2048,256]{1,0:T(8,128)(2,1)S(1)} %get-tuple-element.18.protos_ref) | copy-start | bytes 3145732
  23.5 8.5 %all-to-all-start = ((f32[4,8,256]{2,1,0:T(8,128)}), f32[4,8,256]{2,1,0:T(8,128)S(1)}, u32[]{:S(2)}, u32[]{:S(2)}) async-start(f32[4,8,256]{2,1,0:T(8,128)} %get-tuple-element.19), calls=%async_computation | async-start | bytes 65536 | tf_op jit(solution)/shard_map/all_to_all | solution.py:33
  32.0 5.2 %collective-permute-start.1 = (bf16[128,256]{1,0:T(8,128)(2,1)S(1)}, bf16[128,256]{1,0:T(8,128)(2,1)S(1)}, u32[]{:S(2)}, u32[]{:S(2)}) collective-permute-start(bf16[128,256]{1,0:T(8,128)(2,1)S(1)} %collective-permute-done), channel_id=1, source_target_pairs={{0,1},{1,0},{2,3},{3,2},{4,5},{5,4},{6,7},{7,6},{8,9},{9,8},{10,11... | collective-permute-start | bytes 196616 | tf_op jit(solution)/shard_map/ppermute | solution.py:29
  37.2 16.2 %collective-permute-start.2 = (bf16[256,256]{1,0:T(8,128)(2,1)S(1)}, bf16[256,256]{1,0:T(8,128)(2,1)S(1)}, u32[]{:S(2)}, u32[]{:S(2)}) collective-permute-start(bf16[256,256]{1,0:T(8,128)(2,1)S(1)} %bitcast.43), channel_id=1, source_target_pairs={{0,2},{2,4},{4,6},{6,0},{1,3},{3,5},{5,7},{7,1},{8,10},{10,12},{12... | collective-permute-start | bytes 393224 | tf_op jit(solution)/shard_map/ppermute | solution.py:29
  41.1 16.9 %all-to-all-start.1 = ((f32[16,8,256]{2,1,0:T(8,128)}), f32[16,8,256]{2,1,0:T(8,128)S(1)}, u32[]{:S(2)}, u32[]{:S(2)}) async-start(f32[16,8,256]{2,1,0:T(8,128)} %broadcast_in_dim.84), calls=%async_computation.1 | async-start | bytes 262144 | tf_op jit(solution)/shard_map/all_to_all | solution.py:33
  45.9 7.5 %collective-permute-start.3 = (bf16[256,256]{1,0:T(8,128)(2,1)S(1)}, bf16[256,256]{1,0:T(8,128)(2,1)S(1)}, u32[]{:S(2)}, u32[]{:S(2)}) collective-permute-start(bf16[256,256]{1,0:T(8,128)(2,1)S(1)} %bitcast.44), channel_id=1, source_target_pairs={{0,4},{2,6},{4,0},{6,2},{1,5},{3,7},{5,1},{7,3},{8,12},{10,14},{12... | collective-permute-start | bytes 393224 | tf_op jit(solution)/shard_map/ppermute | solution.py:29
  50.3 6.0 %collective-permute-start.4 = (bf16[256,256]{1,0:T(8,128)(2,1)S(1)}, bf16[256,256]{1,0:T(8,128)(2,1)S(1)}, u32[]{:S(2)}, u32[]{:S(2)}) collective-permute-start(bf16[256,256]{1,0:T(8,128)(2,1)S(1)} %bitcast.45), channel_id=1, source_target_pairs={{0,6},{2,0},{4,2},{6,4},{1,7},{3,1},{5,3},{7,5},{8,14},{10,8},{12,... | collective-permute-start | bytes 393224 | tf_op jit(solution)/shard_map/ppermute | solution.py:29
  61.1 13.3 %copy-start = (f32[1024,2048]{1,0:T(8,128)}, f32[1024,2048]{1,0:T(8,128)S(1)}, u32[]{:S(2)}) copy-start(f32[1024,2048]{1,0:T(8,128)S(1)} %get-tuple-element.23.temp_ref) | copy-start | bytes 25165828
  116.9 11.8 %copy-start.8 = (s32[1024]{0:T(1024)S(1)}, s32[1024]{0:T(1024)}, u32[]{:S(2)}) copy-start(s32[1024]{0:T(1024)} %param.5) | copy-start | bytes 12292
  125.2 15.5 %all-to-all-start.7 = ((f32[16,8,256]{2,1,0:T(8,128)}), f32[16,8,256]{2,1,0:T(8,128)S(1)}, u32[]{:S(2)}, u32[]{:S(2)}) async-start(f32[16,8,256]{2,1,0:T(8,128)} %broadcast_in_dim.94), calls=%async_computation.7 | async-start | bytes 262144 | tf_op jit(solution)/shard_map/all_to_all | solution.py:33
  159.9 5.6 %copy-start.3 = (bf16[1024,256]{1,0:T(8,128)(2,1)S(1)}, bf16[1024,256]{1,0:T(8,128)(2,1)}, u32[]{:S(2)}) copy-start(bf16[1024,256]{1,0:T(8,128)(2,1)} %emb_ref.1) | copy-start | bytes 1572868
  161.0 18.8 %all-to-all-start.9 = ((f16[4,512,256]{2,1,0:T(8,128)(2,1)}), f16[4,512,256]{2,1,0:T(8,128)(2,1)}, u32[]{:S(2)}, u32[]{:S(2)}) async-start(f16[4,512,256]{2,1,0:T(8,128)(2,1)} %bitcast.39), calls=%async_computation.9 | async-start | bytes 2097152 | tf_op jit(solution)/shard_map/all_to_all | solution.py:33
  166.1 19.4 %collective-permute-start.5 = (f16[512,256]{1,0:T(8,128)(2,1)S(1)}, f16[512,256]{1,0:T(8,128)(2,1)S(1)}, u32[]{:S(2)}, u32[]{:S(2)}) collective-permute-start(f16[512,256]{1,0:T(8,128)(2,1)S(1)} %constant_dynamic-slice_fusion.3), channel_id=1, source_target_pairs={{0,1},{1,0},{2,3},{3,2},{4,5},{5,4},{6,7},{7,6},{8,9},{9,8},{10,11... | collective-permute-start | bytes 786440 | tf_op jit(solution)/shard_map/ppermute | solution.py:29
  182.0 16.3 %all-to-all-start.10 = ((f16[16,32,256]{2,1,0:T(8,128)(2,1)}), f16[16,32,256]{2,1,0:T(8,128)(2,1)S(1)}, u32[]{:S(2)}, u32[]{:S(2)}) async-start(f16[16,32,256]{2,1,0:T(8,128)(2,1)} %bitcast.17), calls=%async_computation.10 | async-start | bytes 524288 | tf_op jit(solution)/shard_map/all_to_all | solution.py:33
  185.7 8.6 %collective-permute-start.6 = (f16[128,256]{1,0:T(8,128)(2,1)S(1)}, f16[128,256]{1,0:T(8,128)(2,1)S(1)}, u32[]{:S(2)}, u32[]{:S(2)}) collective-permute-start(f16[128,256]{1,0:T(8,128)(2,1)S(1)} %get-tuple-element.36), channel_id=1, source_target_pairs={{0,2},{2,4},{4,6},{6,0},{1,3},{3,5},{5,7},{7,1},{8,10},{10,12},{12... | collective-permute-start | bytes 196616 | tf_op jit(solution)/shard_map/ppermute | solution.py:29
  187.9 6.8 %collective-permute-start.7 = (f16[128,256]{1,0:T(8,128)(2,1)S(1)}, f16[128,256]{1,0:T(8,128)(2,1)S(1)}, u32[]{:S(2)}, u32[]{:S(2)}) collective-permute-start(f16[128,256]{1,0:T(8,128)(2,1)S(1)} %get-tuple-element.38), channel_id=1, source_target_pairs={{0,4},{2,6},{4,0},{6,2},{1,5},{3,7},{5,1},{7,3},{8,12},{10,14},{12... | collective-permute-start | bytes 196616 | tf_op jit(solution)/shard_map/ppermute | solution.py:29
  191.6 5.8 %collective-permute-start.8 = (f16[128,256]{1,0:T(8,128)(2,1)S(1)}, f16[128,256]{1,0:T(8,128)(2,1)S(1)}, u32[]{:S(2)}, u32[]{:S(2)}) collective-permute-start(f16[128,256]{1,0:T(8,128)(2,1)S(1)} %get-tuple-element.37), channel_id=1, source_target_pairs={{0,6},{2,0},{4,2},{6,4},{1,7},{3,1},{5,3},{7,5},{8,14},{10,8},{12,... | collective-permute-start | bytes 196616 | tf_op jit(solution)/shard_map/ppermute | solution.py:29
  199.4 30.0 %all-to-all-start.11 = ((f16[16,32,256]{2,1,0:T(8,128)(2,1)}), f16[16,32,256]{2,1,0:T(8,128)(2,1)S(1)}, u32[]{:S(2)}, u32[]{:S(2)}) async-start(f16[16,32,256]{2,1,0:T(8,128)(2,1)} %broadcast_in_dim.100), calls=%async_computation.11 | async-start | bytes 524288 | tf_op jit(solution)/shard_map/all_to_all | solution.py:33
  209.8 9.9 %collective-permute-start.9 = (f16[128,256]{1,0:T(8,128)(2,1)S(1)}, f16[128,256]{1,0:T(8,128)(2,1)S(1)}, u32[]{:S(2)}, u32[]{:S(2)}) collective-permute-start(f16[128,256]{1,0:T(8,128)(2,1)S(1)} %get-tuple-element.33), channel_id=1, source_target_pairs={{0,2},{2,4},{4,6},{6,0},{1,3},{3,5},{5,7},{7,1},{8,10},{10,12},{12... | collective-permute-start | bytes 196616 | tf_op jit(solution)/shard_map/ppermute | solution.py:29
  213.5 6.9 %collective-permute-start.10 = (f16[128,256]{1,0:T(8,128)(2,1)S(1)}, f16[128,256]{1,0:T(8,128)(2,1)S(1)}, u32[]{:S(2)}, u32[]{:S(2)}) collective-permute-start(f16[128,256]{1,0:T(8,128)(2,1)S(1)} %get-tuple-element.33), channel_id=1, source_target_pairs={{0,4},{2,6},{4,0},{6,2},{1,5},{3,7},{5,1},{7,3},{8,12},{10,14},{12... | collective-permute-start | bytes 196616 | tf_op jit(solution)/shard_map/ppermute | solution.py:29
  216.9 5.3 %collective-permute-start.11 = (f16[128,256]{1,0:T(8,128)(2,1)S(1)}, f16[128,256]{1,0:T(8,128)(2,1)S(1)}, u32[]{:S(2)}, u32[]{:S(2)}) collective-permute-start(f16[128,256]{1,0:T(8,128)(2,1)S(1)} %get-tuple-element.33), channel_id=1, source_target_pairs={{0,6},{2,0},{4,2},{6,4},{1,7},{3,1},{5,3},{7,5},{8,14},{10,8},{12,... | collective-permute-start | bytes 196616 | tf_op jit(solution)/shard_map/ppermute | solution.py:29
  222.2 11.8 %collective-permute-start.12 = (f16[512,256]{1,0:T(8,128)(2,1)S(1)}, f16[512,256]{1,0:T(8,128)(2,1)S(1)}, u32[]{:S(2)}, u32[]{:S(2)}) collective-permute-start(f16[512,256]{1,0:T(8,128)(2,1)S(1)} %bitcast.41), channel_id=1, source_target_pairs={{0,1},{1,0},{2,3},{3,2},{4,5},{5,4},{6,7},{7,6},{8,9},{9,8},{10,11... | collective-permute-start | bytes 786440 | tf_op jit(solution)/shard_map/ppermute | solution.py:29
  230.4 18.2 %all-to-all-start.12 = ((f16[4,512,256]{2,1,0:T(8,128)(2,1)}), f16[4,512,256]{2,1,0:T(8,128)(2,1)S(1)}, u32[]{:S(2)}, u32[]{:S(2)}) async-start(f16[4,512,256]{2,1,0:T(8,128)(2,1)} %broadcast_in_dim.102), calls=%async_computation.12 | async-start | bytes 2097152 | tf_op jit(solution)/shard_map/all_to_all | solution.py:33
  (5 other events, 12.4 us)

commit v5 on v4

--- a/solution.py
+++ b/solution.py
@@ -21,6 +21,7 @@
 bf16 = jnp.bfloat16
 SENT = jnp.float16
 FOLD = 8
+LOG2_E = 1.4426950408889634
 
 
 def shifted(value, axis, steps):
@@ -54,7 +55,10 @@
 
 
 def total(pieces):
-    return jnp.sum(pieces.astype(f32), axis=0)
+    parts = [pieces[index].astype(f32) for index in range(pieces.shape[0])]
+    while len(parts) > 1:
+        parts = [left + right for left, right in zip(parts[::2], parts[1::2], strict=True)]
+    return parts[0]
 
 
 def block(value, index, count):
@@ -116,7 +120,7 @@
     scores = lax.dot_general(
         units, protos_ref[...], (((1,), (1,)), ((), ())), preferred_element_type=f32
     )
-    return jnp.exp(scores * (1.0 / divisor))
+    return jnp.exp2(scores * (LOG2_E / divisor))
 
 
 def steps(count):
@@ -167,17 +171,6 @@
         if own:
             row_ref[0, 1:, rows] = as_row(soft)
 
-    for_each_receiver(row_ref)
-
-
-def row_kernel(temp_ref, totals_ref, row_ref):
-    column_scale = 1.0 / jnp.sum(totals_ref[...], axis=0)
-    for rows in steps(temp_ref.shape[0]):
-        total = jnp.zeros((ROWS, LANES), f32)
-        for start in tiles(temp_ref):
-            value = temp_ref[rows, start : start + LANES]
-            total = total + value * value * column_tile(column_scale, start)
-        row_ref[0, :, rows] = as_row(total)
     for_each_receiver(row_ref)
 
 
@@ -265,22 +258,16 @@
         )
         return tempered, exchanged(part, proto_axes)
 
-    def row_pass(tempered, totals):
-        sums = ((members, 1, count), f32)
-        (part,) = call(row_kernel, "row_pass", [tempered, totals], [sums], 3 * entries, 4 * count)
-        return exchanged(part, proto_axes)
-
     def column_pass(tempered, totals):
         sums = ((y_count,) + column, f32)
         (part,) = call(col_kernel, "column_pass", [tempered, totals], [sums], 3 * entries, 4 * count)
         return total(exchanged(part, "y"))
 
-    column_part, sent = lax.optimization_barrier((total(exchanged(column_part, "y")), sent))
     sent = gather_blocks(gather_blocks(sent, "core"), "x")
+    column_part = total(exchanged(column_part, "y"))
     column_total, sent = lax.optimization_barrier((gathered(column_part, "z"), sent))
-    tempered, first = tempered_pass(True, views, column_total)
     for sweep in range(1, ITERS):
-        row_total = row_pass(tempered, column_total) if sweep > 1 else first
+        tempered, row_total = tempered_pass(True, views, column_total)
         column_part = column_pass(tempered, row_total)
         if sweep == ITERS - 1:
             column_part, sent = lax.optimization_barrier((column_part, sent))
@@ -289,7 +276,7 @@
     view_part, proto_part = call(
         gradient_kernel,
         "gradient",
-        [other_kernel, column_total, line_total, first, views, protos],
+        [other_kernel, column_total, line_total, row_total, views, protos],
         [((count, width), f32), ((slots, width), f32)],
         flops=6 * entries * width,
         size=8 * slots * width,

time: 252 us -> 247 us (0.980)
  waiting for transfers between devices: 48.1 us -> 44 us
  local copies, waits for them, and re-layouts: 15.3 us -> 11.9 us
    all_to_all x7, waiting for transfers between devices: 39 us -> 34.8 us  [exchanged(): return lax.all_to_all(value, axis, 0, 0, tiled=True)]
    unnamed x18 -> x14, local copies, waits for them, and re-layouts: 6.89 us -> 3.51 us
  transfers between devices with their start and end apart: 20 -> 20, of which waited for: 12 -> 11; matrix products, arithmetic and copies ran while one was open for 4% -> 4% of each run, Pallas kernels for 1% -> 1%
where the time goes in v5:
time: 247 us; the launch traced here: 246 us
  starting transfers between devices  93.5 us (38%)
  blocking collectives  69.9 us (28%)
  waiting for transfers between devices  44 us (18%)
  Pallas kernels  17.7 us (7%)
  local copies, waits for them, and re-layouts  11.9 us (5%)
  other arithmetic  7.57 us (3%)
    all_to_all x6, blocking collectives, exchanged(): return lax.all_to_all(value, axis, 0, 0, tiled=True)  69.9 us
    ppermute x13, starting transfers between devices, shifted(): return lax.ppermute(value, axis, pairs)  57.3 us
    all_to_all x7, starting transfers between devices, exchanged(): return lax.all_to_all(value, axis, 0, 0, tiled=True)  36.1 us
    all_to_all x7, waiting for transfers between devices, exchanged(): return lax.all_to_all(value, axis, 0, 0, tiled=True)  34.8 us
    pallas_call x7, Pallas kernels, call(): pl.pallas_call(kernel, name=name, out_shape=[jax.ShapeDtypeStruct(shape,...  17.7 us
    ppermute x13, waiting for transfers between devices, shifted(): return lax.ppermute(value, axis, pairs)  9.24 us
  transfers between devices with their start and end apart: 20, of which 11 were waited for; matrix products, arithmetic and copies ran while one was open for 4% of the time, Pallas kernels for 1%

profile of v5, /device:TPU:1, one launch (start us, length us, event | category | flops | bytes accessed | tf_op | source)
XLA Modules:
  0.0 245.7 jit_solution(2118063808237430926)
XLA Ops:
  1.5 16.3 %collective-permute-start = (bf16[128,256]{1,0:T(8,128)(2,1)S(1)}, bf16[128,256]{1,0:T(8,128)(2,1)S(1)}, u32[]{:S(2)}, u32[]{:S(2)}) collective-permute-start(bf16[128,256]{1,0:T(8,128)(2,1)S(1)} %constant_dynamic-slice_fusion.4), channel_id=1, source_target_pairs={{0,256},{32,288},{64,320},{96,352},{128,384},{160,416},{192,448},{... | collective-permute-start | bytes 196616 | tf_op jit(solution)/shard_map/ppermute | solution.py:30
  20.0 3.3 %first.1 = (bf16[1024,256]{1,0:T(8,128)(2,1)S(1)}, bf16[2048,256]{1,0:T(8,128)(2,1)S(1)}, f32[4,8,256]{2,1,0:T(8,128)}) custom-call(bf16[1024,256]{1,0:T(8,128)(2,1)S(1)} %copy-done, bf16[2048,256]{1,0:T(8,128)(2,1)S(1)} %copy-done.2), custom_call_target="tpu_custom_call" | custom-call | flops 1073741824 | bytes 2097152 | tf_op jit(solution)/shard_map/first/pallas_call | solution.py:217
  23.3 4.2 %all-to-all-start = ((f32[4,8,256]{2,1,0:T(8,128)}), f32[4,8,256]{2,1,0:T(8,128)S(1)}, u32[]{:S(2)}, u32[]{:S(2)}) async-start(f32[4,8,256]{2,1,0:T(8,128)} %get-tuple-element.19), calls=%async_computation | async-start | bytes 65536 | tf_op jit(solution)/shard_map/all_to_all | solution.py:34
  35.3 6.5 %all-to-all-start.1 = ((f32[16,8,256]{2,1,0:T(8,128)}), f32[16,8,256]{2,1,0:T(8,128)S(1)}, u32[]{:S(2)}, u32[]{:S(2)}) async-start(f32[16,8,256]{2,1,0:T(8,128)} %broadcast_in_dim.89), calls=%async_computation.1 | async-start | bytes 262144 | tf_op jit(solution)/shard_map/all_to_all | solution.py:34
  41.8 4.4 %collective-permute-start.3 = (bf16[256,256]{1,0:T(8,128)(2,1)S(1)}, bf16[256,256]{1,0:T(8,128)(2,1)S(1)}, u32[]{:S(2)}, u32[]{:S(2)}) collective-permute-start(bf16[256,256]{1,0:T(8,128)(2,1)S(1)} %bitcast.53), channel_id=1, source_target_pairs={{0,4},{2,6},{4,0},{6,2},{1,5},{3,7},{5,1},{7,3},{8,12},{10,14},{12... | collective-permute-start | bytes 393224 | tf_op jit(solution)/shard_map/ppermute | solution.py:30
  56.7 12.3 %all_to_all.65.totals_ref = f32[8,2,1024]{2,1,0:T(2,128)S(1)} all-to-all(f32[8,2,1024]{2,1,0:T(2,128)S(1)} %get-tuple-element.22), channel_id=1, replica_groups=mesh['z'=16,'y'=4,'x'=4,'core'=2] {'x','core'}, dimensions={0} | all-to-all | bytes 131072 | tf_op jit(solution)/shard_map/all_to_all | solution.py:34
  70.1 8.3 %all_to_all.66 = f32[4,8,256]{2,1,0:T(8,128)S(1)} all-to-all(f32[4,8,256]{2,1,0:T(8,128)S(1)} %column_pass.2), channel_id=1, replica_groups=mesh['z'=16,'y'=4,'x'=4,'core'=2] {'y'}, dimensions={0} | all-to-all | bytes 65536 | tf_op jit(solution)/shard_map/all_to_all | solution.py:34
  78.4 20.2 %all_to_all.67.totals_ref = f32[16,8,256]{2,1,0:T(8,128)S(1)} all-to-all(f32[16,8,256]{2,1,0:T(8,128)S(1)} %broadcast_in_dim.98), channel_id=1, replica_groups=mesh['z'=16,'y'=4,'x'=4,'core'=2] {'z'}, dimensions={0} | all-to-all | bytes 262144 | tf_op jit(solution)/shard_map/all_to_all | solution.py:34
  101.5 11.1 %all_to_all.68.totals_ref.soft_ref = f32[8,2,1024]{2,1,0:T(2,128)S(1)} all-to-all(f32[8,2,1024]{2,1,0:T(2,128)S(1)} %get-tuple-element.24), channel_id=1, replica_groups=mesh['z'=16,'y'=4,'x'=4,'core'=2] {'x','core'}, dimensions={0} | all-to-all | bytes 131072 | tf_op jit(solution)/shard_map/all_to_all | solution.py:34
  113.6 6.7 %all_to_all.69 = f32[4,8,256]{2,1,0:T(8,128)S(1)} all-to-all(f32[4,8,256]{2,1,0:T(8,128)S(1)} %column_pass.3), channel_id=1, replica_groups=mesh['z'=16,'y'=4,'x'=4,'core'=2] {'y'}, dimensions={0} | all-to-all | bytes 65536 | tf_op jit(solution)/shard_map/all_to_all | solution.py:34
  121.0 3.5 %all-to-all-start.7 = ((f32[16,8,256]{2,1,0:T(8,128)}), f32[16,8,256]{2,1,0:T(8,128)S(1)}, u32[]{:S(2)}, u32[]{:S(2)}) async-start(f32[16,8,256]{2,1,0:T(8,128)} %broadcast_in_dim.100), calls=%async_computation.7 | async-start | bytes 262144 | tf_op jit(solution)/shard_map/all_to_all | solution.py:34
  124.5 3.9 %gather_fusion = bf16[1024,256]{1,0:T(8,128)(2,1)S(1)} fusion(bf16[1024,256]{1,0:T(8,128)(2,1)S(1)} %bitcast.47, s32[1024]{0:T(1024)S(1)} %fusion.18), kind=kCustom, calls=%fused_computation | custom fusion | bytes 1052672 | tf_op jit(solution)/shard_map/gather | solution.py:275
  128.5 7.9 %all-to-all-done.7.totals_ref = f32[16,8,256]{2,1,0:T(8,128)S(1)} async-done(((f32[16,8,256]{2,1,0:T(8,128)}), f32[16,8,256]{2,1,0:T(8,128)S(1)}, u32[]{:S(2)}, u32[]{:S(2)}) %all-to-all-start.7) | async-done | bytes 131104 | tf_op jit(solution)/shard_map/all_to_all | solution.py:34
  138.8 11.2 %all_to_all.70.line_ref = f32[8,1,1024]{2,1,0:T(1,128)S(1)} all-to-all(f32[8,1,1024]{2,1,0:T(1,128)S(1)} %get-tuple-element.29), channel_id=1, replica_groups=mesh['z'=16,'y'=4,'x'=4,'core'=2] {'x','core'}, dimensions={0} | all-to-all | bytes 65536 | tf_op jit(solution)/shard_map/all_to_all | solution.py:34
  151.3 4.2 %gradient.1 = (f32[1024,256]{1,0:T(8,128)S(1)}, f32[2048,256]{1,0:T(8,128)S(1)}) custom-call(f32[1024,2048]{1,0:T(8,128)S(1)} %get-tuple-element.28.other_ref, f32[16,8,256]{2,1,0:T(8,128)S(1)} %all-to-all-done.7.totals_ref, f32[8,1,1024]{2,1,0:T(1,128)S(1)} %all_to_all.70.line_ref, f32[8,2,1024]{2,1,0:T(2,128)S(1)} %all_to_all.68.totals_ref.soft_ref, ...), custom_call_target="tpu_custom_call" | custom-call | flops 3221225472 | bytes 4194304 | tf_op jit(solution)/shard_map/gradient/pallas_call | solution.py:217
  156.6 4.2 %all-to-all-start.9 = ((f16[4,512,256]{2,1,0:T(8,128)(2,1)}), f16[4,512,256]{2,1,0:T(8,128)(2,1)}, u32[]{:S(2)}, u32[]{:S(2)}) async-start(f16[4,512,256]{2,1,0:T(8,128)(2,1)} %bitcast.48), calls=%async_computation.9 | async-start | bytes 2097152 | tf_op jit(solution)/shard_map/all_to_all | solution.py:34
  164.3 11.0 %all-to-all-done.9 = f16[4,512,256]{2,1,0:T(8,128)(2,1)} async-done(((f16[4,512,256]{2,1,0:T(8,128)(2,1)}), f16[4,512,256]{2,1,0:T(8,128)(2,1)}, u32[]{:S(2)}, u32[]{:S(2)}) %all-to-all-start.9) | async-done | bytes 1048608 | tf_op jit(solution)/shard_map/all_to_all | solution.py:34
  177.4 3.5 %all-to-all-start.10 = ((f16[16,32,256]{2,1,0:T(8,128)(2,1)}), f16[16,32,256]{2,1,0:T(8,128)(2,1)S(1)}, u32[]{:S(2)}, u32[]{:S(2)}) async-start(f16[16,32,256]{2,1,0:T(8,128)(2,1)} %bitcast.20), calls=%async_computation.10 | async-start | bytes 524288 | tf_op jit(solution)/shard_map/all_to_all | solution.py:34
  183.3 3.7 %collective-permute-start.7 = (f16[128,256]{1,0:T(8,128)(2,1)S(1)}, f16[128,256]{1,0:T(8,128)(2,1)S(1)}, u32[]{:S(2)}, u32[]{:S(2)}) collective-permute-start(f16[128,256]{1,0:T(8,128)(2,1)S(1)} %get-tuple-element.40), channel_id=1, source_target_pairs={{0,4},{2,6},{4,0},{6,2},{1,5},{3,7},{5,1},{7,3},{8,12},{10,14},{12... | collective-permute-start | bytes 196616 | tf_op jit(solution)/shard_map/ppermute | solution.py:30
  194.7 10.7 %all-to-all-start.11 = ((f16[16,32,256]{2,1,0:T(8,128)(2,1)}), f16[16,32,256]{2,1,0:T(8,128)(2,1)S(1)}, u32[]{:S(2)}, u32[]{:S(2)}) async-start(f16[16,32,256]{2,1,0:T(8,128)(2,1)} %broadcast_in_dim.106), calls=%async_computation.11 | async-start | bytes 524288 | tf_op jit(solution)/shard_map/all_to_all | solution.py:34
  208.8 3.5 %collective-permute-start.10 = (f16[128,256]{1,0:T(8,128)(2,1)S(1)}, f16[128,256]{1,0:T(8,128)(2,1)S(1)}, u32[]{:S(2)}, u32[]{:S(2)}) collective-permute-start(f16[128,256]{1,0:T(8,128)(2,1)S(1)} %get-tuple-element.35), channel_id=1, source_target_pairs={{0,4},{2,6},{4,0},{6,2},{1,5},{3,7},{5,1},{7,3},{8,12},{10,14},{12... | collective-permute-start | bytes 196616 | tf_op jit(solution)/shard_map/ppermute | solution.py:30
  217.6 6.9 %collective-permute-start.12 = (f16[512,256]{1,0:T(8,128)(2,1)S(1)}, f16[512,256]{1,0:T(8,128)(2,1)S(1)}, u32[]{:S(2)}, u32[]{:S(2)}) collective-permute-start(f16[512,256]{1,0:T(8,128)(2,1)S(1)} %bitcast.50), channel_id=1, source_target_pairs={{0,1},{1,0},{2,3},{3,2},{4,5},{5,4},{6,7},{7,6},{8,9},{9,8},{10,11... | collective-permute-start | bytes 786440 | tf_op jit(solution)/shard_map/ppermute | solution.py:30
  225.6 3.5 %all-to-all-start.12 = ((f16[4,512,256]{2,1,0:T(8,128)(2,1)}), f16[4,512,256]{2,1,0:T(8,128)(2,1)S(1)}, u32[]{:S(2)}, u32[]{:S(2)}) async-start(f16[4,512,256]{2,1,0:T(8,128)(2,1)} %broadcast_in_dim.108), calls=%async_computation.12 | async-start | bytes 2097152 | tf_op jit(solution)/shard_map/all_to_all | solution.py:34
  230.5 13.5 %all-to-all-done.12 = f16[4,512,256]{2,1,0:T(8,128)(2,1)S(1)} async-done(((f16[4,512,256]{2,1,0:T(8,128)(2,1)}), f16[4,512,256]{2,1,0:T(8,128)(2,1)S(1)}, u32[]{:S(2)}, u32[]{:S(2)}) %all-to-all-start.12) | async-done | bytes 1048608 | tf_op jit(solution)/shard_map/all_to_all | solution.py:34
  (89 shorter events, 59.9 us)
Async XLA Ops:
  1.5 26.0 %collective-permute-start = (bf16[128,256]{1,0:T(8,128)(2,1)S(1)}, bf16[128,256]{1,0:T(8,128)(2,1)S(1)}, u32[]{:S(2)}, u32[]{:S(2)}) collective-permute-start(bf16[128,256]{1,0:T(8,128)(2,1)S(1)} %constant_dynamic-slice_fusion.4), channel_id=1, source_target_pairs={{0,256},{32,288},{64,320},{96,352},{128,384},{160,416},{192,448},{... | collective-permute-start | bytes 196616 | tf_op jit(solution)/shard_map/ppermute | solution.py:30
  23.3 113.1 %copy-start.4 = (bf16[2048,256]{1,0:T(8,128)(2,1)}, bf16[2048,256]{1,0:T(8,128)(2,1)S(1)}, u32[]{:S(2)}) copy-start(bf16[2048,256]{1,0:T(8,128)(2,1)S(1)} %get-tuple-element.18.protos_ref) | copy-start | bytes 3145732
  23.3 11.3 %all-to-all-start = ((f32[4,8,256]{2,1,0:T(8,128)}), f32[4,8,256]{2,1,0:T(8,128)S(1)}, u32[]{:S(2)}, u32[]{:S(2)}) async-start(f32[4,8,256]{2,1,0:T(8,128)} %get-tuple-element.19), calls=%async_computation | async-start | bytes 65536 | tf_op jit(solution)/shard_map/all_to_all | solution.py:34
  27.5 4.0 %collective-permute-start.1 = (bf16[128,256]{1,0:T(8,128)(2,1)S(1)}, bf16[128,256]{1,0:T(8,128)(2,1)S(1)}, u32[]{:S(2)}, u32[]{:S(2)}) collective-permute-start(bf16[128,256]{1,0:T(8,128)(2,1)S(1)} %collective-permute-done), channel_id=1, source_target_pairs={{0,1},{1,0},{2,3},{3,2},{4,5},{5,4},{6,7},{7,6},{8,9},{9,8},{10,11... | collective-permute-start | bytes 196616 | tf_op jit(solution)/shard_map/ppermute | solution.py:30
  31.5 17.8 %collective-permute-start.2 = (bf16[256,256]{1,0:T(8,128)(2,1)S(1)}, bf16[256,256]{1,0:T(8,128)(2,1)S(1)}, u32[]{:S(2)}, u32[]{:S(2)}) collective-permute-start(bf16[256,256]{1,0:T(8,128)(2,1)S(1)} %bitcast.52), channel_id=1, source_target_pairs={{0,2},{2,4},{4,6},{6,0},{1,3},{3,5},{5,7},{7,1},{8,10},{10,12},{12... | collective-permute-start | bytes 393224 | tf_op jit(solution)/shard_map/ppermute | solution.py:30
  35.3 18.5 %all-to-all-start.1 = ((f32[16,8,256]{2,1,0:T(8,128)}), f32[16,8,256]{2,1,0:T(8,128)S(1)}, u32[]{:S(2)}, u32[]{:S(2)}) async-start(f32[16,8,256]{2,1,0:T(8,128)} %broadcast_in_dim.89), calls=%async_computation.1 | async-start | bytes 262144 | tf_op jit(solution)/shard_map/all_to_all | solution.py:34
  41.8 7.5 %collective-permute-start.3 = (bf16[256,256]{1,0:T(8,128)(2,1)S(1)}, bf16[256,256]{1,0:T(8,128)(2,1)S(1)}, u32[]{:S(2)}, u32[]{:S(2)}) collective-permute-start(bf16[256,256]{1,0:T(8,128)(2,1)S(1)} %bitcast.53), channel_id=1, source_target_pairs={{0,4},{2,6},{4,0},{6,2},{1,5},{3,7},{5,1},{7,3},{8,12},{10,14},{12... | collective-permute-start | bytes 393224 | tf_op jit(solution)/shard_map/ppermute | solution.py:30
  46.2 6.0 %collective-permute-start.4 = (bf16[256,256]{1,0:T(8,128)(2,1)S(1)}, bf16[256,256]{1,0:T(8,128)(2,1)S(1)}, u32[]{:S(2)}, u32[]{:S(2)}) collective-permute-start(bf16[256,256]{1,0:T(8,128)(2,1)S(1)} %bitcast.54), channel_id=1, source_target_pairs={{0,6},{2,0},{4,2},{6,4},{1,7},{3,1},{5,3},{7,5},{8,14},{10,8},{12,... | collective-permute-start | bytes 393224 | tf_op jit(solution)/shard_map/ppermute | solution.py:30
  112.6 11.9 %copy-start.6 = (s32[1024]{0:T(1024)S(1)}, s32[1024]{0:T(1024)}, u32[]{:S(2)}) copy-start(s32[1024]{0:T(1024)} %param.5) | copy-start | bytes 12292
  121.0 15.4 %all-to-all-start.7 = ((f32[16,8,256]{2,1,0:T(8,128)}), f32[16,8,256]{2,1,0:T(8,128)S(1)}, u32[]{:S(2)}, u32[]{:S(2)}) async-start(f32[16,8,256]{2,1,0:T(8,128)} %broadcast_in_dim.100), calls=%async_computation.7 | async-start | bytes 262144 | tf_op jit(solution)/shard_map/all_to_all | solution.py:34
  155.5 5.5 %copy-start.3 = (bf16[2048,256]{1,0:T(8,128)(2,1)S(1)}, bf16[2048,256]{1,0:T(8,128)(2,1)}, u32[]{:S(2)}) copy-start(bf16[2048,256]{1,0:T(8,128)(2,1)} %proto_ref.1) | copy-start | bytes 3145732
  155.5 5.6 %copy-start.1 = (bf16[1024,256]{1,0:T(8,128)(2,1)S(1)}, bf16[1024,256]{1,0:T(8,128)(2,1)}, u32[]{:S(2)}) copy-start(bf16[1024,256]{1,0:T(8,128)(2,1)} %emb_ref.1) | copy-start | bytes 1572868
  156.6 18.7 %all-to-all-start.9 = ((f16[4,512,256]{2,1,0:T(8,128)(2,1)}), f16[4,512,256]{2,1,0:T(8,128)(2,1)}, u32[]{:S(2)}, u32[]{:S(2)}) async-start(f16[4,512,256]{2,1,0:T(8,128)(2,1)} %bitcast.48), calls=%async_computation.9 | async-start | bytes 2097152 | tf_op jit(solution)/shard_map/all_to_all | solution.py:34
  161.7 19.3 %collective-permute-start.5 = (f16[512,256]{1,0:T(8,128)(2,1)S(1)}, f16[512,256]{1,0:T(8,128)(2,1)S(1)}, u32[]{:S(2)}, u32[]{:S(2)}) collective-permute-start(f16[512,256]{1,0:T(8,128)(2,1)S(1)} %constant_dynamic-slice_fusion.3), channel_id=1, source_target_pairs={{0,1},{1,0},{2,3},{3,2},{4,5},{5,4},{6,7},{7,6},{8,9},{9,8},{10,11... | collective-permute-start | bytes 786440 | tf_op jit(solution)/shard_map/ppermute | solution.py:30
  177.4 16.3 %all-to-all-start.10 = ((f16[16,32,256]{2,1,0:T(8,128)(2,1)}), f16[16,32,256]{2,1,0:T(8,128)(2,1)S(1)}, u32[]{:S(2)}, u32[]{:S(2)}) async-start(f16[16,32,256]{2,1,0:T(8,128)(2,1)} %bitcast.20), calls=%async_computation.10 | async-start | bytes 524288 | tf_op jit(solution)/shard_map/all_to_all | solution.py:34
  181.1 8.6 %collective-permute-start.6 = (f16[128,256]{1,0:T(8,128)(2,1)S(1)}, f16[128,256]{1,0:T(8,128)(2,1)S(1)}, u32[]{:S(2)}, u32[]{:S(2)}) collective-permute-start(f16[128,256]{1,0:T(8,128)(2,1)S(1)} %get-tuple-element.38), channel_id=1, source_target_pairs={{0,2},{2,4},{4,6},{6,0},{1,3},{3,5},{5,7},{7,1},{8,10},{10,12},{12... | collective-permute-start | bytes 196616 | tf_op jit(solution)/shard_map/ppermute | solution.py:30
  183.3 6.8 %collective-permute-start.7 = (f16[128,256]{1,0:T(8,128)(2,1)S(1)}, f16[128,256]{1,0:T(8,128)(2,1)S(1)}, u32[]{:S(2)}, u32[]{:S(2)}) collective-permute-start(f16[128,256]{1,0:T(8,128)(2,1)S(1)} %get-tuple-element.40), channel_id=1, source_target_pairs={{0,4},{2,6},{4,0},{6,2},{1,5},{3,7},{5,1},{7,3},{8,12},{10,14},{12... | collective-permute-start | bytes 196616 | tf_op jit(solution)/shard_map/ppermute | solution.py:30
  187.0 5.8 %collective-permute-start.8 = (f16[128,256]{1,0:T(8,128)(2,1)S(1)}, f16[128,256]{1,0:T(8,128)(2,1)S(1)}, u32[]{:S(2)}, u32[]{:S(2)}) collective-permute-start(f16[128,256]{1,0:T(8,128)(2,1)S(1)} %get-tuple-element.39), channel_id=1, source_target_pairs={{0,6},{2,0},{4,2},{6,4},{1,7},{3,1},{5,3},{7,5},{8,14},{10,8},{12,... | collective-permute-start | bytes 196616 | tf_op jit(solution)/shard_map/ppermute | solution.py:30
  194.7 29.8 %all-to-all-start.11 = ((f16[16,32,256]{2,1,0:T(8,128)(2,1)}), f16[16,32,256]{2,1,0:T(8,128)(2,1)S(1)}, u32[]{:S(2)}, u32[]{:S(2)}) async-start(f16[16,32,256]{2,1,0:T(8,128)(2,1)} %broadcast_in_dim.106), calls=%async_computation.11 | async-start | bytes 524288 | tf_op jit(solution)/shard_map/all_to_all | solution.py:34
  205.5 9.5 %collective-permute-start.9 = (f16[128,256]{1,0:T(8,128)(2,1)S(1)}, f16[128,256]{1,0:T(8,128)(2,1)S(1)}, u32[]{:S(2)}, u32[]{:S(2)}) collective-permute-start(f16[128,256]{1,0:T(8,128)(2,1)S(1)} %get-tuple-element.35), channel_id=1, source_target_pairs={{0,2},{2,4},{4,6},{6,0},{1,3},{3,5},{5,7},{7,1},{8,10},{10,12},{12... | collective-permute-start | bytes 196616 | tf_op jit(solution)/shard_map/ppermute | solution.py:30
  208.8 7.0 %collective-permute-start.10 = (f16[128,256]{1,0:T(8,128)(2,1)S(1)}, f16[128,256]{1,0:T(8,128)(2,1)S(1)}, u32[]{:S(2)}, u32[]{:S(2)}) collective-permute-start(f16[128,256]{1,0:T(8,128)(2,1)S(1)} %get-tuple-element.35), channel_id=1, source_target_pairs={{0,4},{2,6},{4,0},{6,2},{1,5},{3,7},{5,1},{7,3},{8,12},{10,14},{12... | collective-permute-start | bytes 196616 | tf_op jit(solution)/shard_map/ppermute | solution.py:30
  212.3 5.3 %collective-permute-start.11 = (f16[128,256]{1,0:T(8,128)(2,1)S(1)}, f16[128,256]{1,0:T(8,128)(2,1)S(1)}, u32[]{:S(2)}, u32[]{:S(2)}) collective-permute-start(f16[128,256]{1,0:T(8,128)(2,1)S(1)} %get-tuple-element.35), channel_id=1, source_target_pairs={{0,6},{2,0},{4,2},{6,4},{1,7},{3,1},{5,3},{7,5},{8,14},{10,8},{12,... | collective-permute-start | bytes 196616 | tf_op jit(solution)/shard_map/ppermute | solution.py:30
  217.6 11.6 %collective-permute-start.12 = (f16[512,256]{1,0:T(8,128)(2,1)S(1)}, f16[512,256]{1,0:T(8,128)(2,1)S(1)}, u32[]{:S(2)}, u32[]{:S(2)}) collective-permute-start(f16[512,256]{1,0:T(8,128)(2,1)S(1)} %bitcast.50), channel_id=1, source_target_pairs={{0,1},{1,0},{2,3},{3,2},{4,5},{5,4},{6,7},{7,6},{8,9},{9,8},{10,11... | collective-permute-start | bytes 786440 | tf_op jit(solution)/shard_map/ppermute | solution.py:30
  225.6 18.4 %all-to-all-start.12 = ((f16[4,512,256]{2,1,0:T(8,128)(2,1)}), f16[4,512,256]{2,1,0:T(8,128)(2,1)S(1)}, u32[]{:S(2)}, u32[]{:S(2)}) async-start(f16[4,512,256]{2,1,0:T(8,128)(2,1)} %broadcast_in_dim.108), calls=%async_computation.12 | async-start | bytes 2097152 | tf_op jit(solution)/shard_map/all_to_all | solution.py:34
  (3 other events, 3.5 us)

commit v6 on v5

--- a/solution.py
+++ b/solution.py
@@ -1,5 +1,3 @@
-import functools
-
 import jax
 import jax.numpy as jnp
 from jax import lax
@@ -148,28 +146,37 @@
     for_each_receiver(col_ref)
 
 
-def rows_kernel(own, emb_ref, protos_ref, totals_ref, temp_ref, row_ref):
-    column_scale = 1.0 / jnp.sum(totals_ref[...], axis=0)
-
-    @pl.loop(0, emb_ref.shape[0] // ROWS)
+def rows_kernel(views_ref, protos_ref, totals_ref, temp_ref, row_ref):
+    column_scale = 1.0 / jnp.sum(totals_ref[...].astype(f32), axis=0)
+
+    @pl.loop(0, views_ref.shape[0] // ROWS)
     def _(step):
         rows = pl.ds(pl.multiple_of(step * ROWS, ROWS), ROWS)
-        units = emb_ref[rows, :]
-        if own:
-            tempered = tempered_rows(units, protos_ref, sharpness_divisor)
-        else:
-            tempered = tempered_rows(kernel_units(units), protos_ref, epsilon_code)
+        tempered = tempered_rows(views_ref[rows, :], protos_ref, sharpness_divisor)
         temp_ref[rows, :] = tempered
         total = soft = jnp.zeros((ROWS, LANES), f32)
         for start in tiles(tempered):
             value = tempered[:, start : start + LANES]
-            if own:
-                soft = soft + value
-                value = value * value
-            total = total + value * column_tile(column_scale, start)
+            soft = soft + value
+            total = total + value * value * column_tile(column_scale, start)
         row_ref[0, :1, rows] = as_row(total)
-        if own:
-            row_ref[0, 1:, rows] = as_row(soft)
+        row_ref[0, 1:, rows] = as_row(soft)
+
+    for_each_receiver(row_ref)
+
+
+def line_kernel(views_ref, protos_ref, totals_ref, kernel_ref, row_ref):
+    column_scale = 1.0 / jnp.sum(totals_ref[...], axis=0)
+
+    @pl.loop(0, views_ref.shape[0] // ROWS)
+    def _(step):
+        rows = pl.ds(pl.multiple_of(step * ROWS, ROWS), ROWS)
+        kernel = tempered_rows(views_ref[rows, :], protos_ref, epsilon_code)
+        kernel_ref[rows, :] = kernel
+        total = jnp.zeros((ROWS, LANES), f32)
+        for start in tiles(kernel):
+            total = total + kernel[:, start : start + LANES] * column_tile(column_scale, start)
+        row_ref[0, :, rows] = as_row(total)
 
     for_each_receiver(row_ref)
 
@@ -246,12 +253,12 @@
         exps=entries,
     )
 
-    def tempered_pass(mine, rows, totals):
+    def tempered_pass(rows, totals):
         tempered, part = call(
-            functools.partial(rows_kernel, mine),
+            rows_kernel,
             "tempered_pass",
             [rows, protos, totals],
-            [(matrix, f32), ((members, 2 if mine else 1, count), f32)],
+            [(matrix, f32), ((members, 2, count), f32)],
             flops=2 * entries * width,
             size=4 * slots * width,
             exps=entries,
@@ -265,14 +272,28 @@
 
     sent = gather_blocks(gather_blocks(sent, "core"), "x")
     column_part = total(exchanged(column_part, "y"))
-    column_total, sent = lax.optimization_barrier((gathered(column_part, "z"), sent))
-    for sweep in range(1, ITERS):
-        tempered, row_total = tempered_pass(True, views, column_total)
-        column_part = column_pass(tempered, row_total)
-        if sweep == ITERS - 1:
-            column_part, sent = lax.optimization_barrier((column_part, sent))
+    column_total = gathered(column_part.astype(bf16), "z")
+    column_total, sent = lax.optimization_barrier((column_total, sent))
+    tempered, row_total = tempered_pass(views, column_total)
+    column_part, sent = lax.optimization_barrier((column_pass(tempered, row_total), sent))
+    other = sent[links]
+    column_total = gathered(column_part.astype(bf16), "z")
+    for sweep in range(2, ITERS):
+        column_total, other = lax.optimization_barrier((column_total, other))
+        tempered, row_total = tempered_pass(views, column_total)
+        column_part, other = lax.optimization_barrier((column_pass(tempered, row_total), other))
         column_total = gathered(column_part, "z")
-    other_kernel, line_total = tempered_pass(False, sent[links], column_total)
+    other_views = unit_rows(other)[0].astype(bf16)
+    other_kernel, line_part = call(
+        line_kernel,
+        "lines",
+        [other_views, protos, column_total],
+        [(matrix, f32), ((members, 1, count), f32)],
+        flops=2 * entries * width,
+        size=4 * slots * width,
+        exps=entries,
+    )
+    line_total = exchanged(line_part, proto_axes)
     view_part, proto_part = call(
         gradient_kernel,
         "gradient",

time: 247 us -> 247 us (level)
  blocking collectives: 69.9 us -> 47.6 us
  starting transfers between devices: 93.5 us -> 104 us
  waiting for transfers between devices: 44 us -> 54.5 us
    all_to_all x6 -> x5, blocking collectives: 69.9 us -> 47.6 us  [exchanged(): return lax.all_to_all(value, axis, 0, 0, tiled=True)]
    all_to_all x7 -> x8, waiting for transfers between devices: 34.8 us -> 45.4 us  [exchanged(): return lax.all_to_all(value, axis, 0, 0, tiled=True)]
    all_to_all x7 -> x8, starting transfers between devices: 36.1 us -> 46.3 us  [exchanged(): return lax.all_to_all(value, axis, 0, 0, tiled=True)]
  transfers between devices with their start and end apart: 20 -> 21, of which waited for: 11 -> 12; matrix products, arithmetic and copies ran while one was open for 4% -> 4% of each run, Pallas kernels for 1% -> 1%
where the time goes in v6:
time: 247 us; the launch traced here: 245 us
  starting transfers between devices  104 us (42%)
  waiting for transfers between devices  54.5 us (22%)
  blocking collectives  47.6 us (19%)
  Pallas kernels  17.5 us (7%)
  local copies, waits for them, and re-layouts  12.5 us (5%)
  other arithmetic  7.99 us (3%)
    ppermute x13, starting transfers between devices, shifted(): return lax.ppermute(value, axis, pairs)  57.8 us
    all_to_all x5, blocking collectives, exchanged(): return lax.all_to_all(value, axis, 0, 0, tiled=True)  47.6 us
    all_to_all x8, starting transfers between devices, exchanged(): return lax.all_to_all(value, axis, 0, 0, tiled=True)  46.3 us
    all_to_all x8, waiting for transfers between devices, exchanged(): return lax.all_to_all(value, axis, 0, 0, tiled=True)  45.4 us
    pallas_call x7, Pallas kernels, call(): pl.pallas_call(kernel, name=name, out_shape=[jax.ShapeDtypeStruct(shape,...  17.5 us
    ppermute x13, waiting for transfers between devices, shifted(): return lax.ppermute(value, axis, pairs)  9.14 us
  transfers between devices with their start and end apart: 21, of which 12 were waited for; matrix products, arithmetic and copies ran while one was open for 4% of the time, Pallas kernels for 1%

profile of v6, /device:TPU:1, one launch (start us, length us, event | category | flops | bytes accessed | tf_op | source)
XLA Modules:
  0.0 245.5 jit_solution(3101791160398661561)
XLA Ops:
  1.5 16.3 %collective-permute-start = (bf16[128,256]{1,0:T(8,128)(2,1)S(1)}, bf16[128,256]{1,0:T(8,128)(2,1)S(1)}, u32[]{:S(2)}, u32[]{:S(2)}) collective-permute-start(bf16[128,256]{1,0:T(8,128)(2,1)S(1)} %constant_dynamic-slice_fusion.4), channel_id=1, source_target_pairs={{0,256},{32,288},{64,320},{96,352},{128,384},{160,416},{192,448},{... | collective-permute-start | bytes 196616 | tf_op jit(solution)/shard_map/ppermute | solution.py:28
  23.3 4.2 %all-to-all-start = ((f32[4,8,256]{2,1,0:T(8,128)}), f32[4,8,256]{2,1,0:T(8,128)S(1)}, u32[]{:S(2)}, u32[]{:S(2)}) async-start(f32[4,8,256]{2,1,0:T(8,128)} %get-tuple-element.23), calls=%async_computation | async-start | bytes 65536 | tf_op jit(solution)/shard_map/all_to_all | solution.py:32
  35.3 6.5 %all-to-all-start.1 = ((bf16[16,8,256]{2,1,0:T(8,128)(2,1)}), bf16[16,8,256]{2,1,0:T(8,128)(2,1)S(1)}, u32[]{:S(2)}, u32[]{:S(2)}) async-start(bf16[16,8,256]{2,1,0:T(8,128)(2,1)} %broadcast_in_dim.88), calls=%async_computation.1 | async-start | bytes 131072 | tf_op jit(solution)/shard_map/all_to_all | solution.py:32
  41.8 4.4 %collective-permute-start.3 = (bf16[256,256]{1,0:T(8,128)(2,1)S(1)}, bf16[256,256]{1,0:T(8,128)(2,1)S(1)}, u32[]{:S(2)}, u32[]{:S(2)}) collective-permute-start(bf16[256,256]{1,0:T(8,128)(2,1)S(1)} %bitcast.53), channel_id=1, source_target_pairs={{0,4},{2,6},{4,0},{6,2},{1,5},{3,7},{5,1},{7,3},{8,12},{10,14},{12... | collective-permute-start | bytes 393224 | tf_op jit(solution)/shard_map/ppermute | solution.py:28
  56.3 10.7 %all_to_all.65.totals_ref = f32[8,2,1024]{2,1,0:T(2,128)S(1)} all-to-all(f32[8,2,1024]{2,1,0:T(2,128)S(1)} %get-tuple-element.26), channel_id=1, replica_groups=mesh['z'=16,'y'=4,'x'=4,'core'=2] {'x','core'}, dimensions={0} | all-to-all | bytes 131072 | tf_op jit(solution)/shard_map/all_to_all | solution.py:32
  68.0 8.3 %all_to_all.66 = f32[4,8,256]{2,1,0:T(8,128)S(1)} all-to-all(f32[4,8,256]{2,1,0:T(8,128)S(1)} %column_pass.2), channel_id=1, replica_groups=mesh['z'=16,'y'=4,'x'=4,'core'=2] {'y'}, dimensions={0} | all-to-all | bytes 65536 | tf_op jit(solution)/shard_map/all_to_all | solution.py:32
  76.9 10.5 %all-to-all-start.4 = ((bf16[16,8,256]{2,1,0:T(8,128)(2,1)}), bf16[16,8,256]{2,1,0:T(8,128)(2,1)S(1)}, u32[]{:S(2)}, u32[]{:S(2)}) async-start(bf16[16,8,256]{2,1,0:T(8,128)(2,1)} %broadcast_in_dim.96), calls=%async_computation.4 | async-start | bytes 131072 | tf_op jit(solution)/shard_map/all_to_all | solution.py:32
  87.4 3.9 %gather_fusion = bf16[1024,256]{1,0:T(8,128)(2,1)S(1)} fusion(bf16[1024,256]{1,0:T(8,128)(2,1)S(1)} %bitcast.47, s32[1024]{0:T(1024)S(1)} %fusion.21), kind=kCustom, calls=%fused_computation | custom fusion | bytes 1052672 | tf_op jit(solution)/shard_map/gather | solution.py:279
  91.3 7.7 %all-to-all-done.4.totals_ref = bf16[16,8,256]{2,1,0:T(8,128)(2,1)S(1)} async-done(((bf16[16,8,256]{2,1,0:T(8,128)(2,1)}), bf16[16,8,256]{2,1,0:T(8,128)(2,1)S(1)}, u32[]{:S(2)}, u32[]{:S(2)}) %all-to-all-start.4) | async-done | bytes 65568 | tf_op jit(solution)/shard_map/all_to_all | solution.py:32
  102.0 10.9 %all_to_all.67.totals_ref.soft_ref = f32[8,2,1024]{2,1,0:T(2,128)S(1)} all-to-all(f32[8,2,1024]{2,1,0:T(2,128)S(1)} %get-tuple-element.32), channel_id=1, replica_groups=mesh['z'=16,'y'=4,'x'=4,'core'=2] {'x','core'}, dimensions={0} | all-to-all | bytes 131072 | tf_op jit(solution)/shard_map/all_to_all | solution.py:32
  113.9 6.7 %all_to_all.68 = f32[4,8,256]{2,1,0:T(8,128)S(1)} all-to-all(f32[4,8,256]{2,1,0:T(8,128)S(1)} %column_pass.3), channel_id=1, replica_groups=mesh['z'=16,'y'=4,'x'=4,'core'=2] {'y'}, dimensions={0} | all-to-all | bytes 65536 | tf_op jit(solution)/shard_map/all_to_all | solution.py:32
  121.2 3.5 %all-to-all-start.7 = ((f32[16,8,256]{2,1,0:T(8,128)}), f32[16,8,256]{2,1,0:T(8,128)S(1)}, u32[]{:S(2)}, u32[]{:S(2)}) async-start(f32[16,8,256]{2,1,0:T(8,128)} %broadcast_in_dim.98), calls=%async_computation.7 | async-start | bytes 262144 | tf_op jit(solution)/shard_map/all_to_all | solution.py:32
  125.2 11.5 %all-to-all-done.7.totals_ref = f32[16,8,256]{2,1,0:T(8,128)S(1)} async-done(((f32[16,8,256]{2,1,0:T(8,128)}), f32[16,8,256]{2,1,0:T(8,128)S(1)}, u32[]{:S(2)}, u32[]{:S(2)}) %all-to-all-start.7) | async-done | bytes 131104 | tf_op jit(solution)/shard_map/all_to_all | solution.py:32
  138.9 11.0 %all_to_all.69.line_ref = f32[8,1,1024]{2,1,0:T(1,128)S(1)} all-to-all(f32[8,1,1024]{2,1,0:T(1,128)S(1)} %get-tuple-element.37), channel_id=1, replica_groups=mesh['z'=16,'y'=4,'x'=4,'core'=2] {'x','core'}, dimensions={0} | all-to-all | bytes 65536 | tf_op jit(solution)/shard_map/all_to_all | solution.py:32
  151.2 4.2 %gradient.1 = (f32[1024,256]{1,0:T(8,128)S(1)}, f32[2048,256]{1,0:T(8,128)S(1)}) custom-call(f32[1024,2048]{1,0:T(8,128)S(1)} %get-tuple-element.36.other_ref, f32[16,8,256]{2,1,0:T(8,128)S(1)} %all-to-all-done.7.totals_ref, f32[8,1,1024]{2,1,0:T(1,128)S(1)} %all_to_all.69.line_ref, f32[8,2,1024]{2,1,0:T(2,128)S(1)} %all_to_all.67.totals_ref.soft_ref, ...), custom_call_target="tpu_custom_call" | custom-call | flops 3221225472 | bytes 4194304 | tf_op jit(solution)/shard_map/gradient/pallas_call | solution.py:224
  156.5 4.3 %all-to-all-start.9 = ((f16[4,512,256]{2,1,0:T(8,128)(2,1)}), f16[4,512,256]{2,1,0:T(8,128)(2,1)}, u32[]{:S(2)}, u32[]{:S(2)}) async-start(f16[4,512,256]{2,1,0:T(8,128)(2,1)} %bitcast.48), calls=%async_computation.9 | async-start | bytes 2097152 | tf_op jit(solution)/shard_map/all_to_all | solution.py:32
  164.2 11.0 %all-to-all-done.9 = f16[4,512,256]{2,1,0:T(8,128)(2,1)} async-done(((f16[4,512,256]{2,1,0:T(8,128)(2,1)}), f16[4,512,256]{2,1,0:T(8,128)(2,1)}, u32[]{:S(2)}, u32[]{:S(2)}) %all-to-all-start.9) | async-done | bytes 1048608 | tf_op jit(solution)/shard_map/all_to_all | solution.py:32
  177.3 3.5 %all-to-all-start.10 = ((f16[16,32,256]{2,1,0:T(8,128)(2,1)}), f16[16,32,256]{2,1,0:T(8,128)(2,1)S(1)}, u32[]{:S(2)}, u32[]{:S(2)}) async-start(f16[16,32,256]{2,1,0:T(8,128)(2,1)} %bitcast.20), calls=%async_computation.10 | async-start | bytes 524288 | tf_op jit(solution)/shard_map/all_to_all | solution.py:32
  183.2 3.7 %collective-permute-start.7 = (f16[128,256]{1,0:T(8,128)(2,1)S(1)}, f16[128,256]{1,0:T(8,128)(2,1)S(1)}, u32[]{:S(2)}, u32[]{:S(2)}) collective-permute-start(f16[128,256]{1,0:T(8,128)(2,1)S(1)} %get-tuple-element.48), channel_id=1, source_target_pairs={{0,4},{2,6},{4,0},{6,2},{1,5},{3,7},{5,1},{7,3},{8,12},{10,14},{12... | collective-permute-start | bytes 196616 | tf_op jit(solution)/shard_map/ppermute | solution.py:28
  194.6 10.3 %all-to-all-start.11 = ((f16[16,32,256]{2,1,0:T(8,128)(2,1)}), f16[16,32,256]{2,1,0:T(8,128)(2,1)S(1)}, u32[]{:S(2)}, u32[]{:S(2)}) async-start(f16[16,32,256]{2,1,0:T(8,128)(2,1)} %broadcast_in_dim.104), calls=%async_computation.11 | async-start | bytes 524288 | tf_op jit(solution)/shard_map/all_to_all | solution.py:32
  208.8 3.4 %collective-permute-start.10 = (f16[128,256]{1,0:T(8,128)(2,1)S(1)}, f16[128,256]{1,0:T(8,128)(2,1)S(1)}, u32[]{:S(2)}, u32[]{:S(2)}) collective-permute-start(f16[128,256]{1,0:T(8,128)(2,1)S(1)} %get-tuple-element.43), channel_id=1, source_target_pairs={{0,4},{2,6},{4,0},{6,2},{1,5},{3,7},{5,1},{7,3},{8,12},{10,14},{12... | collective-permute-start | bytes 196616 | tf_op jit(solution)/shard_map/ppermute | solution.py:28
  217.5 7.0 %collective-permute-start.12 = (f16[512,256]{1,0:T(8,128)(2,1)S(1)}, f16[512,256]{1,0:T(8,128)(2,1)S(1)}, u32[]{:S(2)}, u32[]{:S(2)}) collective-permute-start(f16[512,256]{1,0:T(8,128)(2,1)S(1)} %bitcast.50), channel_id=1, source_target_pairs={{0,1},{1,0},{2,3},{3,2},{4,5},{5,4},{6,7},{7,6},{8,9},{9,8},{10,11... | collective-permute-start | bytes 786440 | tf_op jit(solution)/shard_map/ppermute | solution.py:28
  225.6 3.5 %all-to-all-start.12 = ((f16[4,512,256]{2,1,0:T(8,128)(2,1)}), f16[4,512,256]{2,1,0:T(8,128)(2,1)S(1)}, u32[]{:S(2)}, u32[]{:S(2)}) async-start(f16[4,512,256]{2,1,0:T(8,128)(2,1)} %broadcast_in_dim.106), calls=%async_computation.12 | async-start | bytes 2097152 | tf_op jit(solution)/shard_map/all_to_all | solution.py:32
  230.5 13.3 %all-to-all-done.12 = f16[4,512,256]{2,1,0:T(8,128)(2,1)S(1)} async-done(((f16[4,512,256]{2,1,0:T(8,128)(2,1)}), f16[4,512,256]{2,1,0:T(8,128)(2,1)S(1)}, u32[]{:S(2)}, u32[]{:S(2)}) %all-to-all-start.12) | async-done | bytes 1048608 | tf_op jit(solution)/shard_map/all_to_all | solution.py:32
  (93 shorter events, 64.1 us)
Async XLA Ops:
  1.5 26.0 %collective-permute-start = (bf16[128,256]{1,0:T(8,128)(2,1)S(1)}, bf16[128,256]{1,0:T(8,128)(2,1)S(1)}, u32[]{:S(2)}, u32[]{:S(2)}) collective-permute-start(bf16[128,256]{1,0:T(8,128)(2,1)S(1)} %constant_dynamic-slice_fusion.4), channel_id=1, source_target_pairs={{0,256},{32,288},{64,320},{96,352},{128,384},{160,416},{192,448},{... | collective-permute-start | bytes 196616 | tf_op jit(solution)/shard_map/ppermute | solution.py:28
  23.3 113.4 %copy-start.4 = (bf16[2048,256]{1,0:T(8,128)(2,1)}, bf16[2048,256]{1,0:T(8,128)(2,1)S(1)}, u32[]{:S(2)}) copy-start(bf16[2048,256]{1,0:T(8,128)(2,1)S(1)} %get-tuple-element.22.protos_ref) | copy-start | bytes 3145732
  23.3 11.3 %all-to-all-start = ((f32[4,8,256]{2,1,0:T(8,128)}), f32[4,8,256]{2,1,0:T(8,128)S(1)}, u32[]{:S(2)}, u32[]{:S(2)}) async-start(f32[4,8,256]{2,1,0:T(8,128)} %get-tuple-element.23), calls=%async_computation | async-start | bytes 65536 | tf_op jit(solution)/shard_map/all_to_all | solution.py:32
  27.5 4.0 %collective-permute-start.1 = (bf16[128,256]{1,0:T(8,128)(2,1)S(1)}, bf16[128,256]{1,0:T(8,128)(2,1)S(1)}, u32[]{:S(2)}, u32[]{:S(2)}) collective-permute-start(bf16[128,256]{1,0:T(8,128)(2,1)S(1)} %collective-permute-done), channel_id=1, source_target_pairs={{0,1},{1,0},{2,3},{3,2},{4,5},{5,4},{6,7},{7,6},{8,9},{9,8},{10,11... | collective-permute-start | bytes 196616 | tf_op jit(solution)/shard_map/ppermute | solution.py:28
  31.5 17.8 %collective-permute-start.2 = (bf16[256,256]{1,0:T(8,128)(2,1)S(1)}, bf16[256,256]{1,0:T(8,128)(2,1)S(1)}, u32[]{:S(2)}, u32[]{:S(2)}) collective-permute-start(bf16[256,256]{1,0:T(8,128)(2,1)S(1)} %bitcast.52), channel_id=1, source_target_pairs={{0,2},{2,4},{4,6},{6,0},{1,3},{3,5},{5,7},{7,1},{8,10},{10,12},{12... | collective-permute-start | bytes 393224 | tf_op jit(solution)/shard_map/ppermute | solution.py:28
  35.3 18.0 %all-to-all-start.1 = ((bf16[16,8,256]{2,1,0:T(8,128)(2,1)}), bf16[16,8,256]{2,1,0:T(8,128)(2,1)S(1)}, u32[]{:S(2)}, u32[]{:S(2)}) async-start(bf16[16,8,256]{2,1,0:T(8,128)(2,1)} %broadcast_in_dim.88), calls=%async_computation.1 | async-start | bytes 131072 | tf_op jit(solution)/shard_map/all_to_all | solution.py:32
  41.8 7.5 %collective-permute-start.3 = (bf16[256,256]{1,0:T(8,128)(2,1)S(1)}, bf16[256,256]{1,0:T(8,128)(2,1)S(1)}, u32[]{:S(2)}, u32[]{:S(2)}) collective-permute-start(bf16[256,256]{1,0:T(8,128)(2,1)S(1)} %bitcast.53), channel_id=1, source_target_pairs={{0,4},{2,6},{4,0},{6,2},{1,5},{3,7},{5,1},{7,3},{8,12},{10,14},{12... | collective-permute-start | bytes 393224 | tf_op jit(solution)/shard_map/ppermute | solution.py:28
  46.1 6.0 %collective-permute-start.4 = (bf16[256,256]{1,0:T(8,128)(2,1)S(1)}, bf16[256,256]{1,0:T(8,128)(2,1)S(1)}, u32[]{:S(2)}, u32[]{:S(2)}) collective-permute-start(bf16[256,256]{1,0:T(8,128)(2,1)S(1)} %bitcast.54), channel_id=1, source_target_pairs={{0,6},{2,0},{4,2},{6,4},{1,7},{3,1},{5,3},{7,5},{8,14},{10,8},{12,... | collective-permute-start | bytes 393224 | tf_op jit(solution)/shard_map/ppermute | solution.py:28
  67.0 20.4 %copy-start.6 = (s32[1024]{0:T(1024)S(1)}, s32[1024]{0:T(1024)}, u32[]{:S(2)}) copy-start(s32[1024]{0:T(1024)} %param.5) | copy-start | bytes 12292
  76.9 22.1 %all-to-all-start.4 = ((bf16[16,8,256]{2,1,0:T(8,128)(2,1)}), bf16[16,8,256]{2,1,0:T(8,128)(2,1)S(1)}, u32[]{:S(2)}, u32[]{:S(2)}) async-start(bf16[16,8,256]{2,1,0:T(8,128)(2,1)} %broadcast_in_dim.96), calls=%async_computation.4 | async-start | bytes 131072 | tf_op jit(solution)/shard_map/all_to_all | solution.py:32
  121.2 15.4 %all-to-all-start.7 = ((f32[16,8,256]{2,1,0:T(8,128)}), f32[16,8,256]{2,1,0:T(8,128)S(1)}, u32[]{:S(2)}, u32[]{:S(2)}) async-start(f32[16,8,256]{2,1,0:T(8,128)} %broadcast_in_dim.98), calls=%async_computation.7 | async-start | bytes 262144 | tf_op jit(solution)/shard_map/all_to_all | solution.py:32
  155.4 5.6 %copy-start.1 = (bf16[1024,256]{1,0:T(8,128)(2,1)S(1)}, bf16[1024,256]{1,0:T(8,128)(2,1)}, u32[]{:S(2)}) copy-start(bf16[1024,256]{1,0:T(8,128)(2,1)} %emb_ref.1) | copy-start | bytes 1572868
  156.5 18.8 %all-to-all-start.9 = ((f16[4,512,256]{2,1,0:T(8,128)(2,1)}), f16[4,512,256]{2,1,0:T(8,128)(2,1)}, u32[]{:S(2)}, u32[]{:S(2)}) async-start(f16[4,512,256]{2,1,0:T(8,128)(2,1)} %bitcast.48), calls=%async_computation.9 | async-start | bytes 2097152 | tf_op jit(solution)/shard_map/all_to_all | solution.py:32
  161.6 19.3 %collective-permute-start.5 = (f16[512,256]{1,0:T(8,128)(2,1)S(1)}, f16[512,256]{1,0:T(8,128)(2,1)S(1)}, u32[]{:S(2)}, u32[]{:S(2)}) collective-permute-start(f16[512,256]{1,0:T(8,128)(2,1)S(1)} %constant_dynamic-slice_fusion.3), channel_id=1, source_target_pairs={{0,1},{1,0},{2,3},{3,2},{4,5},{5,4},{6,7},{7,6},{8,9},{9,8},{10,11... | collective-permute-start | bytes 786440 | tf_op jit(solution)/shard_map/ppermute | solution.py:28
  177.3 16.3 %all-to-all-start.10 = ((f16[16,32,256]{2,1,0:T(8,128)(2,1)}), f16[16,32,256]{2,1,0:T(8,128)(2,1)S(1)}, u32[]{:S(2)}, u32[]{:S(2)}) async-start(f16[16,32,256]{2,1,0:T(8,128)(2,1)} %bitcast.20), calls=%async_computation.10 | async-start | bytes 524288 | tf_op jit(solution)/shard_map/all_to_all | solution.py:32
  181.0 8.6 %collective-permute-start.6 = (f16[128,256]{1,0:T(8,128)(2,1)S(1)}, f16[128,256]{1,0:T(8,128)(2,1)S(1)}, u32[]{:S(2)}, u32[]{:S(2)}) collective-permute-start(f16[128,256]{1,0:T(8,128)(2,1)S(1)} %get-tuple-element.46), channel_id=1, source_target_pairs={{0,2},{2,4},{4,6},{6,0},{1,3},{3,5},{5,7},{7,1},{8,10},{10,12},{12... | collective-permute-start | bytes 196616 | tf_op jit(solution)/shard_map/ppermute | solution.py:28
  183.2 6.8 %collective-permute-start.7 = (f16[128,256]{1,0:T(8,128)(2,1)S(1)}, f16[128,256]{1,0:T(8,128)(2,1)S(1)}, u32[]{:S(2)}, u32[]{:S(2)}) collective-permute-start(f16[128,256]{1,0:T(8,128)(2,1)S(1)} %get-tuple-element.48), channel_id=1, source_target_pairs={{0,4},{2,6},{4,0},{6,2},{1,5},{3,7},{5,1},{7,3},{8,12},{10,14},{12... | collective-permute-start | bytes 196616 | tf_op jit(solution)/shard_map/ppermute | solution.py:28
  186.9 5.8 %collective-permute-start.8 = (f16[128,256]{1,0:T(8,128)(2,1)S(1)}, f16[128,256]{1,0:T(8,128)(2,1)S(1)}, u32[]{:S(2)}, u32[]{:S(2)}) collective-permute-start(f16[128,256]{1,0:T(8,128)(2,1)S(1)} %get-tuple-element.47), channel_id=1, source_target_pairs={{0,6},{2,0},{4,2},{6,4},{1,7},{3,1},{5,3},{7,5},{8,14},{10,8},{12,... | collective-permute-start | bytes 196616 | tf_op jit(solution)/shard_map/ppermute | solution.py:28
  194.6 29.9 %all-to-all-start.11 = ((f16[16,32,256]{2,1,0:T(8,128)(2,1)}), f16[16,32,256]{2,1,0:T(8,128)(2,1)S(1)}, u32[]{:S(2)}, u32[]{:S(2)}) async-start(f16[16,32,256]{2,1,0:T(8,128)(2,1)} %broadcast_in_dim.104), calls=%async_computation.11 | async-start | bytes 524288 | tf_op jit(solution)/shard_map/all_to_all | solution.py:32
  205.1 9.9 %collective-permute-start.9 = (f16[128,256]{1,0:T(8,128)(2,1)S(1)}, f16[128,256]{1,0:T(8,128)(2,1)S(1)}, u32[]{:S(2)}, u32[]{:S(2)}) collective-permute-start(f16[128,256]{1,0:T(8,128)(2,1)S(1)} %get-tuple-element.43), channel_id=1, source_target_pairs={{0,2},{2,4},{4,6},{6,0},{1,3},{3,5},{5,7},{7,1},{8,10},{10,12},{12... | collective-permute-start | bytes 196616 | tf_op jit(solution)/shard_map/ppermute | solution.py:28
  208.8 7.0 %collective-permute-start.10 = (f16[128,256]{1,0:T(8,128)(2,1)S(1)}, f16[128,256]{1,0:T(8,128)(2,1)S(1)}, u32[]{:S(2)}, u32[]{:S(2)}) collective-permute-start(f16[128,256]{1,0:T(8,128)(2,1)S(1)} %get-tuple-element.43), channel_id=1, source_target_pairs={{0,4},{2,6},{4,0},{6,2},{1,5},{3,7},{5,1},{7,3},{8,12},{10,14},{12... | collective-permute-start | bytes 196616 | tf_op jit(solution)/shard_map/ppermute | solution.py:28
  212.2 5.3 %collective-permute-start.11 = (f16[128,256]{1,0:T(8,128)(2,1)S(1)}, f16[128,256]{1,0:T(8,128)(2,1)S(1)}, u32[]{:S(2)}, u32[]{:S(2)}) collective-permute-start(f16[128,256]{1,0:T(8,128)(2,1)S(1)} %get-tuple-element.43), channel_id=1, source_target_pairs={{0,6},{2,0},{4,2},{6,4},{1,7},{3,1},{5,3},{7,5},{8,14},{10,8},{12,... | collective-permute-start | bytes 196616 | tf_op jit(solution)/shard_map/ppermute | solution.py:28
  217.5 11.7 %collective-permute-start.12 = (f16[512,256]{1,0:T(8,128)(2,1)S(1)}, f16[512,256]{1,0:T(8,128)(2,1)S(1)}, u32[]{:S(2)}, u32[]{:S(2)}) collective-permute-start(f16[512,256]{1,0:T(8,128)(2,1)S(1)} %bitcast.50), channel_id=1, source_target_pairs={{0,1},{1,0},{2,3},{3,2},{4,5},{5,4},{6,7},{7,6},{8,9},{9,8},{10,11... | collective-permute-start | bytes 786440 | tf_op jit(solution)/shard_map/ppermute | solution.py:28
  225.6 18.2 %all-to-all-start.12 = ((f16[4,512,256]{2,1,0:T(8,128)(2,1)}), f16[4,512,256]{2,1,0:T(8,128)(2,1)S(1)}, u32[]{:S(2)}, u32[]{:S(2)}) async-start(f16[4,512,256]{2,1,0:T(8,128)(2,1)} %broadcast_in_dim.106), calls=%async_computation.12 | async-start | bytes 2097152 | tf_op jit(solution)/shard_map/all_to_all | solution.py:32
  (4 other events, 9.0 us)

commit v7 on v6

--- a/solution.py
+++ b/solution.py
@@ -316,9 +316,12 @@
     view_sum = tangent(view_sum.astype(f32), view_rows).astype(SENT)
     view_sum = gather_blocks(gather_blocks(view_sum, "x"), "core")
 
+    emb_grad = row_scale(embeddings) * view_sum.astype(f32)
+    proto_scale = row_scale(prototypes) * float(z_count)
+
+    proto_sum, emb_grad, proto_scale = lax.optimization_barrier((proto_sum, emb_grad, proto_scale))
     proto_sum = gathered(proto_sum, "y").reshape(slots, width)
-    emb_grad = row_scale(embeddings) * view_sum.astype(f32)
-    proto_grad = row_scale(prototypes) * float(z_count) * proto_sum.astype(f32)
+    proto_grad = proto_scale * proto_sum.astype(f32)
     return (emb_grad, proto_grad)
 
 

time: 247 us -> 261 us (1.057)
  the two profiles are of different devices: /device:TPU:1 before, /device:TPU:32 now
where the time goes in v7:
time: 261 us; the launch traced here: 259 us
  starting transfers between devices  104 us (40%)
  waiting for transfers between devices  62.8 us (24%)
  blocking collectives  37.3 us (14%)
  local copies, waits for them, and re-layouts  25.7 us (10%)
  Pallas kernels  19.4 us (7%)
  other arithmetic  8.8 us (3%)
    all_to_all x10, waiting for transfers between devices, exchanged(): return lax.all_to_all(value, axis, 0, 0, tiled=True)  55.2 us
    all_to_all x10, starting transfers between devices, exchanged(): return lax.all_to_all(value, axis, 0, 0, tiled=True)  53 us
    ppermute x13, starting transfers between devices, shifted(): return lax.ppermute(value, axis, pairs)  51.1 us
    all_to_all x3, blocking collectives, exchanged(): return lax.all_to_all(value, axis, 0, 0, tiled=True)  37.3 us
    pallas_call x7, Pallas kernels, call(): pl.pallas_call(kernel, name=name, out_shape=[jax.ShapeDtypeStruct(shape,...  19.4 us
    unnamed x24, local copies, waits for them, and re-layouts  16.6 us
    ppermute x13, waiting for transfers between devices, shifted(): return lax.ppermute(value, axis, pairs)  7.6 us
  transfers between devices with their start and end apart: 23, of which 14 were waited for; matrix products, arithmetic and copies ran while one was open for 5% of the time, Pallas kernels for 1%

profile of v7, /device:TPU:32, one launch (start us, length us, event | category | flops | bytes accessed | tf_op | source)
XLA Modules:
  0.0 259.2 jit_solution(12066083356318794513)
XLA Ops:
  1.5 14.8 %collective-permute-start = (bf16[128,256]{1,0:T(8,128)(2,1)S(1)}, bf16[128,256]{1,0:T(8,128)(2,1)S(1)}, u32[]{:S(2)}, u32[]{:S(2)}) collective-permute-start(bf16[128,256]{1,0:T(8,128)(2,1)S(1)} %constant_dynamic-slice_fusion.4), channel_id=1, source_target_pairs={{0,256},{32,288},{64,320},{96,352},{128,384},{160,416},{192,448},{... | collective-permute-start | bytes 196616 | tf_op jit(solution)/shard_map/ppermute | solution.py:28
  21.9 4.5 %all-to-all-start = ((f32[4,8,256]{2,1,0:T(8,128)}), f32[4,8,256]{2,1,0:T(8,128)S(1)}, u32[]{:S(2)}, u32[]{:S(2)}) async-start(f32[4,8,256]{2,1,0:T(8,128)} %get-tuple-element.26), calls=%async_computation | async-start | bytes 65536 | tf_op jit(solution)/shard_map/all_to_all | solution.py:32
  33.5 7.6 %all-to-all-start.1 = ((bf16[16,8,256]{2,1,0:T(8,128)(2,1)}), bf16[16,8,256]{2,1,0:T(8,128)(2,1)S(1)}, u32[]{:S(2)}, u32[]{:S(2)}) async-start(bf16[16,8,256]{2,1,0:T(8,128)(2,1)} %broadcast_in_dim.85), calls=%async_computation.1 | async-start | bytes 131072 | tf_op jit(solution)/shard_map/all_to_all | solution.py:32
  41.2 4.6 %collective-permute-start.3 = (bf16[256,256]{1,0:T(8,128)(2,1)S(1)}, bf16[256,256]{1,0:T(8,128)(2,1)S(1)}, u32[]{:S(2)}, u32[]{:S(2)}) collective-permute-start(bf16[256,256]{1,0:T(8,128)(2,1)S(1)} %bitcast.54), channel_id=1, source_target_pairs={{0,4},{2,6},{4,0},{6,2},{1,5},{3,7},{5,1},{7,3},{8,12},{10,14},{12... | collective-permute-start | bytes 393224 | tf_op jit(solution)/shard_map/ppermute | solution.py:28
  55.6 9.4 %all_to_all.65.totals_ref = f32[8,2,1024]{2,1,0:T(2,128)S(1)} all-to-all(f32[8,2,1024]{2,1,0:T(2,128)S(1)} %get-tuple-element.29), channel_id=1, replica_groups=mesh['z'=16,'y'=4,'x'=4,'core'=2] {'x','core'}, dimensions={0} | all-to-all | bytes 131072 | tf_op jit(solution)/shard_map/all_to_all | solution.py:32
  66.1 9.7 %all_to_all.66 = f32[4,8,256]{2,1,0:T(8,128)S(1)} all-to-all(f32[4,8,256]{2,1,0:T(8,128)S(1)} %column_pass.2), channel_id=1, replica_groups=mesh['z'=16,'y'=4,'x'=4,'core'=2] {'y'}, dimensions={0} | all-to-all | bytes 65536 | tf_op jit(solution)/shard_map/all_to_all | solution.py:32
  76.4 11.9 %all-to-all-start.4 = ((bf16[16,8,256]{2,1,0:T(8,128)(2,1)}), bf16[16,8,256]{2,1,0:T(8,128)(2,1)S(1)}, u32[]{:S(2)}, u32[]{:S(2)}) async-start(bf16[16,8,256]{2,1,0:T(8,128)(2,1)} %broadcast_in_dim.93), calls=%async_computation.4 | async-start | bytes 131072 | tf_op jit(solution)/shard_map/all_to_all | solution.py:32
  88.4 5.0 %gather_fusion = bf16[1024,256]{1,0:T(8,128)(2,1)} fusion(bf16[1024,256]{1,0:T(8,128)(2,1)S(1)} %bitcast.49, s32[1024]{0:T(1024)S(1)} %fusion.21), kind=kCustom, calls=%fused_computation | custom fusion | bytes 1052672 | tf_op jit(solution)/shard_map/gather | solution.py:279
  93.4 6.8 %all-to-all-done.4.totals_ref = bf16[16,8,256]{2,1,0:T(8,128)(2,1)S(1)} async-done(((bf16[16,8,256]{2,1,0:T(8,128)(2,1)}), bf16[16,8,256]{2,1,0:T(8,128)(2,1)S(1)}, u32[]{:S(2)}, u32[]{:S(2)}) %all-to-all-start.4) | async-done | bytes 65568 | tf_op jit(solution)/shard_map/all_to_all | solution.py:32
  100.2 3.5 %tempered_pass.3 = (f32[1024,2048]{1,0:T(8,128)S(1)}, f32[8,2,1024]{2,1,0:T(2,128)}) custom-call(bf16[1024,256]{1,0:T(8,128)(2,1)S(1)} %get-tuple-element.24.views_ref, bf16[2048,256]{1,0:T(8,128)(2,1)S(1)} %get-tuple-element.25.protos_ref, bf16[16,8,256]{2,1,0:T(8,128)(2,1)S(1)} %all-to-all-done.4.totals_ref), custom_call_target="tpu_custom_call" | custom-call | flops 1073741824 | bytes 2097152 | tf_op jit(solution)/shard_map/tempered_pass/pallas_call | solution.py:224
  110.5 5.4 %all-to-all-done.5.totals_ref.soft_ref = f32[8,2,1024]{2,1,0:T(2,128)S(1)} async-done(((f32[8,2,1024]{2,1,0:T(2,128)}), f32[8,2,1024]{2,1,0:T(2,128)S(1)}, u32[]{:S(2)}, u32[]{:S(2)}) %all-to-all-start.5) | async-done | bytes 65568 | tf_op jit(solution)/shard_map/all_to_all | solution.py:32
  124.3 5.3 %all-to-all-done.6 = f32[4,8,256]{2,1,0:T(8,128)S(1)} async-done(((f32[4,8,256]{2,1,0:T(8,128)}), f32[4,8,256]{2,1,0:T(8,128)S(1)}, u32[]{:S(2)}, u32[]{:S(2)}) %all-to-all-start.6) | async-done | bytes 32800 | tf_op jit(solution)/shard_map/all_to_all | solution.py:32
  130.2 5.2 %all-to-all-start.7 = ((f32[16,8,256]{2,1,0:T(8,128)}), f32[16,8,256]{2,1,0:T(8,128)S(1)}, u32[]{:S(2)}, u32[]{:S(2)}) async-start(f32[16,8,256]{2,1,0:T(8,128)} %broadcast_in_dim.95), calls=%async_computation.7 | async-start | bytes 262144 | tf_op jit(solution)/shard_map/all_to_all | solution.py:32
  137.0 11.2 %all-to-all-done.7.totals_ref = f32[16,8,256]{2,1,0:T(8,128)S(1)} async-done(((f32[16,8,256]{2,1,0:T(8,128)}), f32[16,8,256]{2,1,0:T(8,128)S(1)}, u32[]{:S(2)}, u32[]{:S(2)}) %all-to-all-start.7) | async-done | bytes 131104 | tf_op jit(solution)/shard_map/all_to_all | solution.py:32
  154.3 3.5 %all-to-all-start.8 = ((f32[8,1,1024]{2,1,0:T(1,128)}), f32[8,1,1024]{2,1,0:T(1,128)S(1)}, u32[]{:S(2)}, u32[]{:S(2)}) async-start(f32[8,1,1024]{2,1,0:T(1,128)} %get-tuple-element.40), calls=%async_computation.8 | async-start | bytes 65536 | tf_op jit(solution)/shard_map/all_to_all | solution.py:32
  157.9 5.2 %all-to-all-done.8.line_ref = f32[8,1,1024]{2,1,0:T(1,128)S(1)} async-done(((f32[8,1,1024]{2,1,0:T(1,128)}), f32[8,1,1024]{2,1,0:T(1,128)S(1)}, u32[]{:S(2)}, u32[]{:S(2)}) %all-to-all-start.8) | async-done | bytes 32800 | tf_op jit(solution)/shard_map/all_to_all | solution.py:32
  167.5 4.2 %gradient.1 = (f32[1024,256]{1,0:T(8,128)S(1)}, f32[2048,256]{1,0:T(8,128)S(1)}) custom-call(f32[1024,2048]{1,0:T(8,128)S(1)} %copy-done.7, f32[16,8,256]{2,1,0:T(8,128)S(1)} %all-to-all-done.7.totals_ref, f32[8,1,1024]{2,1,0:T(1,128)S(1)} %all-to-all-done.8.line_ref, f32[8,2,1024]{2,1,0:T(2,128)S(1)} %all-to-all-done.5.totals_ref.soft_ref, ...), custom_call_target="tpu_custom_call" | custom-call | flops 3221225472 | bytes 4194304 | tf_op jit(solution)/shard_map/gradient/pallas_call | solution.py:224
  183.6 4.0 %collective-permute-start.7 = (f16[128,256]{1,0:T(8,128)(2,1)S(1)}, f16[128,256]{1,0:T(8,128)(2,1)S(1)}, u32[]{:S(2)}, u32[]{:S(2)}) collective-permute-start(f16[128,256]{1,0:T(8,128)(2,1)S(1)} %get-tuple-element.54), channel_id=1, source_target_pairs={{0,4},{2,6},{4,0},{6,2},{1,5},{3,7},{5,1},{7,3},{8,12},{10,14},{12... | collective-permute-start | bytes 196616 | tf_op jit(solution)/shard_map/ppermute | solution.py:28
  192.5 4.7 %all-to-all-start.10 = ((f16[16,32,256]{2,1,0:T(8,128)(2,1)}), f16[16,32,256]{2,1,0:T(8,128)(2,1)S(1)}, u32[]{:S(2)}, u32[]{:S(2)}) async-start(f16[16,32,256]{2,1,0:T(8,128)(2,1)} %bitcast.12), calls=%async_computation.10 | async-start | bytes 524288 | tf_op jit(solution)/shard_map/all_to_all | solution.py:32
  200.3 3.9 %collective-permute-start.10 = (f16[128,256]{1,0:T(8,128)(2,1)S(1)}, f16[128,256]{1,0:T(8,128)(2,1)S(1)}, u32[]{:S(2)}, u32[]{:S(2)}) collective-permute-start(f16[128,256]{1,0:T(8,128)(2,1)S(1)} %get-tuple-element.47), channel_id=1, source_target_pairs={{0,4},{2,6},{4,0},{6,2},{1,5},{3,7},{5,1},{7,3},{8,12},{10,14},{12... | collective-permute-start | bytes 196616 | tf_op jit(solution)/shard_map/ppermute | solution.py:28
  207.9 7.4 %all-to-all-done.10 = f16[16,32,256]{2,1,0:T(8,128)(2,1)S(1)} async-done(((f16[16,32,256]{2,1,0:T(8,128)(2,1)}), f16[16,32,256]{2,1,0:T(8,128)(2,1)S(1)}, u32[]{:S(2)}, u32[]{:S(2)}) %all-to-all-start.10) | async-done | bytes 262176 | tf_op jit(solution)/shard_map/all_to_all | solution.py:32
  216.3 5.5 %all-to-all-start.11 = ((f16[16,32,256]{2,1,0:T(8,128)(2,1)}), f16[16,32,256]{2,1,0:T(8,128)(2,1)S(1)}, u32[]{:S(2)}, u32[]{:S(2)}) async-start(f16[16,32,256]{2,1,0:T(8,128)(2,1)} %broadcast_in_dim.96), calls=%async_computation.11 | async-start | bytes 524288 | tf_op jit(solution)/shard_map/all_to_all | solution.py:32
  226.5 12.8 %all-to-all-done.11 = f16[16,32,256]{2,1,0:T(8,128)(2,1)S(1)} async-done(((f16[16,32,256]{2,1,0:T(8,128)(2,1)}), f16[16,32,256]{2,1,0:T(8,128)(2,1)S(1)}, u32[]{:S(2)}, u32[]{:S(2)}) %all-to-all-start.11) | async-done | bytes 262176 | tf_op jit(solution)/shard_map/all_to_all | solution.py:32
  239.4 18.1 %all_to_all.67 = f16[4,512,256]{2,1,0:T(8,128)(2,1)S(1)} all-to-all(f16[4,512,256]{2,1,0:T(8,128)(2,1)S(1)} %broadcast_in_dim.104), channel_id=1, replica_groups=mesh['z'=16,'y'=4,'x'=4,'core'=2] {'y'}, dimensions={0} | all-to-all | bytes 2097152 | tf_op jit(solution)/shard_map/all_to_all | solution.py:32
  (105 shorter events, 83.7 us)
Async XLA Ops:
  1.5 24.8 %collective-permute-start = (bf16[128,256]{1,0:T(8,128)(2,1)S(1)}, bf16[128,256]{1,0:T(8,128)(2,1)S(1)}, u32[]{:S(2)}, u32[]{:S(2)}) collective-permute-start(bf16[128,256]{1,0:T(8,128)(2,1)S(1)} %constant_dynamic-slice_fusion.4), channel_id=1, source_target_pairs={{0,256},{32,288},{64,320},{96,352},{128,384},{160,416},{192,448},{... | collective-permute-start | bytes 196616 | tf_op jit(solution)/shard_map/ppermute | solution.py:28
  21.9 78.3 %copy-start.8 = (bf16[1024,256]{1,0:T(8,128)(2,1)}, bf16[1024,256]{1,0:T(8,128)(2,1)S(1)}, u32[]{:S(2)}) copy-start(bf16[1024,256]{1,0:T(8,128)(2,1)S(1)} %get-tuple-element.24.views_ref) | copy-start | bytes 1572868
  21.9 11.0 %all-to-all-start = ((f32[4,8,256]{2,1,0:T(8,128)}), f32[4,8,256]{2,1,0:T(8,128)S(1)}, u32[]{:S(2)}, u32[]{:S(2)}) async-start(f32[4,8,256]{2,1,0:T(8,128)} %get-tuple-element.26), calls=%async_computation | async-start | bytes 65536 | tf_op jit(solution)/shard_map/all_to_all | solution.py:32
  26.3 3.1 %collective-permute-start.1 = (bf16[128,256]{1,0:T(8,128)(2,1)S(1)}, bf16[128,256]{1,0:T(8,128)(2,1)S(1)}, u32[]{:S(2)}, u32[]{:S(2)}) collective-permute-start(bf16[128,256]{1,0:T(8,128)(2,1)S(1)} %collective-permute-done), channel_id=1, source_target_pairs={{0,1},{1,0},{2,3},{3,2},{4,5},{5,4},{6,7},{7,6},{8,9},{9,8},{10,11... | collective-permute-start | bytes 196616 | tf_op jit(solution)/shard_map/ppermute | solution.py:28
  29.5 19.8 %collective-permute-start.2 = (bf16[256,256]{1,0:T(8,128)(2,1)S(1)}, bf16[256,256]{1,0:T(8,128)(2,1)S(1)}, u32[]{:S(2)}, u32[]{:S(2)}) collective-permute-start(bf16[256,256]{1,0:T(8,128)(2,1)S(1)} %bitcast.53), channel_id=1, source_target_pairs={{0,2},{2,4},{4,6},{6,0},{1,3},{3,5},{5,7},{7,1},{8,10},{10,12},{12... | collective-permute-start | bytes 393224 | tf_op jit(solution)/shard_map/ppermute | solution.py:28
  33.5 19.2 %all-to-all-start.1 = ((bf16[16,8,256]{2,1,0:T(8,128)(2,1)}), bf16[16,8,256]{2,1,0:T(8,128)(2,1)S(1)}, u32[]{:S(2)}, u32[]{:S(2)}) async-start(bf16[16,8,256]{2,1,0:T(8,128)(2,1)} %broadcast_in_dim.85), calls=%async_computation.1 | async-start | bytes 131072 | tf_op jit(solution)/shard_map/all_to_all | solution.py:32
  41.2 8.4 %collective-permute-start.3 = (bf16[256,256]{1,0:T(8,128)(2,1)S(1)}, bf16[256,256]{1,0:T(8,128)(2,1)S(1)}, u32[]{:S(2)}, u32[]{:S(2)}) collective-permute-start(bf16[256,256]{1,0:T(8,128)(2,1)S(1)} %bitcast.54), channel_id=1, source_target_pairs={{0,4},{2,6},{4,0},{6,2},{1,5},{3,7},{5,1},{7,3},{8,12},{10,14},{12... | collective-permute-start | bytes 393224 | tf_op jit(solution)/shard_map/ppermute | solution.py:28
  45.8 6.9 %collective-permute-start.4 = (bf16[256,256]{1,0:T(8,128)(2,1)S(1)}, bf16[256,256]{1,0:T(8,128)(2,1)S(1)}, u32[]{:S(2)}, u32[]{:S(2)}) collective-permute-start(bf16[256,256]{1,0:T(8,128)(2,1)S(1)} %bitcast.55), channel_id=1, source_target_pairs={{0,6},{2,0},{4,2},{6,4},{1,7},{3,1},{5,3},{7,5},{8,14},{10,8},{12,... | collective-permute-start | bytes 393224 | tf_op jit(solution)/shard_map/ppermute | solution.py:28
  76.4 23.8 %all-to-all-start.4 = ((bf16[16,8,256]{2,1,0:T(8,128)(2,1)}), bf16[16,8,256]{2,1,0:T(8,128)(2,1)S(1)}, u32[]{:S(2)}, u32[]{:S(2)}) async-start(bf16[16,8,256]{2,1,0:T(8,128)(2,1)} %broadcast_in_dim.93), calls=%async_computation.4 | async-start | bytes 131072 | tf_op jit(solution)/shard_map/all_to_all | solution.py:32
  107.0 8.9 %all-to-all-start.5 = ((f32[8,2,1024]{2,1,0:T(2,128)}), f32[8,2,1024]{2,1,0:T(2,128)S(1)}, u32[]{:S(2)}, u32[]{:S(2)}) async-start(f32[8,2,1024]{2,1,0:T(2,128)} %get-tuple-element.35), calls=%async_computation.5 | async-start | bytes 131072 | tf_op jit(solution)/shard_map/all_to_all | solution.py:32
  120.9 8.7 %all-to-all-start.6 = ((f32[4,8,256]{2,1,0:T(8,128)}), f32[4,8,256]{2,1,0:T(8,128)S(1)}, u32[]{:S(2)}, u32[]{:S(2)}) async-start(f32[4,8,256]{2,1,0:T(8,128)} %column_pass.3), calls=%async_computation.6 | async-start | bytes 65536 | tf_op jit(solution)/shard_map/all_to_all | solution.py:32
  130.2 17.9 %all-to-all-start.7 = ((f32[16,8,256]{2,1,0:T(8,128)}), f32[16,8,256]{2,1,0:T(8,128)S(1)}, u32[]{:S(2)}, u32[]{:S(2)}) async-start(f32[16,8,256]{2,1,0:T(8,128)} %broadcast_in_dim.95), calls=%async_computation.7 | async-start | bytes 262144 | tf_op jit(solution)/shard_map/all_to_all | solution.py:32
  154.3 8.7 %all-to-all-start.8 = ((f32[8,1,1024]{2,1,0:T(1,128)}), f32[8,1,1024]{2,1,0:T(1,128)S(1)}, u32[]{:S(2)}, u32[]{:S(2)}) async-start(f32[8,1,1024]{2,1,0:T(1,128)} %get-tuple-element.40), calls=%async_computation.8 | async-start | bytes 65536 | tf_op jit(solution)/shard_map/all_to_all | solution.py:32
  172.9 18.8 %all-to-all-start.9 = ((f16[4,512,256]{2,1,0:T(8,128)(2,1)}), f16[4,512,256]{2,1,0:T(8,128)(2,1)S(1)}, u32[]{:S(2)}, u32[]{:S(2)}) async-start(f16[4,512,256]{2,1,0:T(8,128)(2,1)} %bitcast.11), calls=%async_computation.9 | async-start | bytes 2097152 | tf_op jit(solution)/shard_map/all_to_all | solution.py:32
  176.5 3.6 %collective-permute-start.5 = (f16[512,256]{1,0:T(8,128)(2,1)S(1)}, f16[512,256]{1,0:T(8,128)(2,1)}, u32[]{:S(2)}, u32[]{:S(2)}) collective-permute-start(f16[512,256]{1,0:T(8,128)(2,1)S(1)} %constant_dynamic-slice_fusion.3), channel_id=1, source_target_pairs={{0,1},{1,0},{2,3},{3,2},{4,5},{5,4},{6,7},{7,6},{8,9},{9,8},{10,11... | collective-permute-start | bytes 786440 | tf_op jit(solution)/shard_map/ppermute | solution.py:28
  181.1 16.1 %collective-permute-start.6 = (f16[128,256]{1,0:T(8,128)(2,1)S(1)}, f16[128,256]{1,0:T(8,128)(2,1)S(1)}, u32[]{:S(2)}, u32[]{:S(2)}) collective-permute-start(f16[128,256]{1,0:T(8,128)(2,1)S(1)} %get-tuple-element.52), channel_id=1, source_target_pairs={{0,2},{2,4},{4,6},{6,0},{1,3},{3,5},{5,7},{7,1},{8,10},{10,12},{12... | collective-permute-start | bytes 196616 | tf_op jit(solution)/shard_map/ppermute | solution.py:28
  183.6 13.6 %collective-permute-start.7 = (f16[128,256]{1,0:T(8,128)(2,1)S(1)}, f16[128,256]{1,0:T(8,128)(2,1)S(1)}, u32[]{:S(2)}, u32[]{:S(2)}) collective-permute-start(f16[128,256]{1,0:T(8,128)(2,1)S(1)} %get-tuple-element.54), channel_id=1, source_target_pairs={{0,4},{2,6},{4,0},{6,2},{1,5},{3,7},{5,1},{7,3},{8,12},{10,14},{12... | collective-permute-start | bytes 196616 | tf_op jit(solution)/shard_map/ppermute | solution.py:28
  187.6 9.6 %collective-permute-start.8 = (f16[128,256]{1,0:T(8,128)(2,1)S(1)}, f16[128,256]{1,0:T(8,128)(2,1)S(1)}, u32[]{:S(2)}, u32[]{:S(2)}) collective-permute-start(f16[128,256]{1,0:T(8,128)(2,1)S(1)} %get-tuple-element.53), channel_id=1, source_target_pairs={{0,6},{2,0},{4,2},{6,4},{1,7},{3,1},{5,3},{7,5},{8,14},{10,8},{12,... | collective-permute-start | bytes 196616 | tf_op jit(solution)/shard_map/ppermute | solution.py:28
  192.5 22.8 %all-to-all-start.10 = ((f16[16,32,256]{2,1,0:T(8,128)(2,1)}), f16[16,32,256]{2,1,0:T(8,128)(2,1)S(1)}, u32[]{:S(2)}, u32[]{:S(2)}) async-start(f16[16,32,256]{2,1,0:T(8,128)(2,1)} %bitcast.12), calls=%async_computation.10 | async-start | bytes 524288 | tf_op jit(solution)/shard_map/all_to_all | solution.py:32
  197.6 9.9 %collective-permute-start.9 = (f16[128,256]{1,0:T(8,128)(2,1)S(1)}, f16[128,256]{1,0:T(8,128)(2,1)S(1)}, u32[]{:S(2)}, u32[]{:S(2)}) collective-permute-start(f16[128,256]{1,0:T(8,128)(2,1)S(1)} %get-tuple-element.47), channel_id=1, source_target_pairs={{0,2},{2,4},{4,6},{6,0},{1,3},{3,5},{5,7},{7,1},{8,10},{10,12},{12... | collective-permute-start | bytes 196616 | tf_op jit(solution)/shard_map/ppermute | solution.py:28
  200.3 7.7 %collective-permute-start.10 = (f16[128,256]{1,0:T(8,128)(2,1)S(1)}, f16[128,256]{1,0:T(8,128)(2,1)S(1)}, u32[]{:S(2)}, u32[]{:S(2)}) collective-permute-start(f16[128,256]{1,0:T(8,128)(2,1)S(1)} %get-tuple-element.47), channel_id=1, source_target_pairs={{0,4},{2,6},{4,0},{6,2},{1,5},{3,7},{5,1},{7,3},{8,12},{10,14},{12... | collective-permute-start | bytes 196616 | tf_op jit(solution)/shard_map/ppermute | solution.py:28
  204.2 17.6 %collective-permute-start.11 = (f16[128,256]{1,0:T(8,128)(2,1)S(1)}, f16[128,256]{1,0:T(8,128)(2,1)S(1)}, u32[]{:S(2)}, u32[]{:S(2)}) collective-permute-start(f16[128,256]{1,0:T(8,128)(2,1)S(1)} %get-tuple-element.47), channel_id=1, source_target_pairs={{0,6},{2,0},{4,2},{6,4},{1,7},{3,1},{5,3},{7,5},{8,14},{10,8},{12,... | collective-permute-start | bytes 196616 | tf_op jit(solution)/shard_map/ppermute | solution.py:28
  216.3 23.0 %all-to-all-start.11 = ((f16[16,32,256]{2,1,0:T(8,128)(2,1)}), f16[16,32,256]{2,1,0:T(8,128)(2,1)S(1)}, u32[]{:S(2)}, u32[]{:S(2)}) async-start(f16[16,32,256]{2,1,0:T(8,128)(2,1)} %broadcast_in_dim.96), calls=%async_computation.11 | async-start | bytes 524288 | tf_op jit(solution)/shard_map/all_to_all | solution.py:32
  221.8 3.4 %collective-permute-start.12 = (f16[512,256]{1,0:T(8,128)(2,1)S(1)}, f16[512,256]{1,0:T(8,128)(2,1)S(1)}, u32[]{:S(2)}, u32[]{:S(2)}) collective-permute-start(f16[512,256]{1,0:T(8,128)(2,1)S(1)} %bitcast.51), channel_id=1, source_target_pairs={{0,1},{1,0},{2,3},{3,2},{4,5},{5,4},{6,7},{7,6},{8,9},{9,8},{10,11... | collective-permute-start | bytes 786440 | tf_op jit(solution)/shard_map/ppermute | solution.py:28
  (11 other events, 78.0 us)

commit v8 on v7

--- a/solution.py
+++ b/solution.py
@@ -64,9 +64,8 @@
     return lax.dynamic_slice_in_dim(value, index * size, size, 0)
 
 
-def scatter_sum(value, axis):
+def scatter_sum(value, axis, me):
     count = lax.axis_size(axis)
-    me = lax.axis_index(axis)
     total = block(value, me, count).astype(f32)
     for step in range(1, count):
         piece = shifted(block(value, (me + step) % count, count), axis, step)
@@ -74,13 +73,12 @@
     return total.astype(value.dtype)
 
 
-def gather_blocks(value, axis):
+def gather_blocks(value, axis, me):
     count = lax.axis_size(axis)
-    me = lax.axis_index(axis)
-    pieces = [value] + [shifted(value, axis, step) for step in range(1, count)]
-    out = jnp.zeros((count,) + value.shape, value.dtype)
-    for step, piece in enumerate(pieces):
-        out = lax.dynamic_update_slice_in_dim(out, piece[None], (me + count - step) % count, 0)
+    out = jnp.broadcast_to(value[None], (count,) + value.shape)
+    for step in range(1, count):
+        piece = shifted(value, axis, step)[None]
+        out = lax.dynamic_update_slice_in_dim(out, piece, (me + count - step) % count, 0)
     return out.reshape((-1,) + value.shape[1:])
 
 
@@ -270,10 +268,10 @@
         (part,) = call(col_kernel, "column_pass", [tempered, totals], [sums], 3 * entries, 4 * count)
         return total(exchanged(part, "y"))
 
-    sent = gather_blocks(gather_blocks(sent, "core"), "x")
+    sent = gather_blocks(gather_blocks(sent, "core", core), "x", x)
     column_part = total(exchanged(column_part, "y"))
     column_total = gathered(column_part.astype(bf16), "z")
-    column_total, sent = lax.optimization_barrier((column_total, sent))
+    column_total, sent, place = lax.optimization_barrier((column_total, sent, (y, z, x, core)))
     tempered, row_total = tempered_pass(views, column_total)
     column_part, sent = lax.optimization_barrier((column_pass(tempered, row_total), sent))
     other = sent[links]
@@ -304,20 +302,23 @@
         exps=entries,
     )
 
-    proto_rows = unit_rows(block(prototypes, y * z_count + z, y_count * z_count))[0]
-    view_rows = unit_rows(block(embeddings, core * x_count + x, members))[0]
+    view_part, proto_part, late_emb, late_proto, (y, z, x, core) = lax.optimization_barrier(
+        (view_part, proto_part, embeddings, prototypes, place)
+    )
+    proto_rows = unit_rows(block(late_proto, y * z_count + z, y_count * z_count))[0]
+    view_rows = unit_rows(block(late_emb, core * x_count + x, members))[0]
     proto_pieces = exchanged(proto_part.astype(SENT).reshape(y_count, -1, width), "y")
     proto_sum = total(proto_pieces).astype(SENT)
     proto_pieces = exchanged(proto_sum.reshape(z_count, -1, width), "z")
     proto_sum = (tangent(total(proto_pieces), proto_rows) * (1.0 / z_count)).astype(SENT)
     proto_sum = gathered(proto_sum, "z").reshape(-1, width)
 
-    view_sum = scatter_sum(scatter_sum(view_part.astype(SENT), "core"), "x")
+    view_sum = scatter_sum(scatter_sum(view_part.astype(SENT), "core", core), "x", x)
     view_sum = tangent(view_sum.astype(f32), view_rows).astype(SENT)
-    view_sum = gather_blocks(gather_blocks(view_sum, "x"), "core")
-
-    emb_grad = row_scale(embeddings) * view_sum.astype(f32)
-    proto_scale = row_scale(prototypes) * float(z_count)
+    view_sum = gather_blocks(gather_blocks(view_sum, "x", x), "core", core)
+
+    emb_grad = row_scale(late_emb) * view_sum.astype(f32)
+    proto_scale = row_scale(late_proto) * float(z_count)
 
     proto_sum, emb_grad, proto_scale = lax.optimization_barrier((proto_sum, emb_grad, proto_scale))
     proto_sum = gathered(proto_sum, "y").reshape(slots, width)

time: 261 us -> 251 us (0.962)
  blocking collectives: 37.3 us -> 53.8 us
  local copies, waits for them, and re-layouts: 25.7 us -> 11.2 us
  waiting for transfers between devices: 62.8 us -> 55.6 us
    all_to_all x10 -> x7, waiting for transfers between devices: 55.2 us -> 38.4 us  [exchanged(): return lax.all_to_all(value, axis, 0, 0, tiled=True)]
    all_to_all x3 -> x6, blocking collectives: 37.3 us -> 53.8 us  [exchanged(): return lax.all_to_all(value, axis, 0, 0, tiled=True)]
    unnamed x24 -> x18, local copies, waits for them, and re-layouts: 16.6 us -> 3.25 us
    ppermute x13, waiting for transfers between devices: 7.6 us -> 17.2 us  [shifted(): return lax.ppermute(value, axis, pairs)]
    all_to_all x10 -> x7, starting transfers between devices: 53 us -> 52.9 us  [exchanged(): return lax.all_to_all(value, axis, 0, 0, tiled=True)]
  transfers between devices with their start and end apart: 23 -> 20, of which waited for: 14 -> 11; matrix products, arithmetic and copies ran while one was open for 5% -> 4% of each run, Pallas kernels for 1% -> 1%
where the time goes in v8:
time: 251 us; the launch traced here: 249 us
  starting transfers between devices  102 us (41%)
  waiting for transfers between devices  55.6 us (22%)
  blocking collectives  53.8 us (21%)
  Pallas kernels  17.5 us (7%)
  local copies, waits for them, and re-layouts  11.2 us (4%)
  other arithmetic  7.99 us (3%)
    all_to_all x6, blocking collectives, exchanged(): return lax.all_to_all(value, axis, 0, 0, tiled=True)  53.8 us
    all_to_all x7, starting transfers between devices, exchanged(): return lax.all_to_all(value, axis, 0, 0, tiled=True)  52.9 us
    ppermute x13, starting transfers between devices, shifted(): return lax.ppermute(value, axis, pairs)  49.3 us
    all_to_all x7, waiting for transfers between devices, exchanged(): return lax.all_to_all(value, axis, 0, 0, tiled=True)  38.4 us
    pallas_call x7, Pallas kernels, call(): pl.pallas_call(kernel, name=name, out_shape=[jax.ShapeDtypeStruct(shape,...  17.5 us
    ppermute x13, waiting for transfers between devices, shifted(): return lax.ppermute(value, axis, pairs)  17.2 us
  transfers between devices with their start and end apart: 20, of which 11 were waited for; matrix products, arithmetic and copies ran while one was open for 4% of the time, Pallas kernels for 1%

profile of v8, /device:TPU:32, one launch (start us, length us, event | category | flops | bytes accessed | tf_op | source)
XLA Modules:
  0.0 249.4 jit_solution(13680431987357774528)
XLA Ops:
  1.5 14.8 %collective-permute-start = (bf16[128,256]{1,0:T(8,128)(2,1)S(1)}, bf16[128,256]{1,0:T(8,128)(2,1)S(1)}, u32[]{:S(2)}, u32[]{:S(2)}) collective-permute-start(bf16[128,256]{1,0:T(8,128)(2,1)S(1)} %constant_dynamic-slice_fusion.4), channel_id=1, source_target_pairs={{0,256},{32,288},{64,320},{96,352},{128,384},{160,416},{192,448},{... | collective-permute-start | bytes 196616 | tf_op jit(solution)/shard_map/ppermute | solution.py:28
  27.5 4.5 %all-to-all-start = ((f32[4,8,256]{2,1,0:T(8,128)}), f32[4,8,256]{2,1,0:T(8,128)S(1)}, u32[]{:S(2)}, u32[]{:S(2)}) async-start(f32[4,8,256]{2,1,0:T(8,128)} %get-tuple-element.38), calls=%async_computation | async-start | bytes 65536 | tf_op jit(solution)/shard_map/all_to_all | solution.py:32
  38.1 13.9 %all-to-all-start.1 = ((bf16[16,8,256]{2,1,0:T(8,128)(2,1)}), bf16[16,8,256]{2,1,0:T(8,128)(2,1)S(1)}, u32[]{:S(2)}, u32[]{:S(2)}) async-start(bf16[16,8,256]{2,1,0:T(8,128)(2,1)} %broadcast_in_dim.43), calls=%async_computation.1 | async-start | bytes 131072 | tf_op jit(solution)/shard_map/all_to_all | solution.py:32
  52.0 4.7 %collective-permute-start.4 = (bf16[256,256]{1,0:T(8,128)(2,1)S(1)}, bf16[256,256]{1,0:T(8,128)(2,1)S(1)}, u32[]{:S(2)}, u32[]{:S(2)}) collective-permute-start(bf16[256,256]{1,0:T(8,128)(2,1)S(1)} %bitcast.45), channel_id=1, source_target_pairs={{0,6},{2,0},{4,2},{6,4},{1,7},{3,1},{5,3},{7,5},{8,14},{10,8},{12,... | collective-permute-start | bytes 393224 | tf_op jit(solution)/shard_map/ppermute | solution.py:28
  59.4 5.6 %collective-permute-done.3 = bf16[256,256]{1,0:T(8,128)(2,1)S(1)} collective-permute-done((bf16[256,256]{1,0:T(8,128)(2,1)S(1)}, bf16[256,256]{1,0:T(8,128)(2,1)S(1)}, u32[]{:S(2)}, u32[]{:S(2)}) %collective-permute-start.3) | collective-permute-done | bytes 131104 | tf_op jit(solution)/shard_map/ppermute | solution.py:28
  68.0 8.4 %all_to_all.65.totals_ref = f32[8,2,1024]{2,1,0:T(2,128)S(1)} all-to-all(f32[8,2,1024]{2,1,0:T(2,128)S(1)} %get-tuple-element.41), channel_id=1, replica_groups=mesh['z'=16,'y'=4,'x'=4,'core'=2] {'x','core'}, dimensions={0} | all-to-all | bytes 131072 | tf_op jit(solution)/shard_map/all_to_all | solution.py:32
  77.4 7.8 %all_to_all.66 = f32[4,8,256]{2,1,0:T(8,128)S(1)} all-to-all(f32[4,8,256]{2,1,0:T(8,128)S(1)} %column_pass.2), channel_id=1, replica_groups=mesh['z'=16,'y'=4,'x'=4,'core'=2] {'y'}, dimensions={0} | all-to-all | bytes 65536 | tf_op jit(solution)/shard_map/all_to_all | solution.py:32
  85.8 11.6 %all-to-all-start.4 = ((bf16[16,8,256]{2,1,0:T(8,128)(2,1)}), bf16[16,8,256]{2,1,0:T(8,128)(2,1)S(1)}, u32[]{:S(2)}, u32[]{:S(2)}) async-start(bf16[16,8,256]{2,1,0:T(8,128)(2,1)} %broadcast_in_dim.101), calls=%async_computation.4 | async-start | bytes 131072 | tf_op jit(solution)/shard_map/all_to_all | solution.py:32
  97.5 3.9 %gather_fusion = bf16[1024,256]{1,0:T(8,128)(2,1)S(1)} fusion(bf16[1024,256]{1,0:T(8,128)(2,1)S(1)} %bitcast.39, s32[1024]{0:T(1024)S(1)} %fusion.21), kind=kCustom, calls=%fused_computation | custom fusion | bytes 1052672 | tf_op jit(solution)/shard_map/gather | solution.py:277
  101.4 7.7 %all-to-all-done.4.totals_ref = bf16[16,8,256]{2,1,0:T(8,128)(2,1)S(1)} async-done(((bf16[16,8,256]{2,1,0:T(8,128)(2,1)}), bf16[16,8,256]{2,1,0:T(8,128)(2,1)S(1)}, u32[]{:S(2)}, u32[]{:S(2)}) %all-to-all-start.4) | async-done | bytes 65568 | tf_op jit(solution)/shard_map/all_to_all | solution.py:32
  112.1 8.0 %all_to_all.67.totals_ref.soft_ref = f32[8,2,1024]{2,1,0:T(2,128)S(1)} all-to-all(f32[8,2,1024]{2,1,0:T(2,128)S(1)} %get-tuple-element.47), channel_id=1, replica_groups=mesh['z'=16,'y'=4,'x'=4,'core'=2] {'x','core'}, dimensions={0} | all-to-all | bytes 131072 | tf_op jit(solution)/shard_map/all_to_all | solution.py:32
  121.1 7.8 %all_to_all.68 = f32[4,8,256]{2,1,0:T(8,128)S(1)} all-to-all(f32[4,8,256]{2,1,0:T(8,128)S(1)} %column_pass.3), channel_id=1, replica_groups=mesh['z'=16,'y'=4,'x'=4,'core'=2] {'y'}, dimensions={0} | all-to-all | bytes 65536 | tf_op jit(solution)/shard_map/all_to_all | solution.py:32
  129.5 4.5 %all-to-all-start.7 = ((f32[16,8,256]{2,1,0:T(8,128)}), f32[16,8,256]{2,1,0:T(8,128)S(1)}, u32[]{:S(2)}, u32[]{:S(2)}) async-start(f32[16,8,256]{2,1,0:T(8,128)} %broadcast_in_dim.103), calls=%async_computation.7 | async-start | bytes 262144 | tf_op jit(solution)/shard_map/all_to_all | solution.py:32
  134.5 12.5 %all-to-all-done.7.totals_ref = f32[16,8,256]{2,1,0:T(8,128)S(1)} async-done(((f32[16,8,256]{2,1,0:T(8,128)}), f32[16,8,256]{2,1,0:T(8,128)S(1)}, u32[]{:S(2)}, u32[]{:S(2)}) %all-to-all-start.7) | async-done | bytes 131104 | tf_op jit(solution)/shard_map/all_to_all | solution.py:32
  149.2 7.8 %all_to_all.69.line_ref = f32[8,1,1024]{2,1,0:T(1,128)S(1)} all-to-all(f32[8,1,1024]{2,1,0:T(1,128)S(1)} %get-tuple-element.52), channel_id=1, replica_groups=mesh['z'=16,'y'=4,'x'=4,'core'=2] {'x','core'}, dimensions={0} | all-to-all | bytes 65536 | tf_op jit(solution)/shard_map/all_to_all | solution.py:32
  157.0 4.2 %gradient.1 = (f32[1024,256]{1,0:T(8,128)S(1)}, f32[2048,256]{1,0:T(8,128)S(1)}) custom-call(f32[1024,2048]{1,0:T(8,128)S(1)} %get-tuple-element.51.other_ref, f32[16,8,256]{2,1,0:T(8,128)S(1)} %all-to-all-done.7.totals_ref, f32[8,1,1024]{2,1,0:T(1,128)S(1)} %all_to_all.69.line_ref, f32[8,2,1024]{2,1,0:T(2,128)S(1)} %all_to_all.67.totals_ref.soft_ref, ...), custom_call_target="tpu_custom_call" | custom-call | flops 3221225472 | bytes 4194304 | tf_op jit(solution)/shard_map/gradient/pallas_call | solution.py:222
  163.5 4.4 %all-to-all-start.9 = ((f16[4,512,256]{2,1,0:T(8,128)(2,1)}), f16[4,512,256]{2,1,0:T(8,128)(2,1)}, u32[]{:S(2)}, u32[]{:S(2)}) async-start(f16[4,512,256]{2,1,0:T(8,128)(2,1)} %bitcast.40), calls=%async_computation.9 | async-start | bytes 2097152 | tf_op jit(solution)/shard_map/all_to_all | solution.py:32
  174.1 4.6 %collective-permute-start.8 = (f16[128,256]{1,0:T(8,128)(2,1)S(1)}, f16[128,256]{1,0:T(8,128)(2,1)S(1)}, u32[]{:S(2)}, u32[]{:S(2)}) collective-permute-start(f16[128,256]{1,0:T(8,128)(2,1)S(1)} %get-tuple-element.75), channel_id=1, source_target_pairs={{0,6},{2,0},{4,2},{6,4},{1,7},{3,1},{5,3},{7,5},{8,14},{10,8},{12,... | collective-permute-start | bytes 196616 | tf_op jit(solution)/shard_map/ppermute | solution.py:28
  185.3 4.7 %all-to-all-start.10 = ((f16[16,32,256]{2,1,0:T(8,128)(2,1)}), f16[16,32,256]{2,1,0:T(8,128)(2,1)S(1)}, u32[]{:S(2)}, u32[]{:S(2)}) async-start(f16[16,32,256]{2,1,0:T(8,128)(2,1)} %bitcast.10), calls=%async_computation.10 | async-start | bytes 524288 | tf_op jit(solution)/shard_map/all_to_all | solution.py:32
  192.9 4.6 %collective-permute-start.11 = (f16[128,256]{1,0:T(8,128)(2,1)S(1)}, f16[128,256]{1,0:T(8,128)(2,1)S(1)}, u32[]{:S(2)}, u32[]{:S(2)}) collective-permute-start(f16[128,256]{1,0:T(8,128)(2,1)S(1)} %fusion.4), channel_id=1, source_target_pairs={{0,6},{2,0},{4,2},{6,4},{1,7},{3,1},{5,3},{7,5},{8,14},{10,8},{12,... | collective-permute-start | bytes 196616 | tf_op jit(solution)/shard_map/ppermute | solution.py:28
  199.4 5.7 %collective-permute-done.10 = f16[128,256]{1,0:T(8,128)(2,1)S(1)} collective-permute-done((f16[128,256]{1,0:T(8,128)(2,1)S(1)}, f16[128,256]{1,0:T(8,128)(2,1)S(1)}, u32[]{:S(2)}, u32[]{:S(2)}) %collective-permute-start.10) | collective-permute-done | bytes 65568 | tf_op jit(solution)/shard_map/ppermute | solution.py:28
  209.0 9.2 %all-to-all-start.11 = ((f16[16,32,256]{2,1,0:T(8,128)(2,1)}), f16[16,32,256]{2,1,0:T(8,128)(2,1)S(1)}, u32[]{:S(2)}, u32[]{:S(2)}) async-start(f16[16,32,256]{2,1,0:T(8,128)(2,1)} %broadcast_in_dim.104), calls=%async_computation.11 | async-start | bytes 524288 | tf_op jit(solution)/shard_map/all_to_all | solution.py:32
  222.9 10.8 %all-to-all-done.11 = f16[16,32,256]{2,1,0:T(8,128)(2,1)S(1)} async-done(((f16[16,32,256]{2,1,0:T(8,128)(2,1)}), f16[16,32,256]{2,1,0:T(8,128)(2,1)S(1)}, u32[]{:S(2)}, u32[]{:S(2)}) %all-to-all-start.11) | async-done | bytes 262176 | tf_op jit(solution)/shard_map/all_to_all | solution.py:32
  233.8 13.9 %all_to_all.70 = f16[4,512,256]{2,1,0:T(8,128)(2,1)S(1)} all-to-all(f16[4,512,256]{2,1,0:T(8,128)(2,1)S(1)} %broadcast_in_dim.112), channel_id=1, replica_groups=mesh['z'=16,'y'=4,'x'=4,'core'=2] {'y'}, dimensions={0} | all-to-all | bytes 2097152 | tf_op jit(solution)/shard_map/all_to_all | solution.py:32
  (93 shorter events, 62.7 us)
Async XLA Ops:
  1.5 18.5 %collective-permute-start = (bf16[128,256]{1,0:T(8,128)(2,1)S(1)}, bf16[128,256]{1,0:T(8,128)(2,1)S(1)}, u32[]{:S(2)}, u32[]{:S(2)}) collective-permute-start(bf16[128,256]{1,0:T(8,128)(2,1)S(1)} %constant_dynamic-slice_fusion.4), channel_id=1, source_target_pairs={{0,256},{32,288},{64,320},{96,352},{128,384},{160,416},{192,448},{... | collective-permute-start | bytes 196616 | tf_op jit(solution)/shard_map/ppermute | solution.py:28
  20.0 11.9 %collective-permute-start.1 = (bf16[128,256]{1,0:T(8,128)(2,1)S(1)}, bf16[128,256]{1,0:T(8,128)(2,1)S(1)}, u32[]{:S(2)}, u32[]{:S(2)}) collective-permute-start(bf16[128,256]{1,0:T(8,128)(2,1)S(1)} %collective-permute-done), channel_id=1, source_target_pairs={{0,1},{1,0},{2,3},{3,2},{4,5},{5,4},{6,7},{7,6},{8,9},{9,8},{10,11... | collective-permute-start | bytes 196616 | tf_op jit(solution)/shard_map/ppermute | solution.py:28
  27.5 81.7 %copy-start.6 = (bf16[1024,256]{1,0:T(8,128)(2,1)}, bf16[1024,256]{1,0:T(8,128)(2,1)S(1)}, u32[]{:S(2)}) copy-start(bf16[1024,256]{1,0:T(8,128)(2,1)S(1)} %get-tuple-element.36.views_ref) | copy-start | bytes 1572868
  27.5 9.9 %all-to-all-start = ((f32[4,8,256]{2,1,0:T(8,128)}), f32[4,8,256]{2,1,0:T(8,128)S(1)}, u32[]{:S(2)}, u32[]{:S(2)}) async-start(f32[4,8,256]{2,1,0:T(8,128)} %get-tuple-element.38), calls=%async_computation | async-start | bytes 65536 | tf_op jit(solution)/shard_map/all_to_all | solution.py:32
  32.0 27.4 %collective-permute-start.2 = (bf16[256,256]{1,0:T(8,128)(2,1)S(1)}, bf16[256,256]{1,0:T(8,128)(2,1)S(1)}, u32[]{:S(2)}, u32[]{:S(2)}) collective-permute-start(bf16[256,256]{1,0:T(8,128)(2,1)S(1)} %bitcast.44), channel_id=1, source_target_pairs={{0,2},{2,4},{4,6},{6,0},{1,3},{3,5},{5,7},{7,1},{8,10},{10,12},{12... | collective-permute-start | bytes 393224 | tf_op jit(solution)/shard_map/ppermute | solution.py:28
  38.1 27.0 %all-to-all-start.1 = ((bf16[16,8,256]{2,1,0:T(8,128)(2,1)}), bf16[16,8,256]{2,1,0:T(8,128)(2,1)S(1)}, u32[]{:S(2)}, u32[]{:S(2)}) async-start(bf16[16,8,256]{2,1,0:T(8,128)(2,1)} %broadcast_in_dim.43), calls=%async_computation.1 | async-start | bytes 131072 | tf_op jit(solution)/shard_map/all_to_all | solution.py:32
  52.0 13.0 %collective-permute-start.4 = (bf16[256,256]{1,0:T(8,128)(2,1)S(1)}, bf16[256,256]{1,0:T(8,128)(2,1)S(1)}, u32[]{:S(2)}, u32[]{:S(2)}) collective-permute-start(bf16[256,256]{1,0:T(8,128)(2,1)S(1)} %bitcast.45), channel_id=1, source_target_pairs={{0,6},{2,0},{4,2},{6,4},{1,7},{3,1},{5,3},{7,5},{8,14},{10,8},{12,... | collective-permute-start | bytes 393224 | tf_op jit(solution)/shard_map/ppermute | solution.py:28
  56.6 8.4 %collective-permute-start.3 = (bf16[256,256]{1,0:T(8,128)(2,1)S(1)}, bf16[256,256]{1,0:T(8,128)(2,1)S(1)}, u32[]{:S(2)}, u32[]{:S(2)}) collective-permute-start(bf16[256,256]{1,0:T(8,128)(2,1)S(1)} %bitcast.46), channel_id=1, source_target_pairs={{0,4},{2,6},{4,0},{6,2},{1,5},{3,7},{5,1},{7,3},{8,12},{10,14},{12... | collective-permute-start | bytes 393224 | tf_op jit(solution)/shard_map/ppermute | solution.py:28
  76.4 21.1 %copy-start.8 = (s32[1024]{0:T(1024)S(1)}, s32[1024]{0:T(1024)}, u32[]{:S(2)}) copy-start(s32[1024]{0:T(1024)} %param.5) | copy-start | bytes 12292
  85.8 23.3 %all-to-all-start.4 = ((bf16[16,8,256]{2,1,0:T(8,128)(2,1)}), bf16[16,8,256]{2,1,0:T(8,128)(2,1)S(1)}, u32[]{:S(2)}, u32[]{:S(2)}) async-start(bf16[16,8,256]{2,1,0:T(8,128)(2,1)} %broadcast_in_dim.101), calls=%async_computation.4 | async-start | bytes 131072 | tf_op jit(solution)/shard_map/all_to_all | solution.py:32
  129.5 17.4 %all-to-all-start.7 = ((f32[16,8,256]{2,1,0:T(8,128)}), f32[16,8,256]{2,1,0:T(8,128)S(1)}, u32[]{:S(2)}, u32[]{:S(2)}) async-start(f32[16,8,256]{2,1,0:T(8,128)} %broadcast_in_dim.103), calls=%async_computation.7 | async-start | bytes 262144 | tf_op jit(solution)/shard_map/all_to_all | solution.py:32
  147.0 10.1 %copy-start.7 = (bf16[1024,256]{1,0:T(8,128)(2,1)S(1)}, bf16[1024,256]{1,0:T(8,128)(2,1)}, u32[]{:S(2)}) copy-start(bf16[1024,256]{1,0:T(8,128)(2,1)} %copy-done.6) | copy-start | bytes 1572868
  163.5 6.8 %copy-start.3 = (bf16[2048,256]{1,0:T(8,128)(2,1)S(1)}, bf16[2048,256]{1,0:T(8,128)(2,1)}, u32[]{:S(2)}) copy-start(bf16[2048,256]{1,0:T(8,128)(2,1)} %proto_ref.1) | copy-start | bytes 3145732
  163.5 19.8 %all-to-all-start.9 = ((f16[4,512,256]{2,1,0:T(8,128)(2,1)}), f16[4,512,256]{2,1,0:T(8,128)(2,1)}, u32[]{:S(2)}, u32[]{:S(2)}) async-start(f16[4,512,256]{2,1,0:T(8,128)(2,1)} %bitcast.40), calls=%async_computation.9 | async-start | bytes 2097152 | tf_op jit(solution)/shard_map/all_to_all | solution.py:32
  168.0 3.4 %collective-permute-start.5 = (f16[512,256]{1,0:T(8,128)(2,1)S(1)}, f16[512,256]{1,0:T(8,128)(2,1)S(1)}, u32[]{:S(2)}, u32[]{:S(2)}) collective-permute-start(f16[512,256]{1,0:T(8,128)(2,1)S(1)} %constant_dynamic-slice_fusion.3), channel_id=1, source_target_pairs={{0,1},{1,0},{2,3},{3,2},{4,5},{5,4},{6,7},{7,6},{8,9},{9,8},{10,11... | collective-permute-start | bytes 786440 | tf_op jit(solution)/shard_map/ppermute | solution.py:28
  171.6 18.4 %collective-permute-start.6 = (f16[128,256]{1,0:T(8,128)(2,1)S(1)}, f16[128,256]{1,0:T(8,128)(2,1)S(1)}, u32[]{:S(2)}, u32[]{:S(2)}) collective-permute-start(f16[128,256]{1,0:T(8,128)(2,1)S(1)} %get-tuple-element.74), channel_id=1, source_target_pairs={{0,2},{2,4},{4,6},{6,0},{1,3},{3,5},{5,7},{7,1},{8,10},{10,12},{12... | collective-permute-start | bytes 196616 | tf_op jit(solution)/shard_map/ppermute | solution.py:28
  174.1 15.9 %collective-permute-start.8 = (f16[128,256]{1,0:T(8,128)(2,1)S(1)}, f16[128,256]{1,0:T(8,128)(2,1)S(1)}, u32[]{:S(2)}, u32[]{:S(2)}) collective-permute-start(f16[128,256]{1,0:T(8,128)(2,1)S(1)} %get-tuple-element.75), channel_id=1, source_target_pairs={{0,6},{2,0},{4,2},{6,4},{1,7},{3,1},{5,3},{7,5},{8,14},{10,8},{12,... | collective-permute-start | bytes 196616 | tf_op jit(solution)/shard_map/ppermute | solution.py:28
  178.7 11.4 %collective-permute-start.7 = (f16[128,256]{1,0:T(8,128)(2,1)S(1)}, f16[128,256]{1,0:T(8,128)(2,1)S(1)}, u32[]{:S(2)}, u32[]{:S(2)}) collective-permute-start(f16[128,256]{1,0:T(8,128)(2,1)S(1)} %get-tuple-element.76), channel_id=1, source_target_pairs={{0,4},{2,6},{4,0},{6,2},{1,5},{3,7},{5,1},{7,3},{8,12},{10,14},{12... | collective-permute-start | bytes 196616 | tf_op jit(solution)/shard_map/ppermute | solution.py:28
  185.3 22.7 %all-to-all-start.10 = ((f16[16,32,256]{2,1,0:T(8,128)(2,1)}), f16[16,32,256]{2,1,0:T(8,128)(2,1)S(1)}, u32[]{:S(2)}, u32[]{:S(2)}) async-start(f16[16,32,256]{2,1,0:T(8,128)(2,1)} %bitcast.10), calls=%async_computation.10 | async-start | bytes 524288 | tf_op jit(solution)/shard_map/all_to_all | solution.py:32
  190.3 9.0 %collective-permute-start.9 = (f16[128,256]{1,0:T(8,128)(2,1)S(1)}, f16[128,256]{1,0:T(8,128)(2,1)S(1)}, u32[]{:S(2)}, u32[]{:S(2)}) collective-permute-start(f16[128,256]{1,0:T(8,128)(2,1)S(1)} %fusion.4), channel_id=1, source_target_pairs={{0,2},{2,4},{4,6},{6,0},{1,3},{3,5},{5,7},{7,1},{8,10},{10,12},{12... | collective-permute-start | bytes 196616 | tf_op jit(solution)/shard_map/ppermute | solution.py:28
  192.9 25.3 %collective-permute-start.11 = (f16[128,256]{1,0:T(8,128)(2,1)S(1)}, f16[128,256]{1,0:T(8,128)(2,1)S(1)}, u32[]{:S(2)}, u32[]{:S(2)}) collective-permute-start(f16[128,256]{1,0:T(8,128)(2,1)S(1)} %fusion.4), channel_id=1, source_target_pairs={{0,6},{2,0},{4,2},{6,4},{1,7},{3,1},{5,3},{7,5},{8,14},{10,8},{12,... | collective-permute-start | bytes 196616 | tf_op jit(solution)/shard_map/ppermute | solution.py:28
  197.5 7.7 %collective-permute-start.10 = (f16[128,256]{1,0:T(8,128)(2,1)S(1)}, f16[128,256]{1,0:T(8,128)(2,1)S(1)}, u32[]{:S(2)}, u32[]{:S(2)}) collective-permute-start(f16[128,256]{1,0:T(8,128)(2,1)S(1)} %fusion.4), channel_id=1, source_target_pairs={{0,4},{2,6},{4,0},{6,2},{1,5},{3,7},{5,1},{7,3},{8,12},{10,14},{12... | collective-permute-start | bytes 196616 | tf_op jit(solution)/shard_map/ppermute | solution.py:28
  209.0 24.7 %all-to-all-start.11 = ((f16[16,32,256]{2,1,0:T(8,128)(2,1)}), f16[16,32,256]{2,1,0:T(8,128)(2,1)S(1)}, u32[]{:S(2)}, u32[]{:S(2)}) async-start(f16[16,32,256]{2,1,0:T(8,128)(2,1)} %broadcast_in_dim.104), calls=%async_computation.11 | async-start | bytes 524288 | tf_op jit(solution)/shard_map/all_to_all | solution.py:32
  218.2 3.4 %collective-permute-start.12 = (f16[512,256]{1,0:T(8,128)(2,1)S(1)}, f16[512,256]{1,0:T(8,128)(2,1)S(1)}, u32[]{:S(2)}, u32[]{:S(2)}) collective-permute-start(f16[512,256]{1,0:T(8,128)(2,1)S(1)} %bitcast.41), channel_id=1, source_target_pairs={{0,1},{1,0},{2,3},{3,2},{4,5},{5,4},{6,7},{7,6},{8,9},{9,8},{10,11... | collective-permute-start | bytes 786440 | tf_op jit(solution)/shard_map/ppermute | solution.py:28
  (5 other events, 8.9 us)

commit v9 on v8

--- a/solution.py
+++ b/solution.py
@@ -71,6 +71,15 @@
         piece = shifted(block(value, (me + step) % count, count), axis, step)
         total = total + piece.astype(f32)
     return total.astype(value.dtype)
+
+
+def gather_blocks_early(value, axis, me):
+    count = lax.axis_size(axis)
+    out = jnp.zeros((count,) + value.shape, value.dtype)
+    for step in range(count):
+        piece = (shifted(value, axis, step) if step else value)[None]
+        out = lax.dynamic_update_slice_in_dim(out, piece, (me + count - step) % count, 0)
+    return out.reshape((-1,) + value.shape[1:])
 
 
 def gather_blocks(value, axis, me):
@@ -268,16 +277,16 @@
         (part,) = call(col_kernel, "column_pass", [tempered, totals], [sums], 3 * entries, 4 * count)
         return total(exchanged(part, "y"))
 
-    sent = gather_blocks(gather_blocks(sent, "core", core), "x", x)
+    sent = gather_blocks_early(gather_blocks_early(sent, "core", core), "x", x)
     column_part = total(exchanged(column_part, "y"))
     column_total = gathered(column_part.astype(bf16), "z")
-    column_total, sent, place = lax.optimization_barrier((column_total, sent, (y, z, x, core)))
+    column_total, sent = lax.optimization_barrier((column_total, sent))
     tempered, row_total = tempered_pass(views, column_total)
     column_part, sent = lax.optimization_barrier((column_pass(tempered, row_total), sent))
     other = sent[links]
     column_total = gathered(column_part.astype(bf16), "z")
     for sweep in range(2, ITERS):
-        column_total, other = lax.optimization_barrier((column_total, other))
+        column_total, other, place = lax.optimization_barrier((column_total, other, (y, z, x, core)))
         tempered, row_total = tempered_pass(views, column_total)
         column_part, other = lax.optimization_barrier((column_pass(tempered, row_total), other))
         column_total = gathered(column_part, "z")

time: 251 us -> 241 us (0.960)
  starting transfers between devices: 102 us -> 95.8 us
  waiting for transfers between devices: 55.6 us -> 50 us
  blocking collectives: 53.8 us -> 56.4 us
    all_to_all x7, starting transfers between devices: 52.9 us -> 46.5 us  [exchanged(): return lax.all_to_all(value, axis, 0, 0, tiled=True)]
    ppermute x13, waiting for transfers between devices: 17.2 us -> 13.4 us  [shifted(): return lax.ppermute(value, axis, pairs)]
    all_to_all x6, blocking collectives: 53.8 us -> 56.4 us  [exchanged(): return lax.all_to_all(value, axis, 0, 0, tiled=True)]
  transfers between devices with their start and end apart: 20 -> 20, of which waited for: 11 -> 10; matrix products, arithmetic and copies ran while one was open for 4% -> 4% of each run, Pallas kernels for 1% -> 1%
where the time goes in v9:
time: 241 us; the launch traced here: 240 us
  starting transfers between devices  95.8 us (40%)
  blocking collectives  56.4 us (23%)
  waiting for transfers between devices  50 us (21%)
  Pallas kernels  17.5 us (7%)
  local copies, waits for them, and re-layouts  11.2 us (5%)
  other arithmetic  7.99 us (3%)
    all_to_all x6, blocking collectives, exchanged(): return lax.all_to_all(value, axis, 0, 0, tiled=True)  56.4 us
    ppermute x13, starting transfers between devices, shifted(): return lax.ppermute(value, axis, pairs)  49.3 us
    all_to_all x7, starting transfers between devices, exchanged(): return lax.all_to_all(value, axis, 0, 0, tiled=True)  46.5 us
    all_to_all x7, waiting for transfers between devices, exchanged(): return lax.all_to_all(value, axis, 0, 0, tiled=True)  36.6 us
    pallas_call x7, Pallas kernels, call(): pl.pallas_call(kernel, name=name, out_shape=[jax.ShapeDtypeStruct(shape,...  17.5 us
    ppermute x13, waiting for transfers between devices, shifted(): return lax.ppermute(value, axis, pairs)  13.4 us
  transfers between devices with their start and end apart: 20, of which 10 were waited for; matrix products, arithmetic and copies ran while one was open for 4% of the time, Pallas kernels for 1%

profile of v9, /device:TPU:32, one launch (start us, length us, event | category | flops | bytes accessed | tf_op | source)
XLA Modules:
  0.0 240.1 jit_solution(10093019797059744056)
XLA Ops:
  1.5 14.8 %collective-permute-start = (bf16[128,256]{1,0:T(8,128)(2,1)S(1)}, bf16[128,256]{1,0:T(8,128)(2,1)S(1)}, u32[]{:S(2)}, u32[]{:S(2)}) collective-permute-start(bf16[128,256]{1,0:T(8,128)(2,1)S(1)} %constant_dynamic-slice_fusion.4), channel_id=1, source_target_pairs={{0,256},{32,288},{64,320},{96,352},{128,384},{160,416},{192,448},{... | collective-permute-start | bytes 196616 | tf_op jit(solution)/shard_map/ppermute | solution.py:28
  21.9 4.5 %all-to-all-start = ((f32[4,8,256]{2,1,0:T(8,128)}), f32[4,8,256]{2,1,0:T(8,128)S(1)}, u32[]{:S(2)}, u32[]{:S(2)}) async-start(f32[4,8,256]{2,1,0:T(8,128)} %get-tuple-element.38), calls=%async_computation | async-start | bytes 65536 | tf_op jit(solution)/shard_map/all_to_all | solution.py:32
  33.5 7.6 %all-to-all-start.1 = ((bf16[16,8,256]{2,1,0:T(8,128)(2,1)}), bf16[16,8,256]{2,1,0:T(8,128)(2,1)S(1)}, u32[]{:S(2)}, u32[]{:S(2)}) async-start(bf16[16,8,256]{2,1,0:T(8,128)(2,1)} %broadcast_in_dim.43), calls=%async_computation.1 | async-start | bytes 131072 | tf_op jit(solution)/shard_map/all_to_all | solution.py:32
  44.6 3.9 %collective-permute-start.3 = (bf16[256,256]{1,0:T(8,128)(2,1)S(1)}, bf16[256,256]{1,0:T(8,128)(2,1)S(1)}, u32[]{:S(2)}, u32[]{:S(2)}) collective-permute-start(bf16[256,256]{1,0:T(8,128)(2,1)S(1)} %bitcast.51), channel_id=1, source_target_pairs={{0,4},{2,6},{4,0},{6,2},{1,5},{3,7},{5,1},{7,3},{8,12},{10,14},{12... | collective-permute-start | bytes 393224 | tf_op jit(solution)/shard_map/ppermute | solution.py:28
  48.7 4.3 %collective-permute-done.3 = bf16[256,256]{1,0:T(8,128)(2,1)S(1)} collective-permute-done((bf16[256,256]{1,0:T(8,128)(2,1)S(1)}, bf16[256,256]{1,0:T(8,128)(2,1)S(1)}, u32[]{:S(2)}, u32[]{:S(2)}) %collective-permute-start.3) | collective-permute-done | bytes 131104 | tf_op jit(solution)/shard_map/ppermute | solution.py:28
  56.0 9.1 %all_to_all.65.totals_ref = f32[8,2,1024]{2,1,0:T(2,128)S(1)} all-to-all(f32[8,2,1024]{2,1,0:T(2,128)S(1)} %get-tuple-element.41), channel_id=1, replica_groups=mesh['z'=16,'y'=4,'x'=4,'core'=2] {'x','core'}, dimensions={0} | all-to-all | bytes 131072 | tf_op jit(solution)/shard_map/all_to_all | solution.py:32
  66.1 9.7 %all_to_all.66 = f32[4,8,256]{2,1,0:T(8,128)S(1)} all-to-all(f32[4,8,256]{2,1,0:T(8,128)S(1)} %column_pass.2), channel_id=1, replica_groups=mesh['z'=16,'y'=4,'x'=4,'core'=2] {'y'}, dimensions={0} | all-to-all | bytes 65536 | tf_op jit(solution)/shard_map/all_to_all | solution.py:32
  76.4 11.7 %all-to-all-start.4 = ((bf16[16,8,256]{2,1,0:T(8,128)(2,1)}), bf16[16,8,256]{2,1,0:T(8,128)(2,1)S(1)}, u32[]{:S(2)}, u32[]{:S(2)}) async-start(bf16[16,8,256]{2,1,0:T(8,128)(2,1)} %broadcast_in_dim.97), calls=%async_computation.4 | async-start | bytes 131072 | tf_op jit(solution)/shard_map/all_to_all | solution.py:32
  88.1 3.9 %gather_fusion = bf16[1024,256]{1,0:T(8,128)(2,1)S(1)} fusion(bf16[1024,256]{1,0:T(8,128)(2,1)S(1)} %bitcast.44, s32[1024]{0:T(1024)S(1)} %fusion.21), kind=kCustom, calls=%fused_computation | custom fusion | bytes 1052672 | tf_op jit(solution)/shard_map/gather | solution.py:286
  92.1 7.9 %all-to-all-done.4.totals_ref = bf16[16,8,256]{2,1,0:T(8,128)(2,1)S(1)} async-done(((bf16[16,8,256]{2,1,0:T(8,128)(2,1)}), bf16[16,8,256]{2,1,0:T(8,128)(2,1)S(1)}, u32[]{:S(2)}, u32[]{:S(2)}) %all-to-all-start.4) | async-done | bytes 65568 | tf_op jit(solution)/shard_map/all_to_all | solution.py:32
  102.8 8.0 %all_to_all.67.totals_ref.soft_ref = f32[8,2,1024]{2,1,0:T(2,128)S(1)} all-to-all(f32[8,2,1024]{2,1,0:T(2,128)S(1)} %get-tuple-element.47), channel_id=1, replica_groups=mesh['z'=16,'y'=4,'x'=4,'core'=2] {'x','core'}, dimensions={0} | all-to-all | bytes 131072 | tf_op jit(solution)/shard_map/all_to_all | solution.py:32
  111.8 7.8 %all_to_all.68 = f32[4,8,256]{2,1,0:T(8,128)S(1)} all-to-all(f32[4,8,256]{2,1,0:T(8,128)S(1)} %column_pass.3), channel_id=1, replica_groups=mesh['z'=16,'y'=4,'x'=4,'core'=2] {'y'}, dimensions={0} | all-to-all | bytes 65536 | tf_op jit(solution)/shard_map/all_to_all | solution.py:32
  120.3 4.5 %all-to-all-start.7 = ((f32[16,8,256]{2,1,0:T(8,128)}), f32[16,8,256]{2,1,0:T(8,128)S(1)}, u32[]{:S(2)}, u32[]{:S(2)}) async-start(f32[16,8,256]{2,1,0:T(8,128)} %broadcast_in_dim.99), calls=%async_computation.7 | async-start | bytes 262144 | tf_op jit(solution)/shard_map/all_to_all | solution.py:32
  125.2 12.5 %all-to-all-done.7.totals_ref = f32[16,8,256]{2,1,0:T(8,128)S(1)} async-done(((f32[16,8,256]{2,1,0:T(8,128)}), f32[16,8,256]{2,1,0:T(8,128)S(1)}, u32[]{:S(2)}, u32[]{:S(2)}) %all-to-all-start.7) | async-done | bytes 131104 | tf_op jit(solution)/shard_map/all_to_all | solution.py:32
  139.9 7.8 %all_to_all.69.line_ref = f32[8,1,1024]{2,1,0:T(1,128)S(1)} all-to-all(f32[8,1,1024]{2,1,0:T(1,128)S(1)} %get-tuple-element.52), channel_id=1, replica_groups=mesh['z'=16,'y'=4,'x'=4,'core'=2] {'x','core'}, dimensions={0} | all-to-all | bytes 65536 | tf_op jit(solution)/shard_map/all_to_all | solution.py:32
  147.8 4.2 %gradient.1 = (f32[1024,256]{1,0:T(8,128)S(1)}, f32[2048,256]{1,0:T(8,128)S(1)}) custom-call(f32[1024,2048]{1,0:T(8,128)S(1)} %get-tuple-element.51.other_ref, f32[16,8,256]{2,1,0:T(8,128)S(1)} %all-to-all-done.7.totals_ref, f32[8,1,1024]{2,1,0:T(1,128)S(1)} %all_to_all.69.line_ref, f32[8,2,1024]{2,1,0:T(2,128)S(1)} %all_to_all.67.totals_ref.soft_ref, ...), custom_call_target="tpu_custom_call" | custom-call | flops 3221225472 | bytes 4194304 | tf_op jit(solution)/shard_map/gradient/pallas_call | solution.py:231
  154.2 4.4 %all-to-all-start.9 = ((f16[4,512,256]{2,1,0:T(8,128)(2,1)}), f16[4,512,256]{2,1,0:T(8,128)(2,1)}, u32[]{:S(2)}, u32[]{:S(2)}) async-start(f16[4,512,256]{2,1,0:T(8,128)(2,1)} %bitcast.45), calls=%async_computation.9 | async-start | bytes 2097152 | tf_op jit(solution)/shard_map/all_to_all | solution.py:32
  164.8 4.6 %collective-permute-start.8 = (f16[128,256]{1,0:T(8,128)(2,1)S(1)}, f16[128,256]{1,0:T(8,128)(2,1)S(1)}, u32[]{:S(2)}, u32[]{:S(2)}) collective-permute-start(f16[128,256]{1,0:T(8,128)(2,1)S(1)} %get-tuple-element.75), channel_id=1, source_target_pairs={{0,6},{2,0},{4,2},{6,4},{1,7},{3,1},{5,3},{7,5},{8,14},{10,8},{12,... | collective-permute-start | bytes 196616 | tf_op jit(solution)/shard_map/ppermute | solution.py:28
  176.0 4.7 %all-to-all-start.10 = ((f16[16,32,256]{2,1,0:T(8,128)(2,1)}), f16[16,32,256]{2,1,0:T(8,128)(2,1)S(1)}, u32[]{:S(2)}, u32[]{:S(2)}) async-start(f16[16,32,256]{2,1,0:T(8,128)(2,1)} %bitcast.12), calls=%async_computation.10 | async-start | bytes 524288 | tf_op jit(solution)/shard_map/all_to_all | solution.py:32
  183.6 4.6 %collective-permute-start.11 = (f16[128,256]{1,0:T(8,128)(2,1)S(1)}, f16[128,256]{1,0:T(8,128)(2,1)S(1)}, u32[]{:S(2)}, u32[]{:S(2)}) collective-permute-start(f16[128,256]{1,0:T(8,128)(2,1)S(1)} %fusion.4), channel_id=1, source_target_pairs={{0,6},{2,0},{4,2},{6,4},{1,7},{3,1},{5,3},{7,5},{8,14},{10,8},{12,... | collective-permute-start | bytes 196616 | tf_op jit(solution)/shard_map/ppermute | solution.py:28
  190.1 5.7 %collective-permute-done.10 = f16[128,256]{1,0:T(8,128)(2,1)S(1)} collective-permute-done((f16[128,256]{1,0:T(8,128)(2,1)S(1)}, f16[128,256]{1,0:T(8,128)(2,1)S(1)}, u32[]{:S(2)}, u32[]{:S(2)}) %collective-permute-start.10) | collective-permute-done | bytes 65568 | tf_op jit(solution)/shard_map/ppermute | solution.py:28
  199.7 9.2 %all-to-all-start.11 = ((f16[16,32,256]{2,1,0:T(8,128)(2,1)}), f16[16,32,256]{2,1,0:T(8,128)(2,1)S(1)}, u32[]{:S(2)}, u32[]{:S(2)}) async-start(f16[16,32,256]{2,1,0:T(8,128)(2,1)} %broadcast_in_dim.100), calls=%async_computation.11 | async-start | bytes 524288 | tf_op jit(solution)/shard_map/all_to_all | solution.py:32
  213.6 10.8 %all-to-all-done.11 = f16[16,32,256]{2,1,0:T(8,128)(2,1)S(1)} async-done(((f16[16,32,256]{2,1,0:T(8,128)(2,1)}), f16[16,32,256]{2,1,0:T(8,128)(2,1)S(1)}, u32[]{:S(2)}, u32[]{:S(2)}) %all-to-all-start.11) | async-done | bytes 262176 | tf_op jit(solution)/shard_map/all_to_all | solution.py:32
  224.5 13.9 %all_to_all.70 = f16[4,512,256]{2,1,0:T(8,128)(2,1)S(1)} all-to-all(f16[4,512,256]{2,1,0:T(8,128)(2,1)S(1)} %broadcast_in_dim.108), channel_id=1, replica_groups=mesh['z'=16,'y'=4,'x'=4,'core'=2] {'y'}, dimensions={0} | all-to-all | bytes 2097152 | tf_op jit(solution)/shard_map/all_to_all | solution.py:32
  (95 shorter events, 59.0 us)
Async XLA Ops:
  1.5 24.8 %collective-permute-start = (bf16[128,256]{1,0:T(8,128)(2,1)S(1)}, bf16[128,256]{1,0:T(8,128)(2,1)S(1)}, u32[]{:S(2)}, u32[]{:S(2)}) collective-permute-start(bf16[128,256]{1,0:T(8,128)(2,1)S(1)} %constant_dynamic-slice_fusion.4), channel_id=1, source_target_pairs={{0,256},{32,288},{64,320},{96,352},{128,384},{160,416},{192,448},{... | collective-permute-start | bytes 196616 | tf_op jit(solution)/shard_map/ppermute | solution.py:28
  21.9 78.1 %copy-start.6 = (bf16[1024,256]{1,0:T(8,128)(2,1)}, bf16[1024,256]{1,0:T(8,128)(2,1)S(1)}, u32[]{:S(2)}) copy-start(bf16[1024,256]{1,0:T(8,128)(2,1)S(1)} %get-tuple-element.36.views_ref) | copy-start | bytes 1572868
  21.9 11.0 %all-to-all-start = ((f32[4,8,256]{2,1,0:T(8,128)}), f32[4,8,256]{2,1,0:T(8,128)S(1)}, u32[]{:S(2)}, u32[]{:S(2)}) async-start(f32[4,8,256]{2,1,0:T(8,128)} %get-tuple-element.38), calls=%async_computation | async-start | bytes 65536 | tf_op jit(solution)/shard_map/all_to_all | solution.py:32
  26.3 3.1 %collective-permute-start.1 = (bf16[128,256]{1,0:T(8,128)(2,1)S(1)}, bf16[128,256]{1,0:T(8,128)(2,1)S(1)}, u32[]{:S(2)}, u32[]{:S(2)}) collective-permute-start(bf16[128,256]{1,0:T(8,128)(2,1)S(1)} %collective-permute-done), channel_id=1, source_target_pairs={{0,1},{1,0},{2,3},{3,2},{4,5},{5,4},{6,7},{7,6},{8,9},{9,8},{10,11... | collective-permute-start | bytes 196616 | tf_op jit(solution)/shard_map/ppermute | solution.py:28
  29.5 19.2 %collective-permute-start.2 = (bf16[256,256]{1,0:T(8,128)(2,1)S(1)}, bf16[256,256]{1,0:T(8,128)(2,1)S(1)}, u32[]{:S(2)}, u32[]{:S(2)}) collective-permute-start(bf16[256,256]{1,0:T(8,128)(2,1)S(1)} %bitcast.49), channel_id=1, source_target_pairs={{0,2},{2,4},{4,6},{6,0},{1,3},{3,5},{5,7},{7,1},{8,10},{10,12},{12... | collective-permute-start | bytes 393224 | tf_op jit(solution)/shard_map/ppermute | solution.py:28
  33.5 19.5 %all-to-all-start.1 = ((bf16[16,8,256]{2,1,0:T(8,128)(2,1)}), bf16[16,8,256]{2,1,0:T(8,128)(2,1)S(1)}, u32[]{:S(2)}, u32[]{:S(2)}) async-start(bf16[16,8,256]{2,1,0:T(8,128)(2,1)} %broadcast_in_dim.43), calls=%async_computation.1 | async-start | bytes 131072 | tf_op jit(solution)/shard_map/all_to_all | solution.py:32
  41.2 11.8 %collective-permute-start.4 = (bf16[256,256]{1,0:T(8,128)(2,1)S(1)}, bf16[256,256]{1,0:T(8,128)(2,1)S(1)}, u32[]{:S(2)}, u32[]{:S(2)}) collective-permute-start(bf16[256,256]{1,0:T(8,128)(2,1)S(1)} %bitcast.50), channel_id=1, source_target_pairs={{0,6},{2,0},{4,2},{6,4},{1,7},{3,1},{5,3},{7,5},{8,14},{10,8},{12,... | collective-permute-start | bytes 393224 | tf_op jit(solution)/shard_map/ppermute | solution.py:28
  44.6 8.4 %collective-permute-start.3 = (bf16[256,256]{1,0:T(8,128)(2,1)S(1)}, bf16[256,256]{1,0:T(8,128)(2,1)S(1)}, u32[]{:S(2)}, u32[]{:S(2)}) collective-permute-start(bf16[256,256]{1,0:T(8,128)(2,1)S(1)} %bitcast.51), channel_id=1, source_target_pairs={{0,4},{2,6},{4,0},{6,2},{1,5},{3,7},{5,1},{7,3},{8,12},{10,14},{12... | collective-permute-start | bytes 393224 | tf_op jit(solution)/shard_map/ppermute | solution.py:28
  65.1 23.0 %copy-start.8 = (s32[1024]{0:T(1024)S(1)}, s32[1024]{0:T(1024)}, u32[]{:S(2)}) copy-start(s32[1024]{0:T(1024)} %param.5) | copy-start | bytes 12292
  76.4 23.5 %all-to-all-start.4 = ((bf16[16,8,256]{2,1,0:T(8,128)(2,1)}), bf16[16,8,256]{2,1,0:T(8,128)(2,1)S(1)}, u32[]{:S(2)}, u32[]{:S(2)}) async-start(bf16[16,8,256]{2,1,0:T(8,128)(2,1)} %broadcast_in_dim.97), calls=%async_computation.4 | async-start | bytes 131072 | tf_op jit(solution)/shard_map/all_to_all | solution.py:32
  120.3 17.4 %all-to-all-start.7 = ((f32[16,8,256]{2,1,0:T(8,128)}), f32[16,8,256]{2,1,0:T(8,128)S(1)}, u32[]{:S(2)}, u32[]{:S(2)}) async-start(f32[16,8,256]{2,1,0:T(8,128)} %broadcast_in_dim.99), calls=%async_computation.7 | async-start | bytes 262144 | tf_op jit(solution)/shard_map/all_to_all | solution.py:32
  137.7 10.1 %copy-start.7 = (bf16[1024,256]{1,0:T(8,128)(2,1)S(1)}, bf16[1024,256]{1,0:T(8,128)(2,1)}, u32[]{:S(2)}) copy-start(bf16[1024,256]{1,0:T(8,128)(2,1)} %copy-done.6) | copy-start | bytes 1572868
  154.2 6.8 %copy-start.3 = (bf16[2048,256]{1,0:T(8,128)(2,1)S(1)}, bf16[2048,256]{1,0:T(8,128)(2,1)}, u32[]{:S(2)}) copy-start(bf16[2048,256]{1,0:T(8,128)(2,1)} %proto_ref.1) | copy-start | bytes 3145732
  154.2 19.8 %all-to-all-start.9 = ((f16[4,512,256]{2,1,0:T(8,128)(2,1)}), f16[4,512,256]{2,1,0:T(8,128)(2,1)}, u32[]{:S(2)}, u32[]{:S(2)}) async-start(f16[4,512,256]{2,1,0:T(8,128)(2,1)} %bitcast.45), calls=%async_computation.9 | async-start | bytes 2097152 | tf_op jit(solution)/shard_map/all_to_all | solution.py:32
  158.8 3.4 %collective-permute-start.5 = (f16[512,256]{1,0:T(8,128)(2,1)S(1)}, f16[512,256]{1,0:T(8,128)(2,1)S(1)}, u32[]{:S(2)}, u32[]{:S(2)}) collective-permute-start(f16[512,256]{1,0:T(8,128)(2,1)S(1)} %constant_dynamic-slice_fusion.3), channel_id=1, source_target_pairs={{0,1},{1,0},{2,3},{3,2},{4,5},{5,4},{6,7},{7,6},{8,9},{9,8},{10,11... | collective-permute-start | bytes 786440 | tf_op jit(solution)/shard_map/ppermute | solution.py:28
  162.3 18.4 %collective-permute-start.6 = (f16[128,256]{1,0:T(8,128)(2,1)S(1)}, f16[128,256]{1,0:T(8,128)(2,1)S(1)}, u32[]{:S(2)}, u32[]{:S(2)}) collective-permute-start(f16[128,256]{1,0:T(8,128)(2,1)S(1)} %get-tuple-element.74), channel_id=1, source_target_pairs={{0,2},{2,4},{4,6},{6,0},{1,3},{3,5},{5,7},{7,1},{8,10},{10,12},{12... | collective-permute-start | bytes 196616 | tf_op jit(solution)/shard_map/ppermute | solution.py:28
  164.8 15.9 %collective-permute-start.8 = (f16[128,256]{1,0:T(8,128)(2,1)S(1)}, f16[128,256]{1,0:T(8,128)(2,1)S(1)}, u32[]{:S(2)}, u32[]{:S(2)}) collective-permute-start(f16[128,256]{1,0:T(8,128)(2,1)S(1)} %get-tuple-element.75), channel_id=1, source_target_pairs={{0,6},{2,0},{4,2},{6,4},{1,7},{3,1},{5,3},{7,5},{8,14},{10,8},{12,... | collective-permute-start | bytes 196616 | tf_op jit(solution)/shard_map/ppermute | solution.py:28
  169.4 11.3 %collective-permute-start.7 = (f16[128,256]{1,0:T(8,128)(2,1)S(1)}, f16[128,256]{1,0:T(8,128)(2,1)S(1)}, u32[]{:S(2)}, u32[]{:S(2)}) collective-permute-start(f16[128,256]{1,0:T(8,128)(2,1)S(1)} %get-tuple-element.76), channel_id=1, source_target_pairs={{0,4},{2,6},{4,0},{6,2},{1,5},{3,7},{5,1},{7,3},{8,12},{10,14},{12... | collective-permute-start | bytes 196616 | tf_op jit(solution)/shard_map/ppermute | solution.py:28
  176.0 22.7 %all-to-all-start.10 = ((f16[16,32,256]{2,1,0:T(8,128)(2,1)}), f16[16,32,256]{2,1,0:T(8,128)(2,1)S(1)}, u32[]{:S(2)}, u32[]{:S(2)}) async-start(f16[16,32,256]{2,1,0:T(8,128)(2,1)} %bitcast.12), calls=%async_computation.10 | async-start | bytes 524288 | tf_op jit(solution)/shard_map/all_to_all | solution.py:32
  181.0 9.0 %collective-permute-start.9 = (f16[128,256]{1,0:T(8,128)(2,1)S(1)}, f16[128,256]{1,0:T(8,128)(2,1)S(1)}, u32[]{:S(2)}, u32[]{:S(2)}) collective-permute-start(f16[128,256]{1,0:T(8,128)(2,1)S(1)} %fusion.4), channel_id=1, source_target_pairs={{0,2},{2,4},{4,6},{6,0},{1,3},{3,5},{5,7},{7,1},{8,10},{10,12},{12... | collective-permute-start | bytes 196616 | tf_op jit(solution)/shard_map/ppermute | solution.py:28
  183.6 25.3 %collective-permute-start.11 = (f16[128,256]{1,0:T(8,128)(2,1)S(1)}, f16[128,256]{1,0:T(8,128)(2,1)S(1)}, u32[]{:S(2)}, u32[]{:S(2)}) collective-permute-start(f16[128,256]{1,0:T(8,128)(2,1)S(1)} %fusion.4), channel_id=1, source_target_pairs={{0,6},{2,0},{4,2},{6,4},{1,7},{3,1},{5,3},{7,5},{8,14},{10,8},{12,... | collective-permute-start | bytes 196616 | tf_op jit(solution)/shard_map/ppermute | solution.py:28
  188.1 7.7 %collective-permute-start.10 = (f16[128,256]{1,0:T(8,128)(2,1)S(1)}, f16[128,256]{1,0:T(8,128)(2,1)S(1)}, u32[]{:S(2)}, u32[]{:S(2)}) collective-permute-start(f16[128,256]{1,0:T(8,128)(2,1)S(1)} %fusion.4), channel_id=1, source_target_pairs={{0,4},{2,6},{4,0},{6,2},{1,5},{3,7},{5,1},{7,3},{8,12},{10,14},{12... | collective-permute-start | bytes 196616 | tf_op jit(solution)/shard_map/ppermute | solution.py:28
  199.7 24.7 %all-to-all-start.11 = ((f16[16,32,256]{2,1,0:T(8,128)(2,1)}), f16[16,32,256]{2,1,0:T(8,128)(2,1)S(1)}, u32[]{:S(2)}, u32[]{:S(2)}) async-start(f16[16,32,256]{2,1,0:T(8,128)(2,1)} %broadcast_in_dim.100), calls=%async_computation.11 | async-start | bytes 524288 | tf_op jit(solution)/shard_map/all_to_all | solution.py:32
  208.9 3.4 %collective-permute-start.12 = (f16[512,256]{1,0:T(8,128)(2,1)S(1)}, f16[512,256]{1,0:T(8,128)(2,1)S(1)}, u32[]{:S(2)}, u32[]{:S(2)}) collective-permute-start(f16[512,256]{1,0:T(8,128)(2,1)S(1)} %bitcast.46), channel_id=1, source_target_pairs={{0,1},{1,0},{2,3},{3,2},{4,5},{5,4},{6,7},{7,6},{8,9},{9,8},{10,11... | collective-permute-start | bytes 786440 | tf_op jit(solution)/shard_map/ppermute | solution.py:28
  (5 other events, 8.9 us)

commit v10 on v9

--- a/solution.py
+++ b/solution.py
@@ -312,7 +312,7 @@
     )
 
     view_part, proto_part, late_emb, late_proto, (y, z, x, core) = lax.optimization_barrier(
-        (view_part, proto_part, embeddings, prototypes, place)
+        (view_part.astype(SENT), proto_part, embeddings, prototypes, place)
     )
     proto_rows = unit_rows(block(late_proto, y * z_count + z, y_count * z_count))[0]
     view_rows = unit_rows(block(late_emb, core * x_count + x, members))[0]
@@ -322,7 +322,7 @@
     proto_sum = (tangent(total(proto_pieces), proto_rows) * (1.0 / z_count)).astype(SENT)
     proto_sum = gathered(proto_sum, "z").reshape(-1, width)
 
-    view_sum = scatter_sum(scatter_sum(view_part.astype(SENT), "core", core), "x", x)
+    view_sum = scatter_sum(scatter_sum(view_part, "core", core), "x", x)
     view_sum = tangent(view_sum.astype(f32), view_rows).astype(SENT)
     view_sum = gather_blocks(gather_blocks(view_sum, "x", x), "core", core)
 

time: 241 us -> 239 us (level)
  no operation moved by 1% of the time
where the time goes in v10:
time: 239 us; the launch traced here: 238 us
  starting transfers between devices  95.8 us (40%)
  blocking collectives  56.9 us (24%)
  waiting for transfers between devices  48.3 us (20%)
  Pallas kernels  17.5 us (7%)
  local copies, waits for them, and re-layouts  10.3 us (4%)
  other arithmetic  7.75 us (3%)
    all_to_all x6, blocking collectives, exchanged(): return lax.all_to_all(value, axis, 0, 0, tiled=True)  56.9 us
    ppermute x13, starting transfers between devices, shifted(): return lax.ppermute(value, axis, pairs)  50 us
    all_to_all x7, starting transfers between devices, exchanged(): return lax.all_to_all(value, axis, 0, 0, tiled=True)  45.8 us
    all_to_all x7, waiting for transfers between devices, exchanged(): return lax.all_to_all(value, axis, 0, 0, tiled=True)  35.5 us
    pallas_call x7, Pallas kernels, call(): pl.pallas_call(kernel, name=name, out_shape=[jax.ShapeDtypeStruct(shape,...  17.5 us
    ppermute x13, waiting for transfers between devices, shifted(): return lax.ppermute(value, axis, pairs)  12.8 us
  transfers between devices with their start and end apart: 20, of which 10 were waited for; matrix products, arithmetic and copies ran while one was open for 4% of the time, Pallas kernels for 1%

profile of v10, /device:TPU:32, one launch (start us, length us, event | category | flops | bytes accessed | tf_op | source)
XLA Modules:
  0.0 237.8 jit_solution(10647821657007737130)
XLA Ops:
  1.5 14.8 %collective-permute-start = (bf16[128,256]{1,0:T(8,128)(2,1)S(1)}, bf16[128,256]{1,0:T(8,128)(2,1)S(1)}, u32[]{:S(2)}, u32[]{:S(2)}) collective-permute-start(bf16[128,256]{1,0:T(8,128)(2,1)S(1)} %constant_dynamic-slice_fusion.4), channel_id=1, source_target_pairs={{0,256},{32,288},{64,320},{96,352},{128,384},{160,416},{192,448},{... | collective-permute-start | bytes 196616 | tf_op jit(solution)/shard_map/ppermute | solution.py:28
  21.9 4.5 %all-to-all-start = ((f32[4,8,256]{2,1,0:T(8,128)}), f32[4,8,256]{2,1,0:T(8,128)S(1)}, u32[]{:S(2)}, u32[]{:S(2)}) async-start(f32[4,8,256]{2,1,0:T(8,128)} %get-tuple-element.38), calls=%async_computation | async-start | bytes 65536 | tf_op jit(solution)/shard_map/all_to_all | solution.py:32
  33.5 7.6 %all-to-all-start.1 = ((bf16[16,8,256]{2,1,0:T(8,128)(2,1)}), bf16[16,8,256]{2,1,0:T(8,128)(2,1)S(1)}, u32[]{:S(2)}, u32[]{:S(2)}) async-start(bf16[16,8,256]{2,1,0:T(8,128)(2,1)} %broadcast_in_dim.43), calls=%async_computation.1 | async-start | bytes 131072 | tf_op jit(solution)/shard_map/all_to_all | solution.py:32
  44.6 3.9 %collective-permute-start.3 = (bf16[256,256]{1,0:T(8,128)(2,1)S(1)}, bf16[256,256]{1,0:T(8,128)(2,1)S(1)}, u32[]{:S(2)}, u32[]{:S(2)}) collective-permute-start(bf16[256,256]{1,0:T(8,128)(2,1)S(1)} %bitcast.51), channel_id=1, source_target_pairs={{0,4},{2,6},{4,0},{6,2},{1,5},{3,7},{5,1},{7,3},{8,12},{10,14},{12... | collective-permute-start | bytes 393224 | tf_op jit(solution)/shard_map/ppermute | solution.py:28
  48.7 4.3 %collective-permute-done.3 = bf16[256,256]{1,0:T(8,128)(2,1)S(1)} collective-permute-done((bf16[256,256]{1,0:T(8,128)(2,1)S(1)}, bf16[256,256]{1,0:T(8,128)(2,1)S(1)}, u32[]{:S(2)}, u32[]{:S(2)}) %collective-permute-start.3) | collective-permute-done | bytes 131104 | tf_op jit(solution)/shard_map/ppermute | solution.py:28
  56.0 9.1 %all_to_all.65.totals_ref = f32[8,2,1024]{2,1,0:T(2,128)S(1)} all-to-all(f32[8,2,1024]{2,1,0:T(2,128)S(1)} %get-tuple-element.41), channel_id=1, replica_groups=mesh['z'=16,'y'=4,'x'=4,'core'=2] {'x','core'}, dimensions={0} | all-to-all | bytes 131072 | tf_op jit(solution)/shard_map/all_to_all | solution.py:32
  66.1 9.7 %all_to_all.66 = f32[4,8,256]{2,1,0:T(8,128)S(1)} all-to-all(f32[4,8,256]{2,1,0:T(8,128)S(1)} %column_pass.2), channel_id=1, replica_groups=mesh['z'=16,'y'=4,'x'=4,'core'=2] {'y'}, dimensions={0} | all-to-all | bytes 65536 | tf_op jit(solution)/shard_map/all_to_all | solution.py:32
  76.4 11.7 %all-to-all-start.4 = ((bf16[16,8,256]{2,1,0:T(8,128)(2,1)}), bf16[16,8,256]{2,1,0:T(8,128)(2,1)S(1)}, u32[]{:S(2)}, u32[]{:S(2)}) async-start(bf16[16,8,256]{2,1,0:T(8,128)(2,1)} %broadcast_in_dim.97), calls=%async_computation.4 | async-start | bytes 131072 | tf_op jit(solution)/shard_map/all_to_all | solution.py:32
  88.1 3.9 %gather_fusion = bf16[1024,256]{1,0:T(8,128)(2,1)S(1)} fusion(bf16[1024,256]{1,0:T(8,128)(2,1)S(1)} %bitcast.44, s32[1024]{0:T(1024)S(1)} %fusion.21), kind=kCustom, calls=%fused_computation | custom fusion | bytes 1052672 | tf_op jit(solution)/shard_map/gather | solution.py:286
  92.1 7.9 %all-to-all-done.4.totals_ref = bf16[16,8,256]{2,1,0:T(8,128)(2,1)S(1)} async-done(((bf16[16,8,256]{2,1,0:T(8,128)(2,1)}), bf16[16,8,256]{2,1,0:T(8,128)(2,1)S(1)}, u32[]{:S(2)}, u32[]{:S(2)}) %all-to-all-start.4) | async-done | bytes 65568 | tf_op jit(solution)/shard_map/all_to_all | solution.py:32
  102.8 8.0 %all_to_all.67.totals_ref.soft_ref = f32[8,2,1024]{2,1,0:T(2,128)S(1)} all-to-all(f32[8,2,1024]{2,1,0:T(2,128)S(1)} %get-tuple-element.47), channel_id=1, replica_groups=mesh['z'=16,'y'=4,'x'=4,'core'=2] {'x','core'}, dimensions={0} | all-to-all | bytes 131072 | tf_op jit(solution)/shard_map/all_to_all | solution.py:32
  111.8 7.8 %all_to_all.68 = f32[4,8,256]{2,1,0:T(8,128)S(1)} all-to-all(f32[4,8,256]{2,1,0:T(8,128)S(1)} %column_pass.3), channel_id=1, replica_groups=mesh['z'=16,'y'=4,'x'=4,'core'=2] {'y'}, dimensions={0} | all-to-all | bytes 65536 | tf_op jit(solution)/shard_map/all_to_all | solution.py:32
  120.3 4.5 %all-to-all-start.7 = ((f32[16,8,256]{2,1,0:T(8,128)}), f32[16,8,256]{2,1,0:T(8,128)S(1)}, u32[]{:S(2)}, u32[]{:S(2)}) async-start(f32[16,8,256]{2,1,0:T(8,128)} %broadcast_in_dim.99), calls=%async_computation.7 | async-start | bytes 262144 | tf_op jit(solution)/shard_map/all_to_all | solution.py:32
  125.2 12.5 %all-to-all-done.7.totals_ref = f32[16,8,256]{2,1,0:T(8,128)S(1)} async-done(((f32[16,8,256]{2,1,0:T(8,128)}), f32[16,8,256]{2,1,0:T(8,128)S(1)}, u32[]{:S(2)}, u32[]{:S(2)}) %all-to-all-start.7) | async-done | bytes 131104 | tf_op jit(solution)/shard_map/all_to_all | solution.py:32
  139.9 7.8 %all_to_all.69.line_ref = f32[8,1,1024]{2,1,0:T(1,128)S(1)} all-to-all(f32[8,1,1024]{2,1,0:T(1,128)S(1)} %get-tuple-element.52), channel_id=1, replica_groups=mesh['z'=16,'y'=4,'x'=4,'core'=2] {'x','core'}, dimensions={0} | all-to-all | bytes 65536 | tf_op jit(solution)/shard_map/all_to_all | solution.py:32
  147.8 4.2 %gradient.1 = (f32[1024,256]{1,0:T(8,128)S(1)}, f32[2048,256]{1,0:T(8,128)S(1)}) custom-call(f32[1024,2048]{1,0:T(8,128)S(1)} %get-tuple-element.51.other_ref, f32[16,8,256]{2,1,0:T(8,128)S(1)} %all-to-all-done.7.totals_ref, f32[8,1,1024]{2,1,0:T(1,128)S(1)} %all_to_all.69.line_ref, f32[8,2,1024]{2,1,0:T(2,128)S(1)} %all_to_all.67.totals_ref.soft_ref, ...), custom_call_target="tpu_custom_call" | custom-call | flops 3221225472 | bytes 4194304 | tf_op jit(solution)/shard_map/gradient/pallas_call | solution.py:231
  153.3 3.7 %all-to-all-start.9 = ((f16[4,512,256]{2,1,0:T(8,128)(2,1)}), f16[4,512,256]{2,1,0:T(8,128)(2,1)S(1)}, u32[]{:S(2)}, u32[]{:S(2)}) async-start(f16[4,512,256]{2,1,0:T(8,128)(2,1)} %bitcast.45), calls=%async_computation.9 | async-start | bytes 2097152 | tf_op jit(solution)/shard_map/all_to_all | solution.py:32
  164.2 4.6 %collective-permute-start.8 = (f16[128,256]{1,0:T(8,128)(2,1)S(1)}, f16[128,256]{1,0:T(8,128)(2,1)S(1)}, u32[]{:S(2)}, u32[]{:S(2)}) collective-permute-start(f16[128,256]{1,0:T(8,128)(2,1)S(1)} %get-tuple-element.75), channel_id=1, source_target_pairs={{0,6},{2,0},{4,2},{6,4},{1,7},{3,1},{5,3},{7,5},{8,14},{10,8},{12,... | collective-permute-start | bytes 196616 | tf_op jit(solution)/shard_map/ppermute | solution.py:28
  173.1 4.7 %all-to-all-start.10 = ((f16[16,32,256]{2,1,0:T(8,128)(2,1)}), f16[16,32,256]{2,1,0:T(8,128)(2,1)S(1)}, u32[]{:S(2)}, u32[]{:S(2)}) async-start(f16[16,32,256]{2,1,0:T(8,128)(2,1)} %bitcast.12), calls=%async_computation.10 | async-start | bytes 524288 | tf_op jit(solution)/shard_map/all_to_all | solution.py:32
  180.7 4.6 %collective-permute-start.11 = (f16[128,256]{1,0:T(8,128)(2,1)S(1)}, f16[128,256]{1,0:T(8,128)(2,1)S(1)}, u32[]{:S(2)}, u32[]{:S(2)}) collective-permute-start(f16[128,256]{1,0:T(8,128)(2,1)S(1)} %fusion.4), channel_id=1, source_target_pairs={{0,6},{2,0},{4,2},{6,4},{1,7},{3,1},{5,3},{7,5},{8,14},{10,8},{12,... | collective-permute-start | bytes 196616 | tf_op jit(solution)/shard_map/ppermute | solution.py:28
  188.0 4.9 %collective-permute-done.10 = f16[128,256]{1,0:T(8,128)(2,1)S(1)} collective-permute-done((f16[128,256]{1,0:T(8,128)(2,1)S(1)}, f16[128,256]{1,0:T(8,128)(2,1)S(1)}, u32[]{:S(2)}, u32[]{:S(2)}) %collective-permute-start.10) | collective-permute-done | bytes 65568 | tf_op jit(solution)/shard_map/ppermute | solution.py:28
  196.9 9.2 %all-to-all-start.11 = ((f16[16,32,256]{2,1,0:T(8,128)(2,1)}), f16[16,32,256]{2,1,0:T(8,128)(2,1)S(1)}, u32[]{:S(2)}, u32[]{:S(2)}) async-start(f16[16,32,256]{2,1,0:T(8,128)(2,1)} %broadcast_in_dim.100), calls=%async_computation.11 | async-start | bytes 524288 | tf_op jit(solution)/shard_map/all_to_all | solution.py:32
  210.8 10.8 %all-to-all-done.11 = f16[16,32,256]{2,1,0:T(8,128)(2,1)S(1)} async-done(((f16[16,32,256]{2,1,0:T(8,128)(2,1)}), f16[16,32,256]{2,1,0:T(8,128)(2,1)S(1)}, u32[]{:S(2)}, u32[]{:S(2)}) %all-to-all-start.11) | async-done | bytes 262176 | tf_op jit(solution)/shard_map/all_to_all | solution.py:32
  221.6 14.5 %all_to_all.70 = f16[4,512,256]{2,1,0:T(8,128)(2,1)S(1)} all-to-all(f16[4,512,256]{2,1,0:T(8,128)(2,1)S(1)} %broadcast_in_dim.108), channel_id=1, replica_groups=mesh['z'=16,'y'=4,'x'=4,'core'=2] {'y'}, dimensions={0} | all-to-all | bytes 2097152 | tf_op jit(solution)/shard_map/all_to_all | solution.py:32
  (91 shorter events, 57.6 us)
Async XLA Ops:
  1.5 24.8 %collective-permute-start = (bf16[128,256]{1,0:T(8,128)(2,1)S(1)}, bf16[128,256]{1,0:T(8,128)(2,1)S(1)}, u32[]{:S(2)}, u32[]{:S(2)}) collective-permute-start(bf16[128,256]{1,0:T(8,128)(2,1)S(1)} %constant_dynamic-slice_fusion.4), channel_id=1, source_target_pairs={{0,256},{32,288},{64,320},{96,352},{128,384},{160,416},{192,448},{... | collective-permute-start | bytes 196616 | tf_op jit(solution)/shard_map/ppermute | solution.py:28
  21.9 78.1 %copy-start.4 = (bf16[1024,256]{1,0:T(8,128)(2,1)}, bf16[1024,256]{1,0:T(8,128)(2,1)S(1)}, u32[]{:S(2)}) copy-start(bf16[1024,256]{1,0:T(8,128)(2,1)S(1)} %get-tuple-element.36.views_ref) | copy-start | bytes 1572868
  21.9 11.0 %all-to-all-start = ((f32[4,8,256]{2,1,0:T(8,128)}), f32[4,8,256]{2,1,0:T(8,128)S(1)}, u32[]{:S(2)}, u32[]{:S(2)}) async-start(f32[4,8,256]{2,1,0:T(8,128)} %get-tuple-element.38), calls=%async_computation | async-start | bytes 65536 | tf_op jit(solution)/shard_map/all_to_all | solution.py:32
  26.3 3.1 %collective-permute-start.1 = (bf16[128,256]{1,0:T(8,128)(2,1)S(1)}, bf16[128,256]{1,0:T(8,128)(2,1)S(1)}, u32[]{:S(2)}, u32[]{:S(2)}) collective-permute-start(bf16[128,256]{1,0:T(8,128)(2,1)S(1)} %collective-permute-done), channel_id=1, source_target_pairs={{0,1},{1,0},{2,3},{3,2},{4,5},{5,4},{6,7},{7,6},{8,9},{9,8},{10,11... | collective-permute-start | bytes 196616 | tf_op jit(solution)/shard_map/ppermute | solution.py:28
  29.5 19.2 %collective-permute-start.2 = (bf16[256,256]{1,0:T(8,128)(2,1)S(1)}, bf16[256,256]{1,0:T(8,128)(2,1)S(1)}, u32[]{:S(2)}, u32[]{:S(2)}) collective-permute-start(bf16[256,256]{1,0:T(8,128)(2,1)S(1)} %bitcast.49), channel_id=1, source_target_pairs={{0,2},{2,4},{4,6},{6,0},{1,3},{3,5},{5,7},{7,1},{8,10},{10,12},{12... | collective-permute-start | bytes 393224 | tf_op jit(solution)/shard_map/ppermute | solution.py:28
  33.5 19.5 %all-to-all-start.1 = ((bf16[16,8,256]{2,1,0:T(8,128)(2,1)}), bf16[16,8,256]{2,1,0:T(8,128)(2,1)S(1)}, u32[]{:S(2)}, u32[]{:S(2)}) async-start(bf16[16,8,256]{2,1,0:T(8,128)(2,1)} %broadcast_in_dim.43), calls=%async_computation.1 | async-start | bytes 131072 | tf_op jit(solution)/shard_map/all_to_all | solution.py:32
  41.2 11.8 %collective-permute-start.4 = (bf16[256,256]{1,0:T(8,128)(2,1)S(1)}, bf16[256,256]{1,0:T(8,128)(2,1)S(1)}, u32[]{:S(2)}, u32[]{:S(2)}) collective-permute-start(bf16[256,256]{1,0:T(8,128)(2,1)S(1)} %bitcast.50), channel_id=1, source_target_pairs={{0,6},{2,0},{4,2},{6,4},{1,7},{3,1},{5,3},{7,5},{8,14},{10,8},{12,... | collective-permute-start | bytes 393224 | tf_op jit(solution)/shard_map/ppermute | solution.py:28
  44.6 8.4 %collective-permute-start.3 = (bf16[256,256]{1,0:T(8,128)(2,1)S(1)}, bf16[256,256]{1,0:T(8,128)(2,1)S(1)}, u32[]{:S(2)}, u32[]{:S(2)}) collective-permute-start(bf16[256,256]{1,0:T(8,128)(2,1)S(1)} %bitcast.51), channel_id=1, source_target_pairs={{0,4},{2,6},{4,0},{6,2},{1,5},{3,7},{5,1},{7,3},{8,12},{10,14},{12... | collective-permute-start | bytes 393224 | tf_op jit(solution)/shard_map/ppermute | solution.py:28
  65.1 23.0 %copy-start.6 = (s32[1024]{0:T(1024)S(1)}, s32[1024]{0:T(1024)}, u32[]{:S(2)}) copy-start(s32[1024]{0:T(1024)} %param.5) | copy-start | bytes 12292
  76.4 23.5 %all-to-all-start.4 = ((bf16[16,8,256]{2,1,0:T(8,128)(2,1)}), bf16[16,8,256]{2,1,0:T(8,128)(2,1)S(1)}, u32[]{:S(2)}, u32[]{:S(2)}) async-start(bf16[16,8,256]{2,1,0:T(8,128)(2,1)} %broadcast_in_dim.97), calls=%async_computation.4 | async-start | bytes 131072 | tf_op jit(solution)/shard_map/all_to_all | solution.py:32
  120.3 17.4 %all-to-all-start.7 = ((f32[16,8,256]{2,1,0:T(8,128)}), f32[16,8,256]{2,1,0:T(8,128)S(1)}, u32[]{:S(2)}, u32[]{:S(2)}) async-start(f32[16,8,256]{2,1,0:T(8,128)} %broadcast_in_dim.99), calls=%async_computation.7 | async-start | bytes 262144 | tf_op jit(solution)/shard_map/all_to_all | solution.py:32
  137.7 10.1 %copy-start.5 = (bf16[1024,256]{1,0:T(8,128)(2,1)S(1)}, bf16[1024,256]{1,0:T(8,128)(2,1)}, u32[]{:S(2)}) copy-start(bf16[1024,256]{1,0:T(8,128)(2,1)} %copy-done.4) | copy-start | bytes 1572868
  153.2 6.1 %copy-start.3 = (bf16[2048,256]{1,0:T(8,128)(2,1)S(1)}, bf16[2048,256]{1,0:T(8,128)(2,1)}, u32[]{:S(2)}) copy-start(bf16[2048,256]{1,0:T(8,128)(2,1)} %proto_ref.1) | copy-start | bytes 3145732
  153.3 19.0 %all-to-all-start.9 = ((f16[4,512,256]{2,1,0:T(8,128)(2,1)}), f16[4,512,256]{2,1,0:T(8,128)(2,1)S(1)}, u32[]{:S(2)}, u32[]{:S(2)}) async-start(f16[4,512,256]{2,1,0:T(8,128)(2,1)} %bitcast.45), calls=%async_computation.9 | async-start | bytes 2097152 | tf_op jit(solution)/shard_map/all_to_all | solution.py:32
  157.1 3.6 %collective-permute-start.5 = (f16[512,256]{1,0:T(8,128)(2,1)S(1)}, f16[512,256]{1,0:T(8,128)(2,1)}, u32[]{:S(2)}, u32[]{:S(2)}) collective-permute-start(f16[512,256]{1,0:T(8,128)(2,1)S(1)} %constant_dynamic-slice_fusion.3), channel_id=1, source_target_pairs={{0,1},{1,0},{2,3},{3,2},{4,5},{5,4},{6,7},{7,6},{8,9},{9,8},{10,11... | collective-permute-start | bytes 786440 | tf_op jit(solution)/shard_map/ppermute | solution.py:28
  161.7 16.1 %collective-permute-start.6 = (f16[128,256]{1,0:T(8,128)(2,1)S(1)}, f16[128,256]{1,0:T(8,128)(2,1)S(1)}, u32[]{:S(2)}, u32[]{:S(2)}) collective-permute-start(f16[128,256]{1,0:T(8,128)(2,1)S(1)} %get-tuple-element.74), channel_id=1, source_target_pairs={{0,2},{2,4},{4,6},{6,0},{1,3},{3,5},{5,7},{7,1},{8,10},{10,12},{12... | collective-permute-start | bytes 196616 | tf_op jit(solution)/shard_map/ppermute | solution.py:28
  164.2 13.6 %collective-permute-start.8 = (f16[128,256]{1,0:T(8,128)(2,1)S(1)}, f16[128,256]{1,0:T(8,128)(2,1)S(1)}, u32[]{:S(2)}, u32[]{:S(2)}) collective-permute-start(f16[128,256]{1,0:T(8,128)(2,1)S(1)} %get-tuple-element.75), channel_id=1, source_target_pairs={{0,6},{2,0},{4,2},{6,4},{1,7},{3,1},{5,3},{7,5},{8,14},{10,8},{12,... | collective-permute-start | bytes 196616 | tf_op jit(solution)/shard_map/ppermute | solution.py:28
  168.8 9.1 %collective-permute-start.7 = (f16[128,256]{1,0:T(8,128)(2,1)S(1)}, f16[128,256]{1,0:T(8,128)(2,1)S(1)}, u32[]{:S(2)}, u32[]{:S(2)}) collective-permute-start(f16[128,256]{1,0:T(8,128)(2,1)S(1)} %get-tuple-element.76), channel_id=1, source_target_pairs={{0,4},{2,6},{4,0},{6,2},{1,5},{3,7},{5,1},{7,3},{8,12},{10,14},{12... | collective-permute-start | bytes 196616 | tf_op jit(solution)/shard_map/ppermute | solution.py:28
  173.1 22.7 %all-to-all-start.10 = ((f16[16,32,256]{2,1,0:T(8,128)(2,1)}), f16[16,32,256]{2,1,0:T(8,128)(2,1)S(1)}, u32[]{:S(2)}, u32[]{:S(2)}) async-start(f16[16,32,256]{2,1,0:T(8,128)(2,1)} %bitcast.12), calls=%async_computation.10 | async-start | bytes 524288 | tf_op jit(solution)/shard_map/all_to_all | solution.py:32
  178.2 9.8 %collective-permute-start.9 = (f16[128,256]{1,0:T(8,128)(2,1)S(1)}, f16[128,256]{1,0:T(8,128)(2,1)S(1)}, u32[]{:S(2)}, u32[]{:S(2)}) collective-permute-start(f16[128,256]{1,0:T(8,128)(2,1)S(1)} %fusion.4), channel_id=1, source_target_pairs={{0,2},{2,4},{4,6},{6,0},{1,3},{3,5},{5,7},{7,1},{8,10},{10,12},{12... | collective-permute-start | bytes 196616 | tf_op jit(solution)/shard_map/ppermute | solution.py:28
  180.7 25.3 %collective-permute-start.11 = (f16[128,256]{1,0:T(8,128)(2,1)S(1)}, f16[128,256]{1,0:T(8,128)(2,1)S(1)}, u32[]{:S(2)}, u32[]{:S(2)}) collective-permute-start(f16[128,256]{1,0:T(8,128)(2,1)S(1)} %fusion.4), channel_id=1, source_target_pairs={{0,6},{2,0},{4,2},{6,4},{1,7},{3,1},{5,3},{7,5},{8,14},{10,8},{12,... | collective-permute-start | bytes 196616 | tf_op jit(solution)/shard_map/ppermute | solution.py:28
  185.3 7.7 %collective-permute-start.10 = (f16[128,256]{1,0:T(8,128)(2,1)S(1)}, f16[128,256]{1,0:T(8,128)(2,1)S(1)}, u32[]{:S(2)}, u32[]{:S(2)}) collective-permute-start(f16[128,256]{1,0:T(8,128)(2,1)S(1)} %fusion.4), channel_id=1, source_target_pairs={{0,4},{2,6},{4,0},{6,2},{1,5},{3,7},{5,1},{7,3},{8,12},{10,14},{12... | collective-permute-start | bytes 196616 | tf_op jit(solution)/shard_map/ppermute | solution.py:28
  196.9 24.7 %all-to-all-start.11 = ((f16[16,32,256]{2,1,0:T(8,128)(2,1)}), f16[16,32,256]{2,1,0:T(8,128)(2,1)S(1)}, u32[]{:S(2)}, u32[]{:S(2)}) async-start(f16[16,32,256]{2,1,0:T(8,128)(2,1)} %broadcast_in_dim.100), calls=%async_computation.11 | async-start | bytes 524288 | tf_op jit(solution)/shard_map/all_to_all | solution.py:32
  206.0 3.4 %collective-permute-start.12 = (f16[512,256]{1,0:T(8,128)(2,1)S(1)}, f16[512,256]{1,0:T(8,128)(2,1)S(1)}, u32[]{:S(2)}, u32[]{:S(2)}) collective-permute-start(f16[512,256]{1,0:T(8,128)(2,1)S(1)} %bitcast.46), channel_id=1, source_target_pairs={{0,1},{1,0},{2,3},{3,2},{4,5},{5,4},{6,7},{7,6},{8,9},{9,8},{10,11... | collective-permute-start | bytes 786440 | tf_op jit(solution)/shard_map/ppermute | solution.py:28
  (3 other events, 3.5 us)
